TPU v7x, 32 devices: a whole 2x2x4 slice. The times are simulated.
32 devices in a mesh: groups: 2 (over y), seqin: 4 (over z), seqout: 2 (over x), chan: 2 (over core).
Axes of the slice: x: 2, y: 2, z: 4, core: 2. Of those that a mesh axis runs over, the one named last changes fastest.
Arguments:
- inputs: bfloat16 [4, 512, 2048], P(('groups', 'seqout'), 'seqin', 'chan'), parts along dimension 0, may hold values from -6 to 6
- time_step: float32 [2048], P('chan'), may hold values from 0 to 0.06, as said below
- decay_rate: float32 [32, 2048], P(None, 'chan'), may hold values from 0.25 to 1
- frequency: float32 [32, 2048], P(None, 'chan'), may hold values from 0 to 200
- output_real: float32 [32, 2048], P(None, 'chan'), may hold values from -0.5 to 0.5
- output_imag: float32 [32, 2048], P(None, 'chan'), may hold values from -0.5 to 0.5
- skip_gain: float32 [2048], P('chan'), may hold values from 0.5 to 1.5
Outputs:
- outputs: float32 [4, 512, 2048], P(('groups', 'seqout'), 'seqin', 'chan'), parts along dimension 0
There are 2 independent parts, one for each index of `groups`. A program takes and returns all parts, laid end to end along the dimension named above; an argument that names none is the same for every part. Nothing has to cross between parts.
Inputs may be any that keep to these rules, and one draw needn't show every extreme that they name: `time_step`: every step is positive.
All inputs are finite; a program needn't handle non-finite values.
Results may differ from a plain program's by a relative error of at most 0.0003.
Values may be sent and summed in bfloat16 or wider, within the bound.
No kernel may reach another device: no remote copies, remote signals or barrier semaphores. Data moves between devices by JAX's collectives and lax.ppermute only.
A program may use at most 128 MiB of HBM per device.

v0:
```python
import jax
import jax.numpy as jnp
from jax import lax
from jax.sharding import PartitionSpec as P

FACTOR = 64


highest = lax.Precision.HIGHEST
full_turn = 6.283185307179586
inner_len = 16


def carried_in(shard, axis, combine, identity):
    length, place = (lax.axis_size(axis), lax.axis_index(axis))
    everything = jax.tree.map(lambda part: lax.all_gather(part, axis), shard)
    start = jax.tree.map(
        lambda part, zero: jnp.broadcast_to(jnp.asarray(zero, part.dtype), part.shape),
        shard,
        identity,
    )

    def turn(k, before):
        reached = k < place
        new = combine(before, jax.tree.map(lambda part: part[k], everything))
        return jax.tree.map(lambda a, b: jnp.where(reached, a, b), new, before)

    return lax.fori_loop(0, length, turn, start)


def power_pair(fade_rate, turn_rate, amount):
    shrink = jnp.exp(-fade_rate * amount)
    return (shrink * jnp.cos(turn_rate * amount), shrink * jnp.sin(turn_rate * amount))


def split_places(places):
    inner_count = min(inner_len, places.shape[0])
    outer = places.reshape(-1, inner_count)[:, 0]
    inner = places[:inner_count] - places[0]
    return (outer, inner)


def powers_sum(places, fade_rate, turn_rate, real_part, imag_part):
    outer, inner = split_places(places)
    far_real, far_imag = power_pair(fade_rate, turn_rate, outer[:, None, None])
    lead_real = real_part * far_real - imag_part * far_imag
    lead_imag = real_part * far_imag + imag_part * far_real
    near_real, near_imag = power_pair(fade_rate, turn_rate, inner[:, None, None])
    first = jnp.einsum("anc,unc->auc", lead_real, near_real, precision=highest)
    second = jnp.einsum("anc,unc->auc", lead_imag, near_imag, precision=highest)
    return (2.0 * (first - second)).reshape(places.shape[0], real_part.shape[-1])


def state_sums(places, signal, fade_rate, turn_rate):
    outer, inner = split_places(places)
    grouped = signal.reshape(outer.shape[0], inner.shape[0], signal.shape[-1])
    near_real, near_imag = power_pair(fade_rate, turn_rate, inner[:, None, None])
    inner_real = jnp.einsum("unc,auc->anc", near_real, grouped, precision=highest)
    inner_imag = jnp.einsum("unc,auc->anc", near_imag, grouped, precision=highest)
    far_real, far_imag = power_pair(fade_rate, turn_rate, outer[:, None, None])
    real_sum = jnp.sum(far_real * inner_real - far_imag * inner_imag, axis=0)
    imag_sum = jnp.sum(far_real * inner_imag + far_imag * inner_real, axis=0)
    return (real_sum, imag_sum)


def turn_table(rows, cols, length, row_start, col_start, sign):
    row_ids = lax.broadcasted_iota(jnp.int32, (rows, cols), 0) + row_start
    col_ids = lax.broadcasted_iota(jnp.int32, (rows, cols), 1) + col_start
    phase_angle = (row_ids * col_ids % length).astype(jnp.float32) * (full_turn / length)
    return (jnp.cos(phase_angle), sign * jnp.sin(phase_angle))


def complex_mix(pattern, table, operand):

    def product_of(left_part, right_part):
        return jnp.einsum(pattern, left_part, right_part, precision=highest)

    real_part = product_of(table[0], operand[0]) - product_of(table[1], operand[1])
    imag_part = product_of(table[0], operand[1]) + product_of(table[1], operand[0])
    return (real_part, imag_part)


def chain_step(earlier, later):
    early_ar, early_ai, early_sr, early_si = earlier
    late_ar, late_ai, late_sr, late_si = later
    joined_ar = early_ar * late_ar - early_ai * late_ai
    joined_ai = early_ar * late_ai + early_ai * late_ar
    joined_sr = late_ar * early_sr - late_ai * early_si + late_sr
    joined_si = late_ar * early_si + late_ai * early_sr + late_si
    return (joined_ar, joined_ai, joined_sr, joined_si)


def per_device(inputs, time_step, decay_rate, frequency, output_real, output_imag, skip_gain):
    signal = inputs[0]
    tokens, channels = signal.shape
    parts_in = lax.axis_size("seqin")
    place_in = lax.axis_index("seqin")
    place_out = lax.axis_index("seqout")
    block_len = parts_in * tokens
    fade_rate = time_step[None, :] * decay_rate
    turn_rate = time_step[None, :] * frequency
    input_gain = jnp.sqrt(-jnp.expm1(-2.0 * fade_rate))
    weight_real = input_gain * output_real
    weight_imag = input_gain * output_imag
    values = signal.astype(jnp.float32)
    first_token = place_in * tokens
    offsets = lax.iota(jnp.int32, tokens)
    tail_places = (block_len - 1 - first_token - offsets).astype(jnp.float32)
    tail_real, tail_imag = state_sums(tail_places, values, fade_rate, turn_rate)
    sums_real, sums_imag = lax.psum((input_gain * tail_real, input_gain * tail_imag), "seqin")
    span_real, span_imag = power_pair(fade_rate, turn_rate, float(block_len))
    ones_like = jnp.ones_like(span_real)
    zeros_like = jnp.zeros_like(span_real)
    prior = carried_in(
        (span_real, span_imag, sums_real, sums_imag),
        "seqout",
        chain_step,
        (ones_like, zeros_like, zeros_like, zeros_like),
    )
    prior_real = prior[2]
    prior_imag = prior[3]
    block_places = (first_token + offsets).astype(jnp.float32)
    cols = FACTOR // parts_in
    rows_here = tokens // FACTOR
    full_len = 2 * block_len
    spec_rows = full_len // FACTOR
    half_rows = spec_rows // 2
    freq_here = spec_rows // parts_in
    col_start = place_in * cols
    row_cos, row_sin = turn_table(spec_rows, half_rows, spec_rows, 0, 0, -1.0)
    twist_cos, twist_sin = turn_table(spec_rows, cols, full_len, 0, col_start, -1.0)

    def columns_pass(tile_block):
        tile_block = tile_block.astype(jnp.float32)
        part_real = jnp.einsum("kr,rqc->kqc", row_cos, tile_block, precision=highest)
        part_imag = jnp.einsum("kr,rqc->kqc", row_sin, tile_block, precision=highest)
        twist_real = twist_cos[:, :, None]
        twist_imag = twist_sin[:, :, None]
        return (
            part_real * twist_real - part_imag * twist_imag,
            part_real * twist_imag + part_imag * twist_real,
        )

    wave_real, wave_imag = columns_pass(
        lax.all_to_all(
            signal.reshape(rows_here, FACTOR, channels),
            "seqin",
            split_axis=1,
            concat_axis=0,
            tiled=True,
        )
    )
    chan_share = channels // lax.axis_size("seqout")
    first_chan = place_out * chan_share

    def narrow(operand):
        return lax.dynamic_slice_in_dim(operand, first_chan, chan_share, 1)

    kernel_rows = powers_sum(
        block_places, narrow(fade_rate), narrow(turn_rate), narrow(weight_real), narrow(weight_imag)
    )
    kernel_kernel_rows = kernel_rows.reshape(rows_here, FACTOR, chan_share)
    kern_real, kern_imag = columns_pass(
        lax.all_to_all(kernel_kernel_rows, "seqin", split_axis=1, concat_axis=0, tiled=True)
    )
    wave_real, wave_imag, kern_real, kern_imag = (
        lax.all_to_all(wave_real, "seqin", split_axis=0, concat_axis=1, tiled=True),
        lax.all_to_all(wave_imag, "seqin", split_axis=0, concat_axis=1, tiled=True),
        lax.all_to_all(kern_real, "seqin", split_axis=0, concat_axis=1, tiled=True),
        lax.all_to_all(kern_imag, "seqin", split_axis=0, concat_axis=1, tiled=True),
    )
    forward_table = turn_table(FACTOR, FACTOR, FACTOR, 0, 0, -1.0)
    wave_hat = complex_mix("kq,aqc->akc", forward_table, (wave_real, wave_imag))
    kern_hat = complex_mix("kq,aqc->akc", forward_table, (kern_real, kern_imag))
    kern_hat = (
        lax.all_gather(kern_hat[0], "seqout", axis=2, tiled=True),
        lax.all_gather(kern_hat[1], "seqout", axis=2, tiled=True),
    )
    product_real = wave_hat[0] * kern_hat[0] - wave_hat[1] * kern_hat[1]
    product_imag = wave_hat[0] * kern_hat[1] + wave_hat[1] * kern_hat[0]
    backward_table = turn_table(FACTOR, FACTOR, FACTOR, 0, 0, 1.0)
    mixed = complex_mix("qk,akc->aqc", backward_table, (product_real, product_imag))
    back_cos, back_sin = turn_table(freq_here, FACTOR, full_len, place_in * freq_here, 0, 1.0)
    turned_real = mixed[0] * back_cos[:, :, None] - mixed[1] * back_sin[:, :, None]
    turned_imag = mixed[0] * back_sin[:, :, None] + mixed[1] * back_cos[:, :, None]
    out_cos, out_sin = turn_table(half_rows, spec_rows, spec_rows, 0, 0, 1.0)
    operand = (
        lax.all_to_all(turned_real, "seqin", split_axis=1, concat_axis=0, tiled=True),
        lax.all_to_all(turned_imag, "seqin", split_axis=1, concat_axis=0, tiled=True),
    )
    real_part = jnp.einsum("rk,kqc->rqc", out_cos, operand[0], precision=highest)
    real_part = real_part - jnp.einsum("rk,kqc->rqc", out_sin, operand[1], precision=highest)
    spatial = real_part * (1.0 / full_len)
    convolved = lax.all_to_all(spatial, "seqin", split_axis=0, concat_axis=1, tiled=True).reshape(
        tokens, channels
    )
    lead_real = output_real * prior_real - output_imag * prior_imag
    lead_imag = output_real * prior_imag + output_imag * prior_real
    carried = powers_sum(block_places + 1.0, fade_rate, turn_rate, lead_real, lead_imag)
    result_sum = convolved + carried
    outputs = result_sum + skip_gain[None, :] * values
    return outputs[None].astype(jnp.float32)


def solution(mesh):
    in_specs = (
        P(("groups", "seqout"), "seqin", "chan"),
        P("chan"),
        P(None, "chan"),
        P(None, "chan"),
        P(None, "chan"),
        P(None, "chan"),
        P("chan"),
    )
    out_specs = P(("groups", "seqout"), "seqin", "chan")
    return jax.shard_map(
        per_device, mesh=mesh, in_specs=in_specs, out_specs=out_specs, check_vma=False
    )
```

profile of v0, /device:TPU:0, one launch (start us, length us, event | category | flops | bytes accessed | tf_op | source)
XLA Modules:
  0.0 506.6 jit_solution(16399703461314192884)
XLA Ops:
  14.2 37.0 %fusion.11 = f32[1024,32,8]{1,2,0:T(8,128)} fusion(bf16[8,16,1024]{1,0,2:T(8,128)(2,1)S(1)} %copy.236, f32[16]{0:T(128)S(1)} %slice_subtract_fusion, f32[32,1024]{0,1:T(8,128)S(1)} %copy.235, f32[32,1024]{0,1:T(8,128)} %copy.234), kind=kOutput, calls=%fused_computation.19 | convolution fusion | flops 51904512 | bytes 1572928 | tf_op jit(solution)/shard_map/unc,auc->anc/dot_general | solution.py:58
  51.1 36.3 %fusion.14 = f32[1024,32,8]{1,2,0:T(8,128)} fusion(bf16[8,16,1024]{1,0,2:T(8,128)(2,1)S(1)} %copy.236, f32[16]{0:T(128)S(1)} %slice_subtract_fusion, f32[32,1024]{0,1:T(8,128)S(1)} %copy.235, f32[32,1024]{0,1:T(8,128)S(1)} %copy-done.5), kind=kOutput, calls=%fused_computation.21 | convolution fusion | flops 51904512 | bytes 1572928 | tf_op jit(solution)/shard_map/unc,auc->anc/dot_general | solution.py:59
  90.3 2.8 copy.239
  93.3 4.4 fusion.70
  99.6 29.0 %fusion.17 = f32[512,16,8]{1,2,0:T(8,128)S(1)} fusion(f32[32,512]{0,1:T(8,128)S(1)} %copy.215, f32[16]{0:T(128)S(1)} %slice_subtract_fusion.2, f32[32,512]{0,1:T(8,128)S(1)} %copy.214, f32[32,512]{0,1:T(8,128)S(1)} %copy.219, f32[8]{0:T(128)S(1)} %slice_reduce_fusion.2, f32[32,512]{0,1:T(8,128)S(1)} %copy.216), kind=kOutput, calls=%fused_computation.27 | convolution fusion | flops 26869760 | bytes 524384 | tf_op jit(solution)/shard_map/anc,unc->auc/dot_general | solution.py:49
  128.6 29.0 %multiply_bitcast_fusion.1 = f32[8,16,512]{1,0,2:T(8,128)S(1)} fusion(f32[512,16,8]{1,2,0:T(8,128)S(1)} %fusion.17, f32[32,512]{0,1:T(8,128)S(1)} %copy.215, f32[16]{0:T(128)S(1)} %slice_subtract_fusion.2, f32[32,512]{0,1:T(8,128)S(1)} %copy.214, f32[32,512]{0,1:T(8,128)S(1)} %copy.219, f32[8]{0:T(128)S(1)} %slice_reduce_fusion.2, f32[32,512]{0,1:T(8,128)S(1)} %copy.216), kind=kOutput, calls=%fused_computation.48 | convolution fusion | flops 27000832 | bytes 786528 | tf_op jit(solution)/shard_map/anc,unc->auc/dot_general | solution.py:50
  159.3 6.3 %all-to-all-start.3 = ((f32[2,64,512]{2,0,1:T(2,128)}), f32[2,64,512]{2,0,1:T(2,128)S(1)}, u32[]{:S(2)}, u32[]{:S(2)}) async-start(f32[2,64,512]{2,0,1:T(2,128)} %copy.221), calls=%async_computation.3 | async-start | bytes 524288 | tf_op jit(solution)/shard_map/all_to_all | solution.py:164
  166.7 7.8 %all-to-all-done.3 = f32[2,64,512]{2,0,1:T(2,128)S(1)} async-done(((f32[2,64,512]{2,0,1:T(2,128)}), f32[2,64,512]{2,0,1:T(2,128)S(1)}, u32[]{:S(2)}, u32[]{:S(2)}) %all-to-all-start.3) | async-done | bytes 262176 | tf_op jit(solution)/shard_map/all_to_all | solution.py:164
  174.5 3.4 all-to-all-start
  180.9 3.9 all-to-all-done
  184.9 3.5 all-to-all-start.4
  189.5 10.6 %all-to-all-done.4 = f32[16,16,512]{2,1,0:T(8,128)S(1)} async-done(((f32[16,16,512]{2,1,0:T(8,128)}), f32[16,16,512]{2,1,0:T(8,128)S(1)}, u32[]{:S(2)}, u32[]{:S(2)}) %all-to-all-start.4) | async-done | bytes 524320 | tf_op jit(solution)/shard_map/all_to_all | solution.py:169
  200.1 3.5 all-to-all-start.5
  207.1 8.7 %all-to-all-done.5 = f32[16,16,512]{2,1,0:T(8,128)S(1)} async-done(((f32[16,16,512]{2,1,0:T(8,128)}), f32[16,16,512]{2,1,0:T(8,128)S(1)}, u32[]{:S(2)}, u32[]{:S(2)}) %all-to-all-start.5) | async-done | bytes 524320 | tf_op jit(solution)/shard_map/all_to_all | solution.py:170
  216.6 3.5 all-to-all-start.1
  221.8 21.8 %all-to-all-done.1 = f32[16,16,1024]{2,1,0:T(8,128)S(1)} async-done(((f32[16,16,1024]{2,1,0:T(8,128)}), f32[16,16,1024]{2,1,0:T(8,128)S(1)}, u32[]{:S(2)}, u32[]{:S(2)}) %all-to-all-start.1) | async-done | bytes 1048608 | tf_op jit(solution)/shard_map/all_to_all | solution.py:167
  243.6 3.5 all-to-all-start.2
  253.7 18.6 %all-to-all-done.2 = f32[16,16,1024]{2,1,0:T(8,128)S(1)} async-done(((f32[16,16,1024]{2,1,0:T(8,128)}), f32[16,16,1024]{2,1,0:T(8,128)S(1)}, u32[]{:S(2)}, u32[]{:S(2)}) %all-to-all-start.2) | async-done | bytes 1048608 | tf_op jit(solution)/shard_map/all_to_all | solution.py:168
  276.1 20.3 %all-gather.7.cloned.1.call-done = f32[4,64,1024]{2,1,0:T(8,128)} async-done(((f32[4,64,512]{2,1,0:T(8,128)}), f32[4,64,1024]{2,1,0:T(8,128)}) %all-gather.7.cloned.1.call-update) | async-done | bytes 1048592 | tf_op jit(solution)/shard_map/all_gather | solution.py:177
  296.3 3.3 multiply_subtract_fusion.1
  306.8 4.6 all-to-all-start.6
  312.1 5.7 %all-gather = f32[64,1024]{1,0:T(8,128)S(1)} all-gather(f32[32,1024]{1,0:T(8,128)S(1)} %copy-done.8), channel_id=2, replica_groups=mesh['groups'=2,'seqin'=4,'seqout'=2,'chan'=2] {'seqout'}, dimensions={0}, use_global_device_ids=true | all-gather | bytes 393216 | tf_op jit(solution)/shard_map/all_gather | solution.py:16
  319.4 22.0 %all-to-all-done.6 = f32[4,64,1024]{2,0,1:T(4,128)S(1)} async-done(((f32[4,64,1024]{2,0,1:T(4,128)}), f32[4,64,1024]{2,0,1:T(4,128)S(1)}, u32[]{:S(2)}, u32[]{:S(2)}) %all-to-all-start.6) | async-done | bytes 1048608 | tf_op jit(solution)/shard_map/all_to_all | solution.py:188
  341.4 4.2 all-to-all-start.7
  345.7 5.6 %all-gather.1 = f32[64,1024]{1,0:T(8,128)S(1)} all-gather(f32[32,1024]{1,0:T(8,128)S(1)} %copy-done.7), channel_id=3, replica_groups=mesh['groups'=2,'seqin'=4,'seqout'=2,'chan'=2] {'seqout'}, dimensions={0}, use_global_device_ids=true | all-gather | bytes 393216 | tf_op jit(solution)/shard_map/all_gather | solution.py:16
  351.5 12.0 %all-reduce.3.cloned.1.call-done = (f32[1,32,1024]{2,1,0:T(8,128)}, f32[1,32,1024]{2,1,0:T(8,128)}) async-done(((f32[1,32,1024]{2,1,0:T(8,128)}, f32[1,32,1024]{2,1,0:T(8,128)}), (f32[1,32,1024]{2,1,0:T(8,128)}, f32[1,32,1024]{2,1,0:T(8,128)})) %all-reduce.3.cloned.1.call-update) | async-done | bytes 262160 | tf_op jit(solution)/shard_map/psum | solution.py:110
  363.5 5.8 %all_gather.37 = f32[2,32,1024]{2,1,0:T(8,128)S(1)} all-gather(f32[1,32,1024]{2,1,0:T(8,128)} %get-tuple-element.200), channel_id=1, replica_groups=mesh['groups'=2,'seqin'=4,'seqout'=2,'chan'=2] {'seqout'}, dimensions={0}, use_global_device_ids=true | all-gather | bytes 393216 | tf_op jit(solution)/shard_map/all_gather | solution.py:16
  369.4 5.8 %all_gather.39 = f32[2,32,1024]{2,1,0:T(8,128)S(1)} all-gather(f32[1,32,1024]{2,1,0:T(8,128)} %get-tuple-element.201), channel_id=1, replica_groups=mesh['groups'=2,'seqin'=4,'seqout'=2,'chan'=2] {'seqout'}, dimensions={0}, use_global_device_ids=true | all-gather | bytes 393216 | tf_op jit(solution)/shard_map/all_gather | solution.py:16
  375.5 5.0 multiply_add_fusion
  389.6 10.1 %all-to-all-start.8 = ((f32[8,16,1024]{2,1,0:T(8,128)}), f32[8,16,1024]{2,1,0:T(8,128)S(1)}, u32[]{:S(2)}, u32[]{:S(2)}) async-start(f32[8,16,1024]{2,1,0:T(8,128)} %copy.232), calls=%async_computation.8 | async-start | bytes 1048576 | tf_op jit(solution)/shard_map/all_to_all | solution.py:194
  399.7 46.2 %fusion.5 = f32[1024,16,8]{1,2,0:T(8,128)} fusion(f32[8,32,1024]{1,0,2:T(8,128)} %copy.244, f32[32,1024]{0,1:T(8,128)S(1)} %copy-done.4, f32[16]{0:T(128)S(1)} %slice_subtract_fusion.1, f32[32,1024]{0,1:T(8,128)} %copy.234), kind=kOutput, calls=%fused_computation.15 | convolution fusion | flops 51904512 | bytes 1835072 | tf_op jit(solution)/shard_map/anc,unc->auc/dot_general | solution.py:49
  448.6 46.5 %multiply_bitcast_fusion = f32[8,16,1024]{1,0,2:T(8,128)} fusion(f32[1024,16,8]{1,2,0:T(8,128)} %fusion.5, f32[8,32,1024]{1,0,2:T(8,128)} %copy.245, f32[32,1024]{0,1:T(8,128)S(1)} %copy-done.4, f32[16]{0:T(128)S(1)} %slice_subtract_fusion.1, f32[32,1024]{0,1:T(8,128)S(1)} %copy-done.6), kind=kOutput, calls=%fused_computation.30 | convolution fusion | flops 52166656 | bytes 2359360 | tf_op jit(solution)/shard_map/anc,unc->auc/dot_general | solution.py:50
  (118 shorter events, 60.2 us)
Async XLA Ops:
  8.4 84.9 %copy-start.1 = (f32[32,1024]{1,0:T(8,128)}, f32[32,1024]{1,0:T(8,128)S(1)}, u32[]{:S(2)}) copy-start(f32[32,1024]{1,0:T(8,128)S(1)} %get-tuple-element.202) | copy-start | bytes 393220
  10.6 40.5 %copy-start.3 = (f32[32,1024]{0,1:T(8,128)}, f32[32,1024]{0,1:T(8,128)S(1)}, u32[]{:S(2)}) copy-start(f32[32,1024]{0,1:T(8,128)S(1)} %copy.235) | copy-start | bytes 393220
  14.1 37.0 %copy-start.5 = (f32[32,1024]{0,1:T(8,128)S(1)}, f32[32,1024]{0,1:T(8,128)}, u32[]{:S(2)}) copy-start(f32[32,1024]{0,1:T(8,128)} %copy.234) | copy-start | bytes 393220
  90.2 8.7 %copy-start.9 = (f32[32,1024]{1,0:T(8,128)S(1)}, f32[32,1024]{1,0:T(8,128)}, u32[]{:S(2)}) copy-start(f32[32,1024]{1,0:T(8,128)} %param.13) | copy-start | bytes 393220
  90.2 8.7 %copy-start.11 = (f32[32,1024]{1,0:T(8,128)S(1)}, f32[32,1024]{1,0:T(8,128)}, u32[]{:S(2)}) copy-start(f32[32,1024]{1,0:T(8,128)} %param.14) | copy-start | bytes 393220
  128.6 37.0 %copy-start = (bf16[1,128,1024]{2,1,0:T(8,128)(2,1)S(1)}, bf16[1,128,1024]{2,1,0:T(8,128)(2,1)}, u32[]{:S(2)}) copy-start(bf16[1,128,1024]{2,1,0:T(8,128)(2,1)} %param.9) | copy-start | bytes 786436
  159.3 15.2 %all-to-all-start.3 = ((f32[2,64,512]{2,0,1:T(2,128)}), f32[2,64,512]{2,0,1:T(2,128)S(1)}, u32[]{:S(2)}, u32[]{:S(2)}) async-start(f32[2,64,512]{2,0,1:T(2,128)} %copy.221), calls=%async_computation.3 | async-start | bytes 524288 | tf_op jit(solution)/shard_map/all_to_all | solution.py:164
  174.5 10.4 %all-to-all-start = ((bf16[2,64,1024]{2,0,1:T(2,128)(2,1)}), bf16[2,64,1024]{2,0,1:T(2,128)(2,1)S(1)}, u32[]{:S(2)}, u32[]{:S(2)}) async-start(bf16[2,64,1024]{2,0,1:T(2,128)(2,1)} %copy.207), calls=%async_computation | async-start | bytes 524288 | tf_op jit(solution)/shard_map/all_to_all | solution.py:145
  184.9 15.2 %all-to-all-start.4 = ((f32[16,16,512]{2,1,0:T(8,128)}), f32[16,16,512]{2,1,0:T(8,128)S(1)}, u32[]{:S(2)}, u32[]{:S(2)}) async-start(f32[16,16,512]{2,1,0:T(8,128)} %copy.224), calls=%async_computation.4 | async-start | bytes 1048576 | tf_op jit(solution)/shard_map/all_to_all | solution.py:169
  200.1 15.7 %all-to-all-start.5 = ((f32[16,16,512]{2,1,0:T(8,128)}), f32[16,16,512]{2,1,0:T(8,128)S(1)}, u32[]{:S(2)}, u32[]{:S(2)}) async-start(f32[16,16,512]{2,1,0:T(8,128)} %copy.226), calls=%async_computation.5 | async-start | bytes 1048576 | tf_op jit(solution)/shard_map/all_to_all | solution.py:170
  215.8 0.8 copy-start.2
  216.6 27.0 %all-to-all-start.1 = ((f32[16,16,1024]{2,1,0:T(8,128)}), f32[16,16,1024]{2,1,0:T(8,128)S(1)}, u32[]{:S(2)}, u32[]{:S(2)}) async-start(f32[16,16,1024]{2,1,0:T(8,128)} %copy.210), calls=%async_computation.1 | async-start | bytes 2097152 | tf_op jit(solution)/shard_map/all_to_all | solution.py:167
  243.6 28.7 %all-to-all-start.2 = ((f32[16,16,1024]{2,1,0:T(8,128)}), f32[16,16,1024]{2,1,0:T(8,128)S(1)}, u32[]{:S(2)}, u32[]{:S(2)}) async-start(f32[16,16,1024]{2,1,0:T(8,128)} %copy.212), calls=%async_computation.2 | async-start | bytes 2097152 | tf_op jit(solution)/shard_map/all_to_all | solution.py:168
  247.1 29.0 %all-gather.5.cloned.1.call-start = ((), (), s32[]{:S(2)}) async-start(), calls=%async_computation.9 | async-start | bytes 1572864 | tf_op jit(solution)/shard_map/all_gather | solution.py:176
  250.6 45.7 %all-gather.7.cloned.1.call-start = ((), (), s32[]{:S(2)}) async-start(), calls=%async_computation.10 | async-start | bytes 1572864 | tf_op jit(solution)/shard_map/all_gather | solution.py:177
  303.3 8.7 %copy-start.8 = (f32[32,1024]{1,0:T(8,128)S(1)}, f32[32,1024]{1,0:T(8,128)}, u32[]{:S(2)}) copy-start(f32[32,1024]{1,0:T(8,128)} %get-tuple-element.222) | copy-start | bytes 393220
  305.0 40.7 %copy-start.7 = (f32[32,1024]{1,0:T(8,128)S(1)}, f32[32,1024]{1,0:T(8,128)}, u32[]{:S(2)}) copy-start(f32[32,1024]{1,0:T(8,128)} %get-tuple-element.204) | copy-start | bytes 393220
  306.8 34.6 %all-to-all-start.6 = ((f32[4,64,1024]{2,0,1:T(4,128)}), f32[4,64,1024]{2,0,1:T(4,128)S(1)}, u32[]{:S(2)}, u32[]{:S(2)}) async-start(f32[4,64,1024]{2,0,1:T(4,128)} %copy.228), calls=%async_computation.6 | async-start | bytes 2097152 | tf_op jit(solution)/shard_map/all_to_all | solution.py:188
  311.4 52.1 %all-reduce.3.cloned.1.call-start = ((), (), s32[]{:S(2)}) async-start(), calls=%async_computation.11 | async-start | bytes 524288 | tf_op jit(solution)/shard_map/psum | solution.py:110
  319.4 56.0 %copy-start.10 = (f32[32,1024]{1,0:T(8,128)S(1)}, f32[32,1024]{1,0:T(8,128)}, u32[]{:S(2)}) copy-start(f32[32,1024]{1,0:T(8,128)} %param.13) | copy-start | bytes 393220
  319.4 56.0 %copy-start.12 = (f32[32,1024]{1,0:T(8,128)S(1)}, f32[32,1024]{1,0:T(8,128)}, u32[]{:S(2)}) copy-start(f32[32,1024]{1,0:T(8,128)} %param.14) | copy-start | bytes 393220
  341.4 43.6 %all-to-all-start.7 = ((f32[4,64,1024]{2,0,1:T(4,128)}), f32[4,64,1024]{2,0,1:T(4,128)}, u32[]{:S(2)}, u32[]{:S(2)}) async-start(f32[4,64,1024]{2,0,1:T(4,128)} %copy.230), calls=%async_computation.7 | async-start | bytes 2097152 | tf_op jit(solution)/shard_map/all_to_all | solution.py:189
  386.8 12.9 %copy-start.4 = (f32[32,1024]{0,1:T(8,128)S(1)}, f32[32,1024]{0,1:T(8,128)}, u32[]{:S(2)}) copy-start(f32[32,1024]{0,1:T(8,128)} %copy-done.3) | copy-start | bytes 393220
  389.6 108.4 %all-to-all-start.8 = ((f32[8,16,1024]{2,1,0:T(8,128)}), f32[8,16,1024]{2,1,0:T(8,128)S(1)}, u32[]{:S(2)}, u32[]{:S(2)}) async-start(f32[8,16,1024]{2,1,0:T(8,128)} %copy.232), calls=%async_computation.8 | async-start | bytes 1048576 | tf_op jit(solution)/shard_map/all_to_all | solution.py:194
  445.9 2.7 copy-start.6
  495.2 2.9 copy-start.13
Sparse Core Ops, SparseCore 0:
  250.7 22.6 all-gather.4
  275.0 21.2 all-gather.6
Sparse Core Ops, SparseCore 1:
  314.2 49.2 all-reduce.2
where the time goes:
time: 514 us; the launch traced here: 507 us
  matrix products  247 us (48%)
  waiting for transfers between devices  126 us (25%)
  starting transfers between devices  43.1 us (8%)
  local copies, waits for them, and re-layouts  36.2 us (7%)
  blocking collectives  23 us (4%)
  between operations  15.7 us (3%)
  other arithmetic  15.2 us (3%)
    dot_general x2, matrix products, powers_sum(): second = jnp.einsum('anc,unc->auc', lead_imag, near_imag, precision=highest)  75.6 us
    dot_general x2, matrix products, powers_sum(): first = jnp.einsum('anc,unc->auc', lead_real, near_real, precision=highest)  75.2 us
    dot_general x1, matrix products, state_sums(): jnp.einsum('unc,auc->anc', near_real, grouped, precision=highest)  37 us
    dot_general x1, matrix products, state_sums(): jnp.einsum('unc,auc->anc', near_imag, grouped, precision=highest)  36.3 us
    all_gather x4, blocking collectives, carried_in(): everything = jax.tree.map(lambda part: lax.all_gather(part, axis), shard)  23 us
    all_to_all x1, waiting for transfers between devices, per_device(): lax.all_to_all(turned_real, 'seqin', split_axis=1, concat_axis=0, tiled=T...  22 us
    all_to_all x1, waiting for transfers between devices, per_device(): lax.all_to_all(wave_real, 'seqin', split_axis=0, concat_axis=1, tiled=True)  21.8 us
    all_gather x1, waiting for transfers between devices, per_device(): lax.all_gather(kern_hat[1], 'seqout', axis=2, tiled=True)  20.3 us
  transfers between devices with their start and end apart: 12, of which 9 were waited for; matrix products, arithmetic and copies ran while one was open for 26% of the time, Pallas kernels for 0%

commit v1 on v0

v1 whole, which is shorter than its diff:
```python
import functools

import jax
import jax.numpy as jnp
from jax import lax
from jax.experimental import pallas as pl
from jax.experimental.pallas import tpu as pltpu
from jax.sharding import PartitionSpec as P

LANES = 128
NEAR = 16
SEQ_AXES = ("seqin", "seqout")


def cmul(a, b):
    return (a[0] * b[0] - a[1] * b[1], a[0] * b[1] + a[1] * b[0])


def cos_sin(angle):
    turns = jnp.floor(angle * 0.6366197723675814 + 0.5)
    rest = angle - turns * 1.5703125
    rest = rest - turns * 4.837512969970703125e-4
    rest = rest - turns * 7.549789948768648e-8
    square = rest * rest
    sine = rest + rest * square * (
        -1.6666654611e-1 + square * (8.3321608736e-3 - square * 1.9515295891e-4)
    )
    cosine = (
        1.0
        - 0.5 * square
        + square * square * (4.166664568298827e-2 + square * (-1.388731625493765e-3 + square * 2.443315711809948e-5))
    )
    quarter = turns.astype(jnp.int32) & 3
    swap = (quarter & 1) == 1
    first = jnp.where(swap, sine, cosine)
    second = jnp.where(swap, cosine, sine)
    return (
        jnp.where((quarter == 1) | (quarter == 2), -first, first),
        jnp.where(quarter >= 2, -second, second),
    )


def decay_step(time_step, decay_rate, frequency):
    fade_rate = time_step * decay_rate
    shrink = jnp.exp(-fade_rate)
    cosine, sine = cos_sin(time_step * frequency)
    return (fade_rate, (shrink * cosine, shrink * sine))


def gain_of(fade_rate):
    double = 2.0 * fade_rate
    series = 1.0 / 40320.0
    for factor in (5040.0, 720.0, 120.0, 24.0, 6.0, 2.0, 1.0):
        series = 1.0 / factor - double * series
    small = double * series
    return jnp.sqrt(jnp.where(double < 0.25, small, 1.0 - jnp.exp(-double)))


def power_list(lam, count):
    powers = [None, lam]
    for k in range(2, count + 1):
        powers.append(cmul(powers[k // 2], powers[k - k // 2]))
    return powers


def spread_rows(source_ref, target_ref, rows, groups, stack):
    for start in range(0, rows, stack):
        for k in range(groups):
            part = source_ref[start : start + stack, k * LANES : (k + 1) * LANES]
            target_ref[pl.ds(start * groups + k, stack, stride=groups), :] = part.astype(jnp.float32)


def store_powers(near_ref, n, powers, groups):
    for u in range(1, NEAR):
        for part in range(2):
            row = pl.multiple_of((n * (2 * NEAR) + 2 * u + part) * groups, groups)
            near_ref[pl.ds(row, groups), :] = powers[u][part]


def power_sum(near_ref, lead_ref, states, outer, groups, start_of, emit):
    u_tile, a_tile = 8, min(4, outer)
    for u0 in range(0, NEAR, u_tile):
        for a0 in range(0, outer, a_tile):

            def turn(n, acc, u0=u0, a0=a0):
                def near(u, part):
                    row = pl.multiple_of((n * (2 * NEAR) + 2 * u + part) * groups, groups)
                    return near_ref[pl.ds(row, groups), :]

                def lead(a, part):
                    row = pl.multiple_of((n * (2 * outer) + 2 * a + part) * groups, groups)
                    return lead_ref[pl.ds(row, groups), :]

                leads = [(lead(a0 + a, 0), lead(a0 + a, 1)) for a in range(a_tile)]
                acc = list(acc)
                for u in range(u_tile):
                    if u0 + u == 0:
                        for a in range(a_tile):
                            acc[u * a_tile + a] = acc[u * a_tile + a] + leads[a][0]
                        continue
                    real, imag = near(u0 + u, 0), near(u0 + u, 1)
                    for a in range(a_tile):
                        slot = u * a_tile + a
                        acc[slot] = acc[slot] + leads[a][0] * real - leads[a][1] * imag
                return tuple(acc)

            init = tuple(
                start_of((a0 + a) * NEAR + u0 + u) for u in range(u_tile) for a in range(a_tile)
            )
            acc = lax.fori_loop(0, states, turn, init)
            for u in range(u_tile):
                for a in range(a_tile):
                    emit((a0 + a) * NEAR + u0 + u, acc[u * a_tile + a])


def tables_kernel(
    width, step_ref, decay_ref, freq_ref, real_ref, imag_ref,
    taps_ref, seed_ref, mid_ref,
    decay_sp, freq_sp, real_sp, imag_sp, near_ref, lead_ref,
):
    states = decay_ref.shape[0]
    groups = decay_ref.shape[1] // LANES
    outer = taps_ref.shape[0] // groups // NEAR
    if width == LANES:
        place = lax.axis_index("seqin") * lax.axis_size("seqout") + lax.axis_index("seqout")
        own = pl.ds(pl.multiple_of(place * LANES, LANES), LANES)
        fade, lam = decay_step(step_ref[pl.ds(place, 1), :], decay_ref[:, own], freq_ref[:, own])
        mid_ref[0:states, :] = lam[0]
        mid_ref[states : 2 * states, :] = lam[1]
        mid_ref[2 * states : 3 * states, :] = gain_of(fade)
    for source, target in ((decay_ref, decay_sp), (freq_ref, freq_sp), (real_ref, real_sp), (imag_ref, imag_sp)):
        spread_rows(source, target, states, groups, 8)
    step = step_ref[...]

    def prepare(n, carry):
        at = pl.ds(pl.multiple_of(n * groups, groups), groups)
        fade, lam = decay_step(step, decay_sp[at, :], freq_sp[at, :])
        powers = power_list(lam, NEAR)
        store_powers(near_ref, n, powers, groups)
        weight = (2.0 * real_sp[at, :], 2.0 * imag_sp[at, :])
        shifted = cmul(weight, lam)
        for part in range(2):
            row = pl.multiple_of((n * 4 + part) * groups, groups)
            seed_ref[pl.ds(row, groups), :] = lam[part]
            row = pl.multiple_of((n * 4 + 2 + part) * groups, groups)
            seed_ref[pl.ds(row, groups), :] = shifted[part]
        gain = gain_of(fade)
        lead = (weight[0] * gain, weight[1] * gain)
        for a in range(outer):
            if a:
                lead = cmul(lead, powers[NEAR])
            for part in range(2):
                row = pl.multiple_of((n * (2 * outer) + 2 * a + part) * groups, groups)
                lead_ref[pl.ds(row, groups), :] = lead[part]
        return carry

    lax.fori_loop(0, states, prepare, 0)
    zero = jnp.zeros((groups, LANES), jnp.float32)

    def emit(t, value):
        taps_ref[t * groups : (t + 1) * groups, :] = value

    power_sum(near_ref, lead_ref, states, outer, groups, lambda t: zero, emit)


def conv_kernel(signal_ref, taps_ref, skip_ref, out_ref, signal_sp, taps_pad):
    tokens, channels = signal_ref.shape
    groups = channels // LANES
    tile = 8
    spread_rows(signal_ref, signal_sp, tokens, groups, 16)
    taps_pad[0 : tile * groups, :] = jnp.zeros((tile * groups, LANES), jnp.float32)
    taps_pad[tile * groups : (tile + tokens) * groups, :] = taps_ref[...]
    skip = skip_ref[...]

    def value(t):
        return signal_sp[pl.ds(pl.multiple_of(t * groups, groups), groups), :]

    def row_tile(ti, carry):
        def col_tile(ji, acc):
            gap = (ti - ji) * tile + 1
            window = [
                taps_pad[pl.ds(pl.multiple_of((gap + m) * groups, groups), groups), :]
                for m in range(2 * tile - 1)
            ]
            acc = list(acc)
            for j in range(tile):
                drive = value(ji * tile + j)
                for t in range(tile):
                    acc[t] = acc[t] + window[t - j + tile - 1] * drive
            return tuple(acc)

        acc = lax.fori_loop(0, ti + 1, col_tile, tuple(skip * value(ti * tile + t) for t in range(tile)))
        for t in range(tile):
            row = pl.multiple_of((ti * tile + t) * groups, groups)
            out_ref[pl.ds(row, groups), :] = acc[t]
        return carry

    lax.fori_loop(0, tokens // tile, row_tile, 0)


def states_kernel(n_in, n_out, tokens, signal_ref, mid_ref, out_ref, signal_f, near_ref):
    states = mid_ref.shape[0] // 3
    width = mid_ref.shape[1]
    parts = n_in * n_out
    tiles = states // 8
    a_tile = 4
    signal_f[...] = signal_ref[...].astype(jnp.float32)
    lam = (mid_ref[0:states, :], mid_ref[states : 2 * states, :])
    gain = mid_ref[2 * states : 3 * states, :]
    powers = power_list(lam, NEAR)
    for u in range(1, NEAR):
        for part in range(2):
            near_ref[2 * u + part] = powers[u][part]
    hop1 = powers[NEAR]
    hop2 = cmul(hop1, hop1)
    hop3 = cmul(hop1, hop2)
    hop4 = cmul(hop2, hop2)
    hops = [None, hop1, hop2, hop3]
    per_part = tokens // (NEAR * a_tile)

    def advance(base, state):
        real = [None] * a_tile
        imag = [None] * a_tile
        for u in range(NEAR):
            drive = [
                jnp.broadcast_to(signal_f[pl.ds(base + a * NEAR + u, 1), :], (states, width))
                for a in range(a_tile)
            ]
            power = NEAR - 1 - u
            if power:
                near_real, near_imag = near_ref[2 * power], near_ref[2 * power + 1]
            for a in range(a_tile):
                if power:
                    add_real, add_imag = near_real * drive[a], near_imag * drive[a]
                    real[a] = add_real if real[a] is None else real[a] + add_real
                    imag[a] = add_imag if imag[a] is None else imag[a] + add_imag
                else:
                    real[a] = real[a] + drive[a]
        total = (real[a_tile - 1], imag[a_tile - 1])
        for a in range(a_tile - 1):
            moved = cmul(hops[a_tile - 1 - a], (real[a], imag[a]))
            total = (total[0] + moved[0], total[1] + moved[1])
        moved = cmul(hop4, state)
        return (moved[0] + total[0], moved[1] + total[1])

    def part_turn(s, state):
        place = lax.rem(s, n_in) * n_out + s // n_in
        out_ref[place, 0:states, :] = gain * state[0]
        out_ref[place, states : 2 * states, :] = gain * state[1]

        def inside(i, state):
            base = pl.multiple_of(place * tokens + i * (a_tile * NEAR), a_tile * NEAR)
            return advance(base, state)

        return lax.fori_loop(0, per_part, inside, state)

    zero = jnp.zeros((states, width), jnp.float32)
    state = lax.fori_loop(0, parts - 1, part_turn, (zero, zero))
    out_ref[parts - 1, 0:states, :] = gain * state[0]
    out_ref[parts - 1, states : 2 * states, :] = gain * state[1]


def final_kernel(local_ref, seed_ref, state_ref, out_ref, near_ref, lead_ref, rows_ref):
    tokens = out_ref.shape[0]
    groups = out_ref.shape[1] // LANES
    states = seed_ref.shape[0] // (4 * groups)
    outer = tokens // NEAR

    def prepare(n, carry):
        def seed(i):
            return seed_ref[pl.ds(pl.multiple_of((n * 4 + i) * groups, groups), groups), :]

        lam, weight = (seed(0), seed(1)), (seed(2), seed(3))
        powers = power_list(lam, NEAR)
        store_powers(near_ref, n, powers, groups)
        entering = tuple(
            state_ref[pl.ds(n + part * states, groups, stride=2 * states), :] for part in range(2)
        )
        lead = cmul(weight, entering)
        for a in range(outer):
            if a:
                lead = cmul(lead, powers[NEAR])
            for part in range(2):
                row = pl.multiple_of((n * (2 * outer) + 2 * a + part) * groups, groups)
                lead_ref[pl.ds(row, groups), :] = lead[part]
        return carry

    lax.fori_loop(0, states, prepare, 0)

    def start_of(t):
        return local_ref[t * groups : (t + 1) * groups, :]

    def emit(t, value):
        rows_ref[t * groups : (t + 1) * groups, :] = value

    power_sum(near_ref, lead_ref, states, outer, groups, start_of, emit)
    for start in range(0, tokens, 8):
        for k in range(groups):
            out_ref[start : start + 8, k * LANES : (k + 1) * LANES] = rows_ref[
                pl.ds(start * groups + k, 8, stride=groups), :
            ]


def per_device(n_in, n_out, inputs, time_step, decay_rate, frequency, output_real, output_imag, skip_gain):
    signal = inputs[0]
    tokens, channels = signal.shape
    states = decay_rate.shape[0]
    groups = channels // LANES
    parts = n_in * n_out
    width = channels // parts
    outer = tokens // NEAR
    f32 = jnp.float32
    params = pltpu.CompilerParams(vmem_limit_bytes=40 * 1024 * 1024)

    def rows(count, dtype=f32):
        return pltpu.VMEM((count * groups, LANES), dtype)

    def shape(*dims):
        return jax.ShapeDtypeStruct(dims, f32)

    whole = lax.all_to_all(signal, SEQ_AXES, split_axis=1, concat_axis=0, tiled=True)

    taps, seeds, mid = pl.pallas_call(
        functools.partial(tables_kernel, width),
        out_shape=(
            shape(tokens * groups, LANES),
            shape(states * 4 * groups, LANES),
            shape(3 * states, LANES),
        ),
        scratch_shapes=[rows(states)] * 4 + [rows(states * 2 * NEAR), rows(states * 2 * outer)],
        compiler_params=params,
        cost_estimate=pl.CostEstimate(flops=20_000_000, bytes_accessed=2_000_000, transcendentals=40_000),
        name="tables",
    )(time_step.reshape(groups, LANES), decay_rate, frequency, output_real, output_imag)

    if width != LANES:
        place = lax.axis_index("seqin") * n_out + lax.axis_index("seqout")

        def own(array):
            return lax.dynamic_slice_in_dim(array, place * width, width, array.ndim - 1)

        fade, lam = decay_step(own(time_step)[None, :], own(decay_rate), own(frequency))
        mid = jnp.concatenate([lam[0], lam[1], gain_of(fade)], axis=0)

    entering = pl.pallas_call(
        functools.partial(states_kernel, n_in, n_out, tokens),
        out_shape=shape(parts, 2 * states, width),
        scratch_shapes=[
            pltpu.VMEM((parts * tokens, width), f32),
            pltpu.VMEM((2 * NEAR, states, width), f32),
        ],
        compiler_params=params,
        cost_estimate=pl.CostEstimate(flops=16_000_000, bytes_accessed=1_000_000, transcendentals=0),
        name="states",
    )(whole, mid)

    taps, entering = lax.optimization_barrier((taps, entering))
    entering = lax.all_to_all(entering, SEQ_AXES, split_axis=0, concat_axis=0, tiled=True)
    if width != LANES:
        entering = entering.transpose(1, 0, 2).reshape(2 * states, groups, LANES).transpose(1, 0, 2)
    entering = entering.reshape(groups * 2 * states, LANES)

    local = pl.pallas_call(
        conv_kernel,
        out_shape=shape(tokens * groups, LANES),
        scratch_shapes=[rows(tokens), rows(tokens + 8)],
        compiler_params=params,
        cost_estimate=pl.CostEstimate(flops=18_000_000, bytes_accessed=2_000_000, transcendentals=0),
        name="conv",
    )(signal, taps, skip_gain.reshape(groups, LANES))

    outputs = pl.pallas_call(
        final_kernel,
        out_shape=shape(tokens, channels),
        scratch_shapes=[rows(states * 2 * NEAR), rows(states * 2 * outer), rows(tokens)],
        compiler_params=params,
        cost_estimate=pl.CostEstimate(flops=20_000_000, bytes_accessed=2_000_000, transcendentals=0),
        name="final",
    )(local, seeds, entering)
    return outputs[None]


def solution(mesh):
    in_specs = (
        P(("groups", "seqout"), "seqin", "chan"),
        P("chan"),
        P(None, "chan"),
        P(None, "chan"),
        P(None, "chan"),
        P(None, "chan"),
        P("chan"),
    )
    out_specs = P(("groups", "seqout"), "seqin", "chan")
    return jax.shard_map(
        functools.partial(per_device, mesh.shape["seqin"], mesh.shape["seqout"]),
        mesh=mesh,
        in_specs=in_specs,
        out_specs=out_specs,
        check_vma=False,
    )
```

time: 514 us -> 39.2 us (0.08); the launches traced: 507 us -> 38.8 us
  matrix products: 247 us -> 0 us
  waiting for transfers between devices: 126 us -> 9.13 us
  local copies, waits for them, and re-layouts: 36.2 us -> 1.77 us
  starting transfers between devices: 43.1 us -> 11.1 us
  blocking collectives: 23 us -> 0 us
  Pallas kernels: 0 us -> 16.7 us
  between operations: 15.7 us -> 0.09 us
  other arithmetic: 15.2 us -> 0 us
    dot_general x24 -> x0, matrix products: 247 us -> none  [the longest x2 75.6 us: powers_sum(): second = jnp.einsum('anc,unc->auc', lead_imag, near_imag, precision=highest)]
    all_to_all x9 -> x2, waiting for transfers between devices: 93.5 us -> 9.13 us  [the longest x1 5.47 us: per_device(): lax.all_to_all(entering, SEQ_AXES, split_axis=0, concat_axis=0, tiled=True)]
    all_to_all x9 -> x2, starting transfers between devices: 42.6 us -> 11.1 us  [the longest x1 7.4 us: per_device(): lax.all_to_all(signal, SEQ_AXES, split_axis=1, concat_axis=0, tiled=True)]
    all_gather x4 -> x0, blocking collectives: 23 us -> none  [carried_in(): everything = jax.tree.map(lambda part: lax.all_gather(part, axis), shard)]
    all_gather x2 -> x0, waiting for transfers between devices: 20.3 us -> none  [the longest x1 20.3 us: per_device(): lax.all_gather(kern_hat[1], 'seqout', axis=2, tiled=True)]
    pallas_call x0 -> x4, Pallas kernels: none -> 16.7 us  [the longest x1 5.51 us: per_device(): pl.pallas_call(final_kernel, out_shape=shape(tokens, channels), scratch_s...]
    psum x1 -> x0, waiting for transfers between devices: 12 us -> none  [per_device(): lax.psum((input_gain * tail_real, input_gain * tail_imag), 'seqin')]
    sub x4 -> x0, local copies, waits for them, and re-layouts: 7.25 us -> none  [the longest x1 2.71 us: powers_sum(): lead_real = real_part * far_real - imag_part * far_imag]
  transfers between devices with their start and end apart: 12 -> 2, of which waited for: 9 -> 2; matrix products, arithmetic and copies ran while one was open for 26% -> 0% of each run, Pallas kernels for 0% -> 21%
where the time goes in v1:
time: 39.2 us; the launch traced here: 38.8 us
  Pallas kernels  16.7 us (43%)
  starting transfers between devices  11.1 us (28%)
  waiting for transfers between devices  9.13 us (23%)
  local copies, waits for them, and re-layouts  1.77 us (5%)
    all_to_all x1, starting transfers between devices, per_device(): lax.all_to_all(signal, SEQ_AXES, split_axis=1, concat_axis=0, tiled=True)  7.4 us
    pallas_call x1, Pallas kernels, per_device(): pl.pallas_call(final_kernel, out_shape=shape(tokens, channels), scratch_s...  5.51 us
    all_to_all x1, waiting for transfers between devices, per_device(): lax.all_to_all(entering, SEQ_AXES, split_axis=0, concat_axis=0, tiled=True)  5.47 us
    pallas_call x1, Pallas kernels, per_device(): pl.pallas_call(functools.partial(tables_kernel, width), out_shape=(shape(...  5.21 us
    all_to_all x1, starting transfers between devices, per_device(): lax.all_to_all(entering, SEQ_AXES, split_axis=0, concat_axis=0, tiled=True)  3.72 us
    all_to_all x1, waiting for transfers between devices, per_device(): lax.all_to_all(signal, SEQ_AXES, split_axis=1, concat_axis=0, tiled=True)  3.66 us
    pallas_call x1, Pallas kernels, per_device(): pl.pallas_call(conv_kernel, out_shape=shape(tokens * groups, LANES), scra...  3.07 us
    pallas_call x1, Pallas kernels, per_device(): pl.pallas_call(functools.partial(states_kernel, n_in, n_out, tokens), out...  2.95 us
  transfers between devices with their start and end apart: 2, of which 2 were waited for; matrix products, arithmetic and copies ran while one was open for 0% of the time, Pallas kernels for 21%

profile of v1, /device:TPU:0, one launch (start us, length us, event | category | flops | bytes accessed | tf_op | source)
XLA Modules:
  0.0 38.8 jit_solution(3921492082103105263)
XLA Ops:
  0.0 1.0 %copy.9 = bf16[16,8,8,128]{3,2,1,0:T(8,128)(2,1)S(1)} copy(bf16[16,8,8,128]{3,1,2,0:T(8,128)(2,1)} %bitcast.11) | data formatting | bytes 524288
  1.0 0.0 copy-start.5
  1.0 0.7 %copy.8 = bf16[128,8,128]{2,0,1:T(8,128)(2,1)} copy(bf16[128,8,128]{2,1,0:T(8,128)(2,1)S(1)} %bitcast.17) | data formatting | bytes 524288 | tf_op jit(solution)/shard_map/all_to_all | solution.py:321
  1.8 0.0 copy-start.1
  1.8 0.0 copy-start.2
  1.8 0.0 copy-start.3
  1.8 0.0 copy-start.4
  1.8 7.4 %all-to-all-start = ((bf16[128,8,128]{2,0,1:T(8,128)(2,1)}), bf16[128,8,128]{2,0,1:T(8,128)(2,1)S(1)}, u32[]{:S(2)}, u32[]{:S(2)}) async-start(bf16[128,8,128]{2,0,1:T(8,128)(2,1)} %copy.8), calls=%async_computation | async-start | bytes 524288 | tf_op jit(solution)/shard_map/all_to_all | solution.py:321
  9.2 0.0 copy-done.5
  9.2 0.0 copy-done.1
  9.2 0.0 copy-done.2
  9.2 0.0 copy-done.3
  9.2 0.0 copy-done.4
  9.2 5.2 %tables.1 = (f32[1024,128]{1,0:T(8,128)S(1)}, f32[1024,128]{1,0:T(8,128)S(1)}, f32[96,128]{1,0:T(8,128)S(1)}) custom-call(f32[8,128]{1,0:T(8,128)S(1)} %bitcast.15, f32[32,1024]{1,0:T(8,128)S(1)} %copy-done.1, f32[32,1024]{1,0:T(8,128)S(1)} %copy-done.2, f32[32,1024]{1,0:T(8,128)S(1)} %copy-done.3, f32[32,1024]{1,0:T(8,128)S(1)} %copy-done.4), custom_call_target="tpu_custom_call" | custom-call | flops 20000000 | bytes 2000000 | tf_op jit(solution)/shard_map/tables/pallas_call | solution.py:323
  14.4 3.7 %all-to-all-done = bf16[128,8,128]{2,0,1:T(8,128)(2,1)S(1)} async-done(((bf16[128,8,128]{2,0,1:T(8,128)(2,1)}), bf16[128,8,128]{2,0,1:T(8,128)(2,1)S(1)}, u32[]{:S(2)}, u32[]{:S(2)}) %all-to-all-start) | async-done | bytes 262176 | tf_op jit(solution)/shard_map/all_to_all | solution.py:321
  18.1 3.0 %states.1 = f32[8,64,128]{2,1,0:T(8,128)} custom-call(bf16[1024,128]{1,0:T(8,128)(2,1)S(1)} %bitcast.14, f32[96,128]{1,0:T(8,128)S(1)} %get-tuple-element.11.mid_ref), custom_call_target="tpu_custom_call" | custom-call | flops 16000000 | bytes 1000000 | tf_op jit(solution)/shard_map/states/pallas_call | solution.py:345
  21.0 0.0 copy-start
  21.0 0.0 copy-start.6
  21.0 3.7 %all-to-all-start.1 = ((f32[8,64,128]{2,1,0:T(8,128)}), f32[8,64,128]{2,1,0:T(8,128)S(1)}, u32[]{:S(2)}, u32[]{:S(2)}) async-start(f32[8,64,128]{2,1,0:T(8,128)} %states.1), calls=%async_computation.1 | async-start | bytes 524288 | tf_op jit(solution)/shard_map/all_to_all | solution.py:358
  24.8 0.0 copy-done
  24.8 0.0 copy-done.6
  24.8 3.1 %conv.1.local_ref = f32[1024,128]{1,0:T(8,128)S(1)} custom-call(bf16[128,1024]{1,0:T(8,128)(2,1)S(1)} %bitcast.12, f32[1024,128]{1,0:T(8,128)S(1)} %get-tuple-element.12.taps_ref, f32[8,128]{1,0:T(8,128)S(1)} %bitcast.16), custom_call_target="tpu_custom_call" | custom-call | flops 18000000 | bytes 2000000 | tf_op jit(solution)/shard_map/conv/pallas_call | solution.py:363
  27.9 5.5 %all-to-all-done.1 = f32[8,64,128]{2,1,0:T(8,128)S(1)} async-done(((f32[8,64,128]{2,1,0:T(8,128)}), f32[8,64,128]{2,1,0:T(8,128)S(1)}, u32[]{:S(2)}, u32[]{:S(2)}) %all-to-all-start.1) | async-done | bytes 262176 | tf_op jit(solution)/shard_map/all_to_all | solution.py:358
  33.3 5.5 %final.1 = f32[128,1024]{1,0:T(8,128)} custom-call(f32[1024,128]{1,0:T(8,128)S(1)} %conv.1.local_ref, f32[1024,128]{1,0:T(8,128)S(1)} %get-tuple-element.13.seed_ref, f32[512,128]{1,0:T(8,128)S(1)} %bitcast.13), custom_call_target="tpu_custom_call" | custom-call | flops 20000000 | bytes 2000000 | tf_op jit(solution)/shard_map/final/pallas_call | solution.py:372
Async XLA Ops:
  1.0 8.2 %copy-start.5 = (f32[1024]{0:T(1024)S(1)}, f32[1024]{0:T(1024)}, u32[]{:S(2)}) copy-start(f32[1024]{0:T(1024)} %param.8) | copy-start | bytes 12292
  1.8 7.4 %copy-start.1 = (f32[32,1024]{1,0:T(8,128)S(1)}, f32[32,1024]{1,0:T(8,128)}, u32[]{:S(2)}) copy-start(f32[32,1024]{1,0:T(8,128)} %decay_ref.1) | copy-start | bytes 393220
  1.8 7.4 %copy-start.2 = (f32[32,1024]{1,0:T(8,128)S(1)}, f32[32,1024]{1,0:T(8,128)}, u32[]{:S(2)}) copy-start(f32[32,1024]{1,0:T(8,128)} %freq_ref.1) | copy-start | bytes 393220
  1.8 7.4 %copy-start.3 = (f32[32,1024]{1,0:T(8,128)S(1)}, f32[32,1024]{1,0:T(8,128)}, u32[]{:S(2)}) copy-start(f32[32,1024]{1,0:T(8,128)} %real_ref.1) | copy-start | bytes 393220
  1.8 7.4 %copy-start.4 = (f32[32,1024]{1,0:T(8,128)S(1)}, f32[32,1024]{1,0:T(8,128)}, u32[]{:S(2)}) copy-start(f32[32,1024]{1,0:T(8,128)} %imag_ref.1) | copy-start | bytes 393220
  1.8 16.3 %all-to-all-start = ((bf16[128,8,128]{2,0,1:T(8,128)(2,1)}), bf16[128,8,128]{2,0,1:T(8,128)(2,1)S(1)}, u32[]{:S(2)}, u32[]{:S(2)}) async-start(bf16[128,8,128]{2,0,1:T(8,128)(2,1)} %copy.8), calls=%async_computation | async-start | bytes 524288 | tf_op jit(solution)/shard_map/all_to_all | solution.py:321
  21.0 3.7 %copy-start = (bf16[1,128,1024]{2,1,0:T(8,128)(2,1)S(1)}, bf16[1,128,1024]{2,1,0:T(8,128)(2,1)}, u32[]{:S(2)}) copy-start(bf16[1,128,1024]{2,1,0:T(8,128)(2,1)} %param.7) | copy-start | bytes 786436
  21.0 3.7 %copy-start.6 = (f32[1024]{0:T(1024)S(1)}, f32[1024]{0:T(1024)}, u32[]{:S(2)}) copy-start(f32[1024]{0:T(1024)} %param.13) | copy-start | bytes 12292
  21.0 12.3 %all-to-all-start.1 = ((f32[8,64,128]{2,1,0:T(8,128)}), f32[8,64,128]{2,1,0:T(8,128)S(1)}, u32[]{:S(2)}, u32[]{:S(2)}) async-start(f32[8,64,128]{2,1,0:T(8,128)} %states.1), calls=%async_computation.1 | async-start | bytes 524288 | tf_op jit(solution)/shard_map/all_to_all | solution.py:358

commit v2 on v1

v2 whole, which is shorter than its diff:
```python
import functools

import jax
import jax.numpy as jnp
from jax import lax
from jax.experimental import pallas as pl
from jax.experimental.pallas import tpu as pltpu
from jax.sharding import PartitionSpec as P

LANES = 128
NEAR = 16
FINAL_NEAR = 8
SEQ_AXES = ("seqin", "seqout")


def cmul(a, b):
    return (a[0] * b[0] - a[1] * b[1], a[0] * b[1] + a[1] * b[0])


def cos_sin(angle):
    turns = jnp.floor(angle * 0.6366197723675814 + 0.5)
    rest = angle - turns * 1.5703125
    rest = rest - turns * 4.837512969970703125e-4
    rest = rest - turns * 7.549789948768648e-8
    square = rest * rest
    sine = rest + rest * square * (
        -1.6666654611e-1 + square * (8.3321608736e-3 - square * 1.9515295891e-4)
    )
    cosine = (
        1.0
        - 0.5 * square
        + square * square * (4.166664568298827e-2 + square * (-1.388731625493765e-3 + square * 2.443315711809948e-5))
    )
    quarter = turns.astype(jnp.int32) & 3
    swap = (quarter & 1) == 1
    first = jnp.where(swap, sine, cosine)
    second = jnp.where(swap, cosine, sine)
    return (
        jnp.where((quarter == 1) | (quarter == 2), -first, first),
        jnp.where(quarter >= 2, -second, second),
    )


def decay_step(time_step, decay_rate, frequency):
    fade_rate = time_step * decay_rate
    shrink = jnp.exp(-fade_rate)
    cosine, sine = cos_sin(time_step * frequency)
    return (fade_rate, (shrink * cosine, shrink * sine))


def gain_of(fade_rate):
    double = 2.0 * fade_rate
    series = 1.0 / 40320.0
    for factor in (5040.0, 720.0, 120.0, 24.0, 6.0, 2.0, 1.0):
        series = 1.0 / factor - double * series
    small = double * series
    return jnp.sqrt(jnp.where(double < 0.25, small, 1.0 - jnp.exp(-double)))


def power_list(lam, count):
    powers = [None, lam]
    for k in range(2, count + 1):
        powers.append(cmul(powers[k // 2], powers[k - k // 2]))
    return powers


def spread_rows(source_ref, target_ref, rows, groups, stack):
    for start in range(0, rows, stack):
        for k in range(groups):
            part = source_ref[start : start + stack, k * LANES : (k + 1) * LANES]
            target_ref[pl.ds(start * groups + k, stack, stride=groups), :] = part.astype(jnp.float32)


def row_at(ref, index, groups):
    return ref[pl.ds(pl.multiple_of(index * groups, groups), groups), :]


def put_row(ref, index, groups, value):
    ref[pl.ds(pl.multiple_of(index * groups, groups), groups), :] = value


def power_sum(near_ref, lead_of, states, groups, near, count, init):

    def turn(n, acc):
        leads = lead_of(n)
        acc = list(acc)
        for a in range(count):
            acc[a * near] = acc[a * near] + leads[a][0]
        for u in range(1, near):
            real = row_at(near_ref, n * (2 * near) + 2 * u, groups)
            imag = row_at(near_ref, n * (2 * near) + 2 * u + 1, groups)
            for a in range(count):
                slot = a * near + u
                acc[slot] = acc[slot] + (leads[a][0] * real - leads[a][1] * imag)
        return tuple(acc)

    return lax.fori_loop(0, states, turn, tuple(init), unroll=16)


def split_kernel(signal_ref, out_ref, sems):
    parts, _, width = out_ref.shape
    copies = [
        pltpu.make_async_copy(signal_ref.at[:, pl.ds(k * width, width)], out_ref.at[k], sems.at[k])
        for k in range(parts)
    ]
    for copy in copies:
        copy.start()
    for copy in copies:
        copy.wait()


def tables_kernel(
    width, step_hbm, decay_hbm, freq_hbm, real_hbm, imag_hbm,
    pack_ref, mid_ref,
    step_ref, decay_ref, freq_ref, real_ref, imag_ref,
    decay_sp, freq_sp, real_sp, imag_sp, near_ref, lead_ref, sems,
):
    pairs = (
        (step_hbm, step_ref), (decay_hbm, decay_ref), (freq_hbm, freq_ref), (real_hbm, real_ref), (imag_hbm, imag_ref),
    )
    copies = [pltpu.make_async_copy(pair[0], pair[1], sems.at[i]) for i, pair in enumerate(pairs)]
    for copy in copies:
        copy.start()
    for copy in copies:
        copy.wait()
    states = decay_ref.shape[0]
    groups = decay_ref.shape[1] // LANES
    tokens = pack_ref.shape[0] // groups - 4 * states
    outer = tokens // NEAR
    taps_ref = pack_ref.at[0 : tokens * groups]
    seed_ref = pack_ref.at[tokens * groups : (tokens + 4 * states) * groups]
    if width == LANES:
        place = lax.axis_index("seqin") * lax.axis_size("seqout") + lax.axis_index("seqout")
        own = pl.ds(pl.multiple_of(place * LANES, LANES), LANES)
        fade, lam = decay_step(step_ref[pl.ds(place, 1), :], decay_ref[:, own], freq_ref[:, own])
        mid_ref[0:states, :] = lam[0]
        mid_ref[states : 2 * states, :] = lam[1]
        mid_ref[2 * states : 3 * states, :] = gain_of(fade)
    for source, target in ((decay_ref, decay_sp), (freq_ref, freq_sp), (real_ref, real_sp), (imag_ref, imag_sp)):
        spread_rows(source, target, states, groups, 8)
    step = step_ref[...]

    def prepare(n, carry):
        fade, lam = decay_step(step, row_at(decay_sp, n, groups), row_at(freq_sp, n, groups))
        powers = power_list(lam, NEAR)
        for u in range(1, NEAR):
            for part in range(2):
                put_row(near_ref, n * (2 * NEAR) + 2 * u + part, groups, powers[u][part])
        weight = (2.0 * row_at(real_sp, n, groups), 2.0 * row_at(imag_sp, n, groups))
        gain = gain_of(fade)
        lead = (weight[0] * gain, weight[1] * gain)
        for part in range(2):
            put_row(seed_ref, 4 * n + part, groups, lam[part])
            put_row(seed_ref, 4 * n + 2 + part, groups, weight[part])
        for a in range(outer):
            if a:
                lead = cmul(lead, powers[NEAR])
            for part in range(2):
                put_row(lead_ref, n * (2 * outer) + 2 * a + part, groups, lead[part])
        return carry

    lax.fori_loop(0, states, prepare, 0)
    zero = jnp.zeros((groups, LANES), jnp.float32)

    count = min(2, outer)
    for first in range(0, outer, count):

        def lead_of(n, first=first):
            return [
                tuple(row_at(lead_ref, n * (2 * outer) + 2 * (first + a) + part, groups) for part in range(2))
                for a in range(count)
            ]

        acc = power_sum(near_ref, lead_of, states, groups, NEAR, count, [zero] * (count * NEAR))
        for t in range(count * NEAR):
            row = (first * NEAR + t) * groups
            taps_ref[row : row + groups, :] = acc[t]


def split_pack(pack_ref, tokens, states, groups):
    first = tokens * groups
    second = first + states * 2 * FINAL_NEAR * groups
    return (pack_ref.at[0:first], pack_ref.at[first:second], pack_ref.at[second : second + 2 * states * groups])


def conv_kernel(
    signal_hbm, skip_hbm, given_ref, pack_ref, signal_ref, skip_ref, signal_sp, taps_pad, sems
):
    copies = [
        pltpu.make_async_copy(pair[0], pair[1], sems.at[i])
        for i, pair in enumerate(((signal_hbm, signal_ref), (skip_hbm, skip_ref)))
    ]
    for copy in copies:
        copy.start()
    tokens, channels = signal_ref.shape
    groups = channels // LANES
    states = (given_ref.shape[0] // groups - tokens) // 4
    taps_ref = given_ref.at[0 : tokens * groups]
    seed_ref = given_ref.at[tokens * groups : (tokens + 4 * states) * groups]
    out_ref, near_ref, lead_ref = split_pack(pack_ref, tokens, states, groups)
    tile = 8

    def prepare(n, carry):
        lam, weight = (tuple(row_at(seed_ref, 4 * n + 2 * i + part, groups) for part in range(2)) for i in range(2))
        powers = power_list(lam, FINAL_NEAR)
        powers[0] = powers[FINAL_NEAR]
        lead = cmul(weight, lam)
        for part in range(2):
            put_row(lead_ref, 2 * n + part, groups, lead[part])
            for u in range(FINAL_NEAR):
                put_row(near_ref, n * (2 * FINAL_NEAR) + 2 * u + part, groups, powers[u][part])
        return carry

    lax.fori_loop(0, states, prepare, 0)
    for copy in copies:
        copy.wait()
    spread_rows(signal_ref, signal_sp, tokens, groups, 16)
    taps_pad[0 : tile * groups, :] = jnp.zeros((tile * groups, LANES), jnp.float32)
    taps_pad[tile * groups : (tile + tokens) * groups, :] = taps_ref[...]
    skip = skip_ref[...]

    def row_tile(ti, carry):
        def col_tile(ji, acc):
            gap = (ti - ji) * tile + 1
            window = [row_at(taps_pad, gap + m, groups) for m in range(2 * tile - 1)]
            acc = list(acc)
            for j in range(tile):
                drive = row_at(signal_sp, ji * tile + j, groups)
                for t in range(tile):
                    acc[t] = acc[t] + window[t - j + tile - 1] * drive
            return tuple(acc)

        init = tuple(skip * row_at(signal_sp, ti * tile + t, groups) for t in range(tile))
        acc = lax.fori_loop(0, ti + 1, col_tile, init)
        for t in range(tile):
            put_row(out_ref, ti * tile + t, groups, acc[t])
        return carry

    lax.fori_loop(0, tokens // tile, row_tile, 0)


def states_kernel(n_in, n_out, tokens, signal_ref, mid_ref, out_ref, signal_f, near_ref, out_buf, sems):
    states = mid_ref.shape[0] // 3
    width = mid_ref.shape[1]
    parts = n_in * n_out
    a_tile = 4
    signal_f[...] = signal_ref[...].astype(jnp.float32)
    lam = (mid_ref[0:states, :], mid_ref[states : 2 * states, :])
    gain = mid_ref[2 * states : 3 * states, :]
    powers = power_list(lam, NEAR)
    for u in range(1, NEAR):
        for part in range(2):
            near_ref[2 * u + part] = powers[u][part]
    hops = [None, powers[NEAR]]
    for a in range(2, a_tile + 1):
        hops.append(cmul(hops[a // 2], hops[a - a // 2]))

    def advance(base, state):
        real = [None] * a_tile
        imag = [None] * a_tile
        for u in range(NEAR):
            drive = [
                jnp.broadcast_to(signal_f[pl.ds(base + a * NEAR + u, 1), :], (states, width))
                for a in range(a_tile)
            ]
            power = NEAR - 1 - u
            if power:
                near_real, near_imag = near_ref[2 * power], near_ref[2 * power + 1]
            for a in range(a_tile):
                if power:
                    add_real, add_imag = near_real * drive[a], near_imag * drive[a]
                    real[a] = add_real if real[a] is None else real[a] + add_real
                    imag[a] = add_imag if imag[a] is None else imag[a] + add_imag
                else:
                    real[a] = real[a] + drive[a]
        total = (real[a_tile - 1], imag[a_tile - 1])
        for a in range(a_tile - 1):
            moved = cmul(hops[a_tile - 1 - a], (real[a], imag[a]))
            total = (total[0] + moved[0], total[1] + moved[1])
        moved = cmul(hops[a_tile], state)
        return (moved[0] + total[0], moved[1] + total[1])

    def place_of(s):
        return lax.rem(s, n_in) * n_out + s // n_in

    def copy_of(s):
        place = place_of(s)
        return pltpu.make_async_copy(out_buf.at[s], out_ref.at[place], sems.at[s])

    def send(s, state):
        out_buf[s, 0:states, :] = gain * state[0]
        out_buf[s, states : 2 * states, :] = gain * state[1]
        copy_of(s).start()

    zero = jnp.zeros((states, width), jnp.float32)
    send(0, (zero, zero))

    def part_turn(s, state):
        for i in range(tokens // (NEAR * a_tile)):
            base = pl.multiple_of(place_of(s - 1) * tokens + i * (a_tile * NEAR), a_tile * NEAR)
            state = advance(base, state)
        send(s, state)
        return state

    lax.fori_loop(1, parts, part_turn, (zero, zero), unroll=min(7, parts - 1))

    def finish(s, carry):
        copy_of(s).wait()
        return carry

    lax.fori_loop(0, parts, finish, 0)


def final_kernel(pack_ref, state_ref, out_ref, state_sp, rows_ref, out_buf, sems):
    tokens, channels = out_ref.shape
    groups = channels // LANES
    near = FINAL_NEAR
    outer = tokens // near
    states = state_ref.shape[0] // (2 * groups)
    local_ref, near_ref, lead_ref = split_pack(pack_ref, tokens, states, groups)

    def pair_at(ref, index):
        return tuple(row_at(ref, index + part, groups) for part in range(2))

    for n in range(states):
        entering = tuple(state_ref[pl.ds(n + part * states, groups, stride=2 * states), :] for part in range(2))
        lead = cmul(pair_at(lead_ref, 2 * n), entering)
        for part in range(2):
            put_row(state_sp, 2 * n + part, groups, lead[part])

    count = min(4, outer)
    span = count * near
    copies = []
    for index in range(outer // count):
        last = index + 1 == outer // count

        def lead_of(n, last=last):
            hop = pair_at(near_ref, n * (2 * near))
            leads = [pair_at(state_sp, 2 * n)]
            for _ in range(count - 1 if last else count):
                leads.append(cmul(leads[-1], hop))
            if not last:
                for part in range(2):
                    put_row(state_sp, 2 * n + part, groups, leads[count][part])
            return leads

        start = index * span
        init = [local_ref[(start + t) * groups : (start + t + 1) * groups, :] for t in range(span)]
        acc = power_sum(near_ref, lead_of, states, groups, near, count, init)
        for t in range(span):
            rows_ref[t * groups : (t + 1) * groups, :] = acc[t]
        for t in range(0, span, 8):
            for k in range(groups):
                out_buf[start + t : start + t + 8, k * LANES : (k + 1) * LANES] = rows_ref[
                    pl.ds(t * groups + k, 8, stride=groups), :
                ]
        copy = pltpu.make_async_copy(
            out_buf.at[pl.ds(start, span)], out_ref.at[pl.ds(start, span)], sems.at[index]
        )
        copy.start()
        copies.append(copy)
    for copy in copies:
        copy.wait()


def per_device(n_in, n_out, inputs, time_step, decay_rate, frequency, output_real, output_imag, skip_gain):
    signal = inputs[0]
    tokens, channels = signal.shape
    states = decay_rate.shape[0]
    groups = channels // LANES
    parts = n_in * n_out
    width = channels // parts
    outer = tokens // NEAR
    f32 = jnp.float32

    def hbm(array):
        return pltpu.with_memory_space_constraint(array, pltpu.HBM)

    def params(mebibytes):
        return pltpu.CompilerParams(vmem_limit_bytes=mebibytes * 1024 * 1024)

    def rows(count, dtype=f32):
        return pltpu.VMEM((count * groups, LANES), dtype)

    def shape(*dims):
        return jax.ShapeDtypeStruct(dims, f32)

    if width == LANES:
        tiled = pl.pallas_call(
            split_kernel,
            out_shape=pltpu.VMEM((parts, tokens, width), signal.dtype),
            in_specs=[pl.BlockSpec(memory_space=pl.ANY)],
            out_specs=pl.BlockSpec(memory_space=pltpu.VMEM),
            scratch_shapes=[pltpu.SemaphoreType.DMA((parts,))],
            compiler_params=params(2),
            name="split",
        )(hbm(signal))
    else:
        tiled = signal.reshape(tokens, parts, width).transpose(1, 0, 2)
    whole = lax.all_to_all(tiled, SEQ_AXES, split_axis=0, concat_axis=0, tiled=True)
    whole = whole.reshape(parts * tokens, width)

    given, mid = pl.pallas_call(
        functools.partial(tables_kernel, width),
        out_shape=(
            shape((tokens + states * 4) * groups, LANES),
            shape(3 * states, LANES),
        ),
        in_specs=[pl.BlockSpec(memory_space=pl.ANY)] * 5,
        scratch_shapes=[
            rows(1),
            *[pltpu.VMEM((states, channels), f32)] * 4,
            *[rows(states)] * 4,
            rows(states * 2 * NEAR),
            rows(states * 2 * outer),
            pltpu.SemaphoreType.DMA((5,)),
        ],
        compiler_params=params(40),
        cost_estimate=pl.CostEstimate(flops=20_000_000, bytes_accessed=2_000_000, transcendentals=40_000),
        name="tables",
    )(*(hbm(array) for array in (time_step.reshape(groups, LANES), decay_rate, frequency, output_real, output_imag)))

    if width != LANES:
        place = lax.axis_index("seqin") * n_out + lax.axis_index("seqout")

        def own(array):
            return lax.dynamic_slice_in_dim(array, place * width, width, array.ndim - 1)

        fade, lam = decay_step(own(time_step)[None, :], own(decay_rate), own(frequency))
        mid = jnp.concatenate([lam[0], lam[1], gain_of(fade)], axis=0)

    entering = pl.pallas_call(
        functools.partial(states_kernel, n_in, n_out, tokens),
        out_shape=shape(parts, 2 * states, width),
        out_specs=pl.BlockSpec(memory_space=pl.ANY),
        scratch_shapes=[
            pltpu.VMEM((parts * tokens, width), f32),
            pltpu.VMEM((2 * NEAR, states, width), f32),
            pltpu.VMEM((parts, 2 * states, width), f32),
            pltpu.SemaphoreType.DMA((parts,)),
        ],
        compiler_params=params(40),
        cost_estimate=pl.CostEstimate(flops=16_000_000, bytes_accessed=1_000_000, transcendentals=0),
        name="states",
    )(whole, mid)

    given, entering = lax.optimization_barrier((given, entering))
    entering = lax.all_to_all(entering, SEQ_AXES, split_axis=0, concat_axis=0, tiled=True)
    if width != LANES:
        entering = entering.transpose(1, 0, 2).reshape(2 * states, groups, LANES).transpose(1, 0, 2)
    entering = entering.reshape(groups * 2 * states, LANES)

    pack = pl.pallas_call(
        conv_kernel,
        out_shape=shape((tokens + states * 2 * FINAL_NEAR + states * 2) * groups, LANES),
        in_specs=[
            pl.BlockSpec(memory_space=pl.ANY),
            pl.BlockSpec(memory_space=pl.ANY),
            pl.BlockSpec(memory_space=pltpu.VMEM),
        ],
        scratch_shapes=[
            pltpu.VMEM((tokens, channels), signal.dtype),
            rows(1),
            rows(tokens),
            rows(tokens + 8),
            pltpu.SemaphoreType.DMA((2,)),
        ],
        compiler_params=params(40),
        cost_estimate=pl.CostEstimate(flops=18_000_000, bytes_accessed=2_000_000, transcendentals=0),
        name="conv",
    )(hbm(signal), hbm(skip_gain.reshape(groups, LANES)), given)

    count = min(4, tokens // FINAL_NEAR)
    outputs = pl.pallas_call(
        final_kernel,
        out_shape=shape(tokens, channels),
        out_specs=pl.BlockSpec(memory_space=pl.ANY),
        scratch_shapes=[
            rows(2 * states),
            rows(count * FINAL_NEAR),
            pltpu.VMEM((tokens, channels), f32),
            pltpu.SemaphoreType.DMA((tokens // FINAL_NEAR // count,)),
        ],
        compiler_params=params(40),
        cost_estimate=pl.CostEstimate(flops=20_000_000, bytes_accessed=2_000_000, transcendentals=0),
        name="final",
    )(pack, entering)
    return outputs[None]


def solution(mesh):
    in_specs = (
        P(("groups", "seqout"), "seqin", "chan"),
        P("chan"),
        P(None, "chan"),
        P(None, "chan"),
        P(None, "chan"),
        P(None, "chan"),
        P("chan"),
    )
    out_specs = P(("groups", "seqout"), "seqin", "chan")
    return jax.shard_map(
        functools.partial(per_device, mesh.shape["seqin"], mesh.shape["seqout"]),
        mesh=mesh,
        in_specs=in_specs,
        out_specs=out_specs,
        check_vma=False,
    )
```

time: 39.2 us -> 36.6 us (0.934)
  waiting for transfers between devices: 9.13 us -> 6.11 us
  local copies, waits for them, and re-layouts: 1.77 us -> 2.19 us
    all_to_all x1, waiting for transfers between devices: 5.47 us -> 3.3 us  [per_device(): lax.all_to_all(entering, SEQ_AXES, split_axis=0, concat_axis=0, tiled=True)]
    unnamed x15 -> x4, local copies, waits for them, and re-layouts: 1.02 us -> 2.19 us
    all_to_all x1, waiting for transfers between devices: 3.66 us -> 2.81 us  [per_device(): lax.all_to_all(tiled, SEQ_AXES, split_axis=0, concat_axis=0, tiled=True)]
    all_to_all x1 -> x0, local copies, waits for them, and re-layouts: 0.75 us -> none  [per_device(): lax.all_to_all(signal, SEQ_AXES, split_axis=1, concat_axis=0, tiled=True)]
    pallas_call x2 -> x3, Pallas kernels: 8.58 us -> 9.07 us  [the longest x1 4.03 us: per_device(): pl.pallas_call(conv_kernel, out_shape=shape((tokens + states * 2 * FINAL_...]
  transfers between devices with their start and end apart: 2 -> 2, of which waited for: 2 -> 2; matrix products, arithmetic and copies ran while one was open for 0% -> 0% of each run, Pallas kernels for 21% -> 25%
where the time goes in v2:
time: 36.6 us; the launch traced here: 36.2 us
  Pallas kernels  17 us (46%)
  starting transfers between devices  10.9 us (30%)
  waiting for transfers between devices  6.11 us (17%)
  local copies, waits for them, and re-layouts  2.19 us (6%)
    all_to_all x1, starting transfers between devices, per_device(): lax.all_to_all(tiled, SEQ_AXES, split_axis=0, concat_axis=0, tiled=True)  7.26 us
    pallas_call x1, Pallas kernels, per_device(): pl.pallas_call(functools.partial(tables_kernel, width), out_shape=(shape(...  5.13 us
    pallas_call x1, Pallas kernels, per_device(): pl.pallas_call(conv_kernel, out_shape=shape((tokens + states * 2 * FINAL_...  4.03 us
    all_to_all x1, starting transfers between devices, per_device(): lax.all_to_all(entering, SEQ_AXES, split_axis=0, concat_axis=0, tiled=True)  3.6 us
    pallas_call x1, Pallas kernels, per_device(): pl.pallas_call(final_kernel, out_shape=shape(tokens, channels), out_specs...  3.39 us
    all_to_all x1, waiting for transfers between devices, per_device(): lax.all_to_all(entering, SEQ_AXES, split_axis=0, concat_axis=0, tiled=True)  3.3 us
    all_to_all x1, waiting for transfers between devices, per_device(): lax.all_to_all(tiled, SEQ_AXES, split_axis=0, concat_axis=0, tiled=True)  2.81 us
    pallas_call x1, Pallas kernels, per_device(): pl.pallas_call(functools.partial(states_kernel, n_in, n_out, tokens), out...  2.76 us
  transfers between devices with their start and end apart: 2, of which 2 were waited for; matrix products, arithmetic and copies ran while one was open for 0% of the time, Pallas kernels for 25%

profile of v2, /device:TPU:0, one launch (start us, length us, event | category | flops | bytes accessed | tf_op | source)
XLA Modules:
  0.0 36.2 jit_solution(14271026002361671196)
XLA Ops:
  0.0 1.6 %split.1 = bf16[8,128,128]{2,1,0:T(8,128)(2,1)} custom-call(bf16[128,1024]{1,0:T(8,128)(2,1)} %bitcast.8), custom_call_target="tpu_custom_call" | custom-call | tf_op jit(solution)/shard_map/split/pallas_call | solution.py:389
  1.7 7.3 %all-to-all-start = ((bf16[8,128,128]{2,1,0:T(8,128)(2,1)}), bf16[8,128,128]{2,1,0:T(8,128)(2,1)S(1)}, u32[]{:S(2)}, u32[]{:S(2)}) async-start(bf16[8,128,128]{2,1,0:T(8,128)(2,1)} %split.1), calls=%async_computation | async-start | bytes 524288 | tf_op jit(solution)/shard_map/all_to_all | solution.py:400
  8.9 5.1 %tables.1 = (f32[2048,128]{1,0:T(8,128)S(1)}, f32[96,128]{1,0:T(8,128)S(1)}) custom-call(f32[8,128]{1,0:T(8,128)} %bitcast.10, f32[32,1024]{1,0:T(8,128)} %decay_hbm.1, f32[32,1024]{1,0:T(8,128)} %freq_hbm.1, f32[32,1024]{1,0:T(8,128)} %real_hbm.1, f32[32,1024]{1,0:T(8,128)} %imag_hbm.1), custom_call_target="tpu_custom_call" | custom-call | flops 20000000 | bytes 2000000 | tf_op jit(solution)/shard_map/tables/pallas_call | solution.py:403
  14.1 0.0 copy-start
  14.1 1.0 %copy-done = f32[2048,128]{1,0:T(8,128)} copy-done((f32[2048,128]{1,0:T(8,128)}, f32[2048,128]{1,0:T(8,128)S(1)}, u32[]{:S(2)}) %copy-start) | copy-done | bytes 1048600
  15.0 2.8 %all-to-all-done = bf16[8,128,128]{2,1,0:T(8,128)(2,1)S(1)} async-done(((bf16[8,128,128]{2,1,0:T(8,128)(2,1)}), bf16[8,128,128]{2,1,0:T(8,128)(2,1)S(1)}, u32[]{:S(2)}, u32[]{:S(2)}) %all-to-all-start) | async-done | bytes 262176 | tf_op jit(solution)/shard_map/all_to_all | solution.py:400
  17.8 2.8 %states.1 = f32[8,64,128]{2,1,0:T(8,128)} custom-call(bf16[1024,128]{1,0:T(8,128)(2,1)S(1)} %bitcast.7, f32[96,128]{1,0:T(8,128)S(1)} %get-tuple-element.10.mid_ref), custom_call_target="tpu_custom_call" | custom-call | flops 16000000 | bytes 1000000 | tf_op jit(solution)/shard_map/states/pallas_call | solution.py:432
  20.6 3.6 %all-to-all-start.1 = ((f32[8,64,128]{2,1,0:T(8,128)}), f32[8,64,128]{2,1,0:T(8,128)S(1)}, u32[]{:S(2)}, u32[]{:S(2)}) async-start(f32[8,64,128]{2,1,0:T(8,128)} %states.1), calls=%async_computation.1 | async-start | bytes 524288 | tf_op jit(solution)/shard_map/all_to_all | solution.py:448
  24.2 0.0 copy-start.1
  24.2 1.2 %copy-done.1 = f32[2048,128]{1,0:T(8,128)S(1)} copy-done((f32[2048,128]{1,0:T(8,128)S(1)}, f32[2048,128]{1,0:T(8,128)}, u32[]{:S(2)}) %copy-start.1) | copy-done | bytes 1048600
  25.4 4.0 %conv.1.pack_ref = f32[5632,128]{1,0:T(8,128)S(1)} custom-call(bf16[128,1024]{1,0:T(8,128)(2,1)} %bitcast.9, f32[8,128]{1,0:T(8,128)} %bitcast.11, f32[2048,128]{1,0:T(8,128)S(1)} %copy-done.1), custom_call_target="tpu_custom_call" | custom-call | flops 18000000 | bytes 2000000 | tf_op jit(solution)/shard_map/conv/pallas_call | solution.py:453
  29.5 3.3 %all-to-all-done.1 = f32[8,64,128]{2,1,0:T(8,128)S(1)} async-done(((f32[8,64,128]{2,1,0:T(8,128)}), f32[8,64,128]{2,1,0:T(8,128)S(1)}, u32[]{:S(2)}, u32[]{:S(2)}) %all-to-all-start.1) | async-done | bytes 262176 | tf_op jit(solution)/shard_map/all_to_all | solution.py:448
  32.8 3.4 %final.1 = f32[128,1024]{1,0:T(8,128)} custom-call(f32[5632,128]{1,0:T(8,128)S(1)} %conv.1.pack_ref, f32[512,128]{1,0:T(8,128)S(1)} %bitcast.6), custom_call_target="tpu_custom_call" | custom-call | flops 20000000 | bytes 2000000 | tf_op jit(solution)/shard_map/final/pallas_call | solution.py:474
Async XLA Ops:
  1.7 16.2 %all-to-all-start = ((bf16[8,128,128]{2,1,0:T(8,128)(2,1)}), bf16[8,128,128]{2,1,0:T(8,128)(2,1)S(1)}, u32[]{:S(2)}, u32[]{:S(2)}) async-start(bf16[8,128,128]{2,1,0:T(8,128)(2,1)} %split.1), calls=%async_computation | async-start | bytes 524288 | tf_op jit(solution)/shard_map/all_to_all | solution.py:400
  14.1 1.0 %copy-start = (f32[2048,128]{1,0:T(8,128)}, f32[2048,128]{1,0:T(8,128)S(1)}, u32[]{:S(2)}) copy-start(f32[2048,128]{1,0:T(8,128)S(1)} %get-tuple-element.11.given_ref) | copy-start | bytes 3145732
  20.6 12.2 %all-to-all-start.1 = ((f32[8,64,128]{2,1,0:T(8,128)}), f32[8,64,128]{2,1,0:T(8,128)S(1)}, u32[]{:S(2)}, u32[]{:S(2)}) async-start(f32[8,64,128]{2,1,0:T(8,128)} %states.1), calls=%async_computation.1 | async-start | bytes 524288 | tf_op jit(solution)/shard_map/all_to_all | solution.py:448
  24.2 1.2 %copy-start.1 = (f32[2048,128]{1,0:T(8,128)S(1)}, f32[2048,128]{1,0:T(8,128)}, u32[]{:S(2)}) copy-start(f32[2048,128]{1,0:T(8,128)} %copy-done) | copy-start | bytes 3145732

commit v3 on v2

--- a/solution.py
+++ b/solution.py
@@ -10,6 +10,9 @@
 LANES = 128
 NEAR = 16
 FINAL_NEAR = 8
+HALF_RANGE = 125.0
+LOG_TWO = 0.6931471805599453
+SCALE_ROWS = 8
 SEQ_AXES = ("seqin", "seqout")
 
 
@@ -97,22 +100,26 @@
     return lax.fori_loop(0, states, turn, tuple(init), unroll=16)
 
 
-def split_kernel(signal_ref, out_ref, sems):
+def split_kernel(signal_ref, out_ref, buf, in_sems, out_sems):
     parts, _, width = out_ref.shape
-    copies = [
-        pltpu.make_async_copy(signal_ref.at[:, pl.ds(k * width, width)], out_ref.at[k], sems.at[k])
-        for k in range(parts)
-    ]
-    for copy in copies:
-        copy.start()
-    for copy in copies:
-        copy.wait()
+    loads, stores = [], []
+    for k in range(parts):
+        load = pltpu.make_async_copy(signal_ref.at[:, pl.ds(k * width, width)], buf.at[k], in_sems.at[k])
+        load.start()
+        loads.append(load)
+    for k in range(parts):
+        loads[k].wait()
+        store = pltpu.make_async_copy(buf.at[k], out_ref.at[k], out_sems.at[k])
+        store.start()
+        stores.append(store)
+    for store in stores:
+        store.wait()
 
 
 def tables_kernel(
     width, step_hbm, decay_hbm, freq_hbm, real_hbm, imag_hbm,
-    pack_ref, mid_ref,
-    step_ref, decay_ref, freq_ref, real_ref, imag_ref,
+    taps_hbm, seed_hbm, mid_ref,
+    taps_ref, seed_ref, step_ref, decay_ref, freq_ref, real_ref, imag_ref,
     decay_sp, freq_sp, real_sp, imag_sp, near_ref, lead_ref, sems,
 ):
     pairs = (
@@ -125,10 +132,8 @@
         copy.wait()
     states = decay_ref.shape[0]
     groups = decay_ref.shape[1] // LANES
-    tokens = pack_ref.shape[0] // groups - 4 * states
+    tokens = taps_ref.shape[0] // groups
     outer = tokens // NEAR
-    taps_ref = pack_ref.at[0 : tokens * groups]
-    seed_ref = pack_ref.at[tokens * groups : (tokens + 4 * states) * groups]
     if width == LANES:
         place = lax.axis_index("seqin") * lax.axis_size("seqout") + lax.axis_index("seqout")
         own = pl.ds(pl.multiple_of(place * LANES, LANES), LANES)
@@ -160,6 +165,8 @@
         return carry
 
     lax.fori_loop(0, states, prepare, 0)
+    copies = [pltpu.make_async_copy(seed_ref, seed_hbm, sems.at[0])]
+    copies[0].start()
     zero = jnp.zeros((groups, LANES), jnp.float32)
 
     count = min(2, outer)
@@ -175,6 +182,11 @@
         for t in range(count * NEAR):
             row = (first * NEAR + t) * groups
             taps_ref[row : row + groups, :] = acc[t]
+        part = pl.ds(first * NEAR * groups, count * NEAR * groups)
+        copies.append(pltpu.make_async_copy(taps_ref.at[part], taps_hbm.at[part], sems.at[len(copies)]))
+        copies[-1].start()
+    for copy in copies:
+        copy.wait()
 
 
 def split_pack(pack_ref, tokens, states, groups):
@@ -184,21 +196,26 @@
 
 
 def conv_kernel(
-    signal_hbm, skip_hbm, given_ref, pack_ref, signal_ref, skip_ref, signal_sp, taps_pad, sems
+    signal_hbm, skip_hbm, taps_hbm, seed_hbm, pack_ref, signal_ref, skip_ref, seed_ref, signal_sp, taps_pad, sems
 ):
+    tokens, channels = signal_ref.shape
+    groups = channels // LANES
+    states = seed_ref.shape[0] // (4 * groups)
+    tile = 8
     copies = [
         pltpu.make_async_copy(pair[0], pair[1], sems.at[i])
-        for i, pair in enumerate(((signal_hbm, signal_ref), (skip_hbm, skip_ref)))
+        for i, pair in enumerate((
+            (seed_hbm, seed_ref),
+            (signal_hbm, signal_ref),
+            (skip_hbm, skip_ref),
+            (taps_hbm, taps_pad.at[tile * groups : (tile + tokens) * groups]),
+        ))
     ]
     for copy in copies:
         copy.start()
-    tokens, channels = signal_ref.shape
-    groups = channels // LANES
-    states = (given_ref.shape[0] // groups - tokens) // 4
-    taps_ref = given_ref.at[0 : tokens * groups]
-    seed_ref = given_ref.at[tokens * groups : (tokens + 4 * states) * groups]
     out_ref, near_ref, lead_ref = split_pack(pack_ref, tokens, states, groups)
-    tile = 8
+    taps_pad[0 : tile * groups, :] = jnp.zeros((tile * groups, LANES), jnp.float32)
+    copies[0].wait()
 
     def prepare(n, carry):
         lam, weight = (tuple(row_at(seed_ref, 4 * n + 2 * i + part, groups) for part in range(2)) for i in range(2))
@@ -212,31 +229,36 @@
         return carry
 
     lax.fori_loop(0, states, prepare, 0)
-    for copy in copies:
+    for copy in copies[1:]:
         copy.wait()
     spread_rows(signal_ref, signal_sp, tokens, groups, 16)
-    taps_pad[0 : tile * groups, :] = jnp.zeros((tile * groups, LANES), jnp.float32)
-    taps_pad[tile * groups : (tile + tokens) * groups, :] = taps_ref[...]
     skip = skip_ref[...]
 
-    def row_tile(ti, carry):
-        def col_tile(ji, acc):
-            gap = (ti - ji) * tile + 1
-            window = [row_at(taps_pad, gap + m, groups) for m in range(2 * tile - 1)]
-            acc = list(acc)
-            for j in range(tile):
-                drive = row_at(signal_sp, ji * tile + j, groups)
-                for t in range(tile):
-                    acc[t] = acc[t] + window[t - j + tile - 1] * drive
-            return tuple(acc)
-
+    def col_tile(ji, acc, ti):
+        gap = (ti - ji) * tile + 1
+        window = [row_at(taps_pad, gap + m, groups) for m in range(2 * tile - 1)]
+        acc = list(acc)
+        for j in range(tile):
+            drive = row_at(signal_sp, ji * tile + j, groups)
+            for t in range(tile):
+                acc[t] = acc[t] + window[t - j + tile - 1] * drive
+        return tuple(acc)
+
+    for ti in range(tokens // tile):
         init = tuple(skip * row_at(signal_sp, ti * tile + t, groups) for t in range(tile))
-        acc = lax.fori_loop(0, ti + 1, col_tile, init)
+        acc = lax.fori_loop(0, ti + 1, functools.partial(col_tile, ti=ti), init, unroll=4)
         for t in range(tile):
             put_row(out_ref, ti * tile + t, groups, acc[t])
-        return carry
-
-    lax.fori_loop(0, tokens // tile, row_tile, 0)
+
+
+def encode(value, inverse):
+    code = jnp.exp2(jnp.abs(value) * inverse * (2.0 * HALF_RANGE) - HALF_RANGE)
+    return jnp.where(value < 0.0, -code, code).astype(jnp.bfloat16)
+
+
+def decode(code, scale):
+    size = (jnp.log(jnp.abs(code)) * (0.5 / HALF_RANGE / LOG_TWO) + 0.5) * scale
+    return jnp.where(code < 0.0, -size, size)
 
 
 def states_kernel(n_in, n_out, tokens, signal_ref, mid_ref, out_ref, signal_f, near_ref, out_buf, sems):
@@ -244,7 +266,6 @@
     width = mid_ref.shape[1]
     parts = n_in * n_out
     a_tile = 4
-    signal_f[...] = signal_ref[...].astype(jnp.float32)
     lam = (mid_ref[0:states, :], mid_ref[states : 2 * states, :])
     gain = mid_ref[2 * states : 3 * states, :]
     powers = power_list(lam, NEAR)
@@ -281,6 +302,8 @@
         return (moved[0] + total[0], moved[1] + total[1])
 
     def place_of(s):
+        if isinstance(s, int):
+            return s % n_in * n_out + s // n_in
         return lax.rem(s, n_in) * n_out + s // n_in
 
     def copy_of(s):
@@ -288,21 +311,40 @@
         return pltpu.make_async_copy(out_buf.at[s], out_ref.at[place], sems.at[s])
 
     def send(s, state):
-        out_buf[s, 0:states, :] = gain * state[0]
-        out_buf[s, states : 2 * states, :] = gain * state[1]
+        entering = (gain * state[0], gain * state[1])
+        top = jnp.max(jnp.maximum(jnp.abs(entering[0]), jnp.abs(entering[1])), axis=0, keepdims=True)
+        scale = (1.01 * top).astype(jnp.bfloat16)
+        wide = scale.astype(jnp.float32)
+        inverse = jnp.where(wide > 1e-36, 1.0 / jnp.maximum(wide, 1e-36), 0.0)
+        for part in range(2):
+            out_buf[s, part * states : (part + 1) * states, :] = encode(entering[part], inverse)
+        out_buf[s, 2 * states :, :] = jnp.broadcast_to(wide, (SCALE_ROWS, width)).astype(jnp.bfloat16)
         copy_of(s).start()
 
     zero = jnp.zeros((states, width), jnp.float32)
-    send(0, (zero, zero))
+    out_buf[0, 0 : 2 * states, :] = jnp.ones((2 * states, width), jnp.bfloat16)
+    out_buf[0, 2 * states :, :] = jnp.zeros((SCALE_ROWS, width), jnp.bfloat16)
+    copy_of(0).start()
 
     def part_turn(s, state):
+        start = place_of(s - 1) * tokens
+        if not isinstance(s, int):
+            start = pl.multiple_of(start, tokens)
+        signal_f[pl.ds(start, tokens), :] = signal_ref[pl.ds(start, tokens), :].astype(jnp.float32)
         for i in range(tokens // (NEAR * a_tile)):
-            base = pl.multiple_of(place_of(s - 1) * tokens + i * (a_tile * NEAR), a_tile * NEAR)
-            state = advance(base, state)
+            state = advance(start + i * (a_tile * NEAR), state)
         send(s, state)
         return state
 
-    lax.fori_loop(1, parts, part_turn, (zero, zero), unroll=min(7, parts - 1))
+    if parts <= 8:
+        state = (zero, zero)
+        for s in range(1, parts):
+            state = part_turn(s, state)
+        for s in range(parts):
+            copy_of(s).wait()
+        return
+
+    lax.fori_loop(1, parts, part_turn, (zero, zero))
 
     def finish(s, carry):
         copy_of(s).wait()
@@ -311,17 +353,22 @@
     lax.fori_loop(0, parts, finish, 0)
 
 
-def final_kernel(pack_ref, state_ref, out_ref, state_sp, rows_ref, out_buf, sems):
+def final_kernel(states, pack_ref, code_ref, out_ref, state_ref, state_sp, rows_ref, out_buf, sems):
     tokens, channels = out_ref.shape
     groups = channels // LANES
     near = FINAL_NEAR
     outer = tokens // near
-    states = state_ref.shape[0] // (2 * groups)
     local_ref, near_ref, lead_ref = split_pack(pack_ref, tokens, states, groups)
 
     def pair_at(ref, index):
         return tuple(row_at(ref, index + part, groups) for part in range(2))
 
+    stride = 2 * states + SCALE_ROWS
+    for k in range(groups):
+        code = code_ref[k * stride : (k + 1) * stride, :].astype(jnp.float32)
+        state_ref[k * 2 * states : (k + 1) * 2 * states, :] = decode(
+            code[0 : 2 * states, :], code[2 * states : 2 * states + 1, :]
+        )
     for n in range(states):
         entering = tuple(state_ref[pl.ds(n + part * states, groups, stride=2 * states), :] for part in range(2))
         lead = cmul(pair_at(lead_ref, 2 * n), entering)
@@ -372,6 +419,7 @@
     width = channels // parts
     outer = tokens // NEAR
     f32 = jnp.float32
+    code_rows = 2 * states + SCALE_ROWS
 
     def hbm(array):
         return pltpu.with_memory_space_constraint(array, pltpu.HBM)
@@ -388,10 +436,14 @@
     if width == LANES:
         tiled = pl.pallas_call(
             split_kernel,
-            out_shape=pltpu.VMEM((parts, tokens, width), signal.dtype),
+            out_shape=jax.ShapeDtypeStruct((parts, tokens, width), signal.dtype),
             in_specs=[pl.BlockSpec(memory_space=pl.ANY)],
-            out_specs=pl.BlockSpec(memory_space=pltpu.VMEM),
-            scratch_shapes=[pltpu.SemaphoreType.DMA((parts,))],
+            out_specs=pl.BlockSpec(memory_space=pl.ANY),
+            scratch_shapes=[
+                pltpu.VMEM((parts, tokens, width), signal.dtype),
+                pltpu.SemaphoreType.DMA((parts,)),
+                pltpu.SemaphoreType.DMA((parts,)),
+            ],
             compiler_params=params(2),
             name="split",
         )(hbm(signal))
@@ -400,20 +452,28 @@
     whole = lax.all_to_all(tiled, SEQ_AXES, split_axis=0, concat_axis=0, tiled=True)
     whole = whole.reshape(parts * tokens, width)
 
-    given, mid = pl.pallas_call(
+    taps, seeds, mid = pl.pallas_call(
         functools.partial(tables_kernel, width),
         out_shape=(
-            shape((tokens + states * 4) * groups, LANES),
+            pltpu.HBM((tokens * groups, LANES), f32),
+            pltpu.HBM((states * 4 * groups, LANES), f32),
             shape(3 * states, LANES),
+        ),
+        out_specs=(
+            pl.BlockSpec(memory_space=pltpu.HBM),
+            pl.BlockSpec(memory_space=pltpu.HBM),
+            pl.BlockSpec(memory_space=pltpu.VMEM),
         ),
         in_specs=[pl.BlockSpec(memory_space=pl.ANY)] * 5,
         scratch_shapes=[
+            rows(tokens),
+            rows(states * 4),
             rows(1),
             *[pltpu.VMEM((states, channels), f32)] * 4,
             *[rows(states)] * 4,
             rows(states * 2 * NEAR),
             rows(states * 2 * outer),
-            pltpu.SemaphoreType.DMA((5,)),
+            pltpu.SemaphoreType.DMA((max(5, 1 + outer // min(2, outer)),)),
         ],
         compiler_params=params(40),
         cost_estimate=pl.CostEstimate(flops=20_000_000, bytes_accessed=2_000_000, transcendentals=40_000),
@@ -431,12 +491,12 @@
 
     entering = pl.pallas_call(
         functools.partial(states_kernel, n_in, n_out, tokens),
-        out_shape=shape(parts, 2 * states, width),
+        out_shape=jax.ShapeDtypeStruct((parts, code_rows, width), jnp.bfloat16),
         out_specs=pl.BlockSpec(memory_space=pl.ANY),
         scratch_shapes=[
             pltpu.VMEM((parts * tokens, width), f32),
             pltpu.VMEM((2 * NEAR, states, width), f32),
-            pltpu.VMEM((parts, 2 * states, width), f32),
+            pltpu.VMEM((parts, code_rows, width), jnp.bfloat16),
             pltpu.SemaphoreType.DMA((parts,)),
         ],
         compiler_params=params(40),
@@ -444,38 +504,36 @@
         name="states",
     )(whole, mid)
 
-    given, entering = lax.optimization_barrier((given, entering))
+    taps, entering = lax.optimization_barrier((taps, entering))
     entering = lax.all_to_all(entering, SEQ_AXES, split_axis=0, concat_axis=0, tiled=True)
     if width != LANES:
-        entering = entering.transpose(1, 0, 2).reshape(2 * states, groups, LANES).transpose(1, 0, 2)
-    entering = entering.reshape(groups * 2 * states, LANES)
+        entering = entering.transpose(1, 0, 2).reshape(code_rows, groups, LANES).transpose(1, 0, 2)
+    entering = entering.reshape(groups * code_rows, LANES)
 
     pack = pl.pallas_call(
         conv_kernel,
         out_shape=shape((tokens + states * 2 * FINAL_NEAR + states * 2) * groups, LANES),
-        in_specs=[
-            pl.BlockSpec(memory_space=pl.ANY),
-            pl.BlockSpec(memory_space=pl.ANY),
-            pl.BlockSpec(memory_space=pltpu.VMEM),
-        ],
+        in_specs=[pl.BlockSpec(memory_space=pl.ANY)] * 4,
         scratch_shapes=[
             pltpu.VMEM((tokens, channels), signal.dtype),
             rows(1),
+            rows(states * 4),
             rows(tokens),
             rows(tokens + 8),
-            pltpu.SemaphoreType.DMA((2,)),
+            pltpu.SemaphoreType.DMA((4,)),
         ],
         compiler_params=params(40),
         cost_estimate=pl.CostEstimate(flops=18_000_000, bytes_accessed=2_000_000, transcendentals=0),
         name="conv",
-    )(hbm(signal), hbm(skip_gain.reshape(groups, LANES)), given)
+    )(hbm(signal), hbm(skip_gain.reshape(groups, LANES)), hbm(taps), hbm(seeds))
 
     count = min(4, tokens // FINAL_NEAR)
     outputs = pl.pallas_call(
-        final_kernel,
+        functools.partial(final_kernel, states),
         out_shape=shape(tokens, channels),
         out_specs=pl.BlockSpec(memory_space=pl.ANY),
         scratch_shapes=[
+            rows(2 * states),
             rows(2 * states),
             rows(count * FINAL_NEAR),
             pltpu.VMEM((tokens, channels), f32),

time: 36.6 us -> 35.7 us (0.975)
  local copies, waits for them, and re-layouts: 2.19 us -> 0 us
  Pallas kernels: 17 us -> 17.8 us
  waiting for transfers between devices: 6.11 us -> 6.51 us
    unnamed x4 -> x0, local copies, waits for them, and re-layouts: 2.19 us -> none
    pallas_call x3, Pallas kernels: 10.2 us -> 10.9 us  [the longest x1 5.78 us: per_device(): pl.pallas_call(functools.partial(tables_kernel, width), out_shape=(pltpu....]
  transfers between devices with their start and end apart: 2 -> 2, of which waited for: 2 -> 2; matrix products, arithmetic and copies ran while one was open for 0% -> 0% of each run, Pallas kernels for 25% -> 28%
where the time goes in v3:
time: 35.7 us; the launch traced here: 35.2 us
  Pallas kernels  17.8 us (50%)
  starting transfers between devices  10.9 us (31%)
  waiting for transfers between devices  6.51 us (18%)
    all_to_all x1, starting transfers between devices, per_device(): lax.all_to_all(tiled, SEQ_AXES, split_axis=0, concat_axis=0, tiled=True)  7.26 us
    pallas_call x1, Pallas kernels, per_device(): pl.pallas_call(functools.partial(tables_kernel, width), out_shape=(pltpu....  5.78 us
    pallas_call x1, Pallas kernels, per_device(): pl.pallas_call(conv_kernel, out_shape=shape((tokens + states * 2 * FINAL_...  4.07 us
    all_to_all x1, starting transfers between devices, per_device(): lax.all_to_all(entering, SEQ_AXES, split_axis=0, concat_axis=0, tiled=True)  3.6 us
    pallas_call x1, Pallas kernels, per_device(): pl.pallas_call(functools.partial(final_kernel, states), out_shape=shape(t...  3.48 us
    all_to_all x1, waiting for transfers between devices, per_device(): lax.all_to_all(entering, SEQ_AXES, split_axis=0, concat_axis=0, tiled=True)  3.38 us
    all_to_all x1, waiting for transfers between devices, per_device(): lax.all_to_all(tiled, SEQ_AXES, split_axis=0, concat_axis=0, tiled=True)  3.13 us
    pallas_call x1, Pallas kernels, per_device(): pl.pallas_call(functools.partial(states_kernel, n_in, n_out, tokens), out...  2.87 us
  transfers between devices with their start and end apart: 2, of which 2 were waited for; matrix products, arithmetic and copies ran while one was open for 0% of the time, Pallas kernels for 28%

profile of v3, /device:TPU:0, one launch (start us, length us, event | category | flops | bytes accessed | tf_op | source)
XLA Modules:
  0.0 35.2 jit_solution(9674895302231147645)
XLA Ops:
  0.0 1.6 %split.1 = bf16[8,128,128]{2,1,0:T(8,128)(2,1)} custom-call(bf16[128,1024]{1,0:T(8,128)(2,1)} %bitcast.8), custom_call_target="tpu_custom_call" | custom-call | tf_op jit(solution)/shard_map/split/pallas_call | solution.py:437
  1.6 7.3 %all-to-all-start = ((bf16[8,128,128]{2,1,0:T(8,128)(2,1)}), bf16[8,128,128]{2,1,0:T(8,128)(2,1)S(1)}, u32[]{:S(2)}, u32[]{:S(2)}) async-start(bf16[8,128,128]{2,1,0:T(8,128)(2,1)} %split.1), calls=%async_computation | async-start | bytes 524288 | tf_op jit(solution)/shard_map/all_to_all | solution.py:452
  8.9 5.8 %tables.1 = (f32[1024,128]{1,0:T(8,128)}, f32[1024,128]{1,0:T(8,128)}, f32[96,128]{1,0:T(8,128)S(1)}) custom-call(f32[8,128]{1,0:T(8,128)} %bitcast.10, f32[32,1024]{1,0:T(8,128)} %decay_hbm.1, f32[32,1024]{1,0:T(8,128)} %freq_hbm.1, f32[32,1024]{1,0:T(8,128)} %real_hbm.1, f32[32,1024]{1,0:T(8,128)} %imag_hbm.1), custom_call_target="tpu_custom_call" | custom-call | flops 20000000 | bytes 2000000 | tf_op jit(solution)/shard_map/tables/pallas_call | solution.py:455
  14.7 3.1 %all-to-all-done = bf16[8,128,128]{2,1,0:T(8,128)(2,1)S(1)} async-done(((bf16[8,128,128]{2,1,0:T(8,128)(2,1)}), bf16[8,128,128]{2,1,0:T(8,128)(2,1)S(1)}, u32[]{:S(2)}, u32[]{:S(2)}) %all-to-all-start) | async-done | bytes 262176 | tf_op jit(solution)/shard_map/all_to_all | solution.py:452
  17.8 2.9 %states.1 = bf16[8,72,128]{2,1,0:T(8,128)(2,1)} custom-call(bf16[1024,128]{1,0:T(8,128)(2,1)S(1)} %bitcast.6, f32[96,128]{1,0:T(8,128)S(1)} %get-tuple-element.11.mid_ref), custom_call_target="tpu_custom_call" | custom-call | flops 16000000 | bytes 1000000 | tf_op jit(solution)/shard_map/states/pallas_call | solution.py:492
  20.7 3.6 %all-to-all-start.1 = ((bf16[8,72,128]{2,1,0:T(8,128)(2,1)}), bf16[8,72,128]{2,1,0:T(8,128)(2,1)S(1)}, u32[]{:S(2)}, u32[]{:S(2)}) async-start(bf16[8,72,128]{2,1,0:T(8,128)(2,1)} %states.1), calls=%async_computation.1 | async-start | bytes 294912 | tf_op jit(solution)/shard_map/all_to_all | solution.py:508
  24.3 4.1 %conv.1.pack_ref = f32[5632,128]{1,0:T(8,128)S(1)} custom-call(bf16[128,1024]{1,0:T(8,128)(2,1)} %bitcast.9, f32[8,128]{1,0:T(8,128)} %bitcast.11, f32[1024,128]{1,0:T(8,128)} %get-tuple-element.12.taps_hbm, f32[1024,128]{1,0:T(8,128)} %get-tuple-element.13.seed_hbm), custom_call_target="tpu_custom_call" | custom-call | flops 18000000 | bytes 2000000 | tf_op jit(solution)/shard_map/conv/pallas_call | solution.py:513
  28.4 3.4 %all-to-all-done.1 = bf16[8,72,128]{2,1,0:T(8,128)(2,1)S(1)} async-done(((bf16[8,72,128]{2,1,0:T(8,128)(2,1)}), bf16[8,72,128]{2,1,0:T(8,128)(2,1)S(1)}, u32[]{:S(2)}, u32[]{:S(2)}) %all-to-all-start.1) | async-done | bytes 147488 | tf_op jit(solution)/shard_map/all_to_all | solution.py:508
  31.8 3.5 %final.1 = f32[128,1024]{1,0:T(8,128)} custom-call(f32[5632,128]{1,0:T(8,128)S(1)} %conv.1.pack_ref, bf16[576,128]{1,0:T(8,128)(2,1)S(1)} %bitcast.7), custom_call_target="tpu_custom_call" | custom-call | flops 20000000 | bytes 2000000 | tf_op jit(solution)/shard_map/final/pallas_call | solution.py:531
Async XLA Ops:
  1.6 16.2 %all-to-all-start = ((bf16[8,128,128]{2,1,0:T(8,128)(2,1)}), bf16[8,128,128]{2,1,0:T(8,128)(2,1)S(1)}, u32[]{:S(2)}, u32[]{:S(2)}) async-start(bf16[8,128,128]{2,1,0:T(8,128)(2,1)} %split.1), calls=%async_computation | async-start | bytes 524288 | tf_op jit(solution)/shard_map/all_to_all | solution.py:452
  20.7 11.1 %all-to-all-start.1 = ((bf16[8,72,128]{2,1,0:T(8,128)(2,1)}), bf16[8,72,128]{2,1,0:T(8,128)(2,1)S(1)}, u32[]{:S(2)}, u32[]{:S(2)}) async-start(bf16[8,72,128]{2,1,0:T(8,128)(2,1)} %states.1), calls=%async_computation.1 | async-start | bytes 294912 | tf_op jit(solution)/shard_map/all_to_all | solution.py:508

commit v4 on v3

v4 whole, which is shorter than its diff:
```python
import functools

import jax
import jax.numpy as jnp
from jax import lax
from jax.experimental import pallas as pl
from jax.experimental.pallas import tpu as pltpu
from jax.sharding import PartitionSpec as P

LANES = 128
NEAR = 16
FINAL_NEAR = 8
HALF_RANGE = 125.0
LOG_TWO = 0.6931471805599453


def cmul(a, b):
    return (a[0] * b[0] - a[1] * b[1], a[0] * b[1] + a[1] * b[0])


def cos_sin(angle):
    turns = jnp.floor(angle * 0.6366197723675814 + 0.5)
    rest = angle - turns * 1.5703125
    rest = rest - turns * 4.837512969970703125e-4
    rest = rest - turns * 7.549789948768648e-8
    square = rest * rest
    sine = rest + rest * square * (
        -1.6666654611e-1 + square * (8.3321608736e-3 - square * 1.9515295891e-4)
    )
    cosine = (
        1.0
        - 0.5 * square
        + square * square * (4.166664568298827e-2 + square * (-1.388731625493765e-3 + square * 2.443315711809948e-5))
    )
    quarter = turns.astype(jnp.int32) & 3
    swap = (quarter & 1) == 1
    first = jnp.where(swap, sine, cosine)
    second = jnp.where(swap, cosine, sine)
    return (
        jnp.where((quarter == 1) | (quarter == 2), -first, first),
        jnp.where(quarter >= 2, -second, second),
    )


def decay_step(time_step, decay_rate, frequency):
    fade_rate = time_step * decay_rate
    shrink = jnp.exp(-fade_rate)
    cosine, sine = cos_sin(time_step * frequency)
    return (fade_rate, (shrink * cosine, shrink * sine))


def gain_of(fade_rate):
    double = 2.0 * fade_rate
    series = 1.0 / 40320.0
    for factor in (5040.0, 720.0, 120.0, 24.0, 6.0, 2.0, 1.0):
        series = 1.0 / factor - double * series
    small = double * series
    return jnp.sqrt(jnp.where(double < 0.25, small, 1.0 - jnp.exp(-double)))


def power_list(lam, count):
    powers = [None, lam]
    for k in range(2, count + 1):
        powers.append(cmul(powers[k // 2], powers[k - k // 2]))
    return powers


def spread_rows(source_ref, target_ref, rows, groups, stack):
    for start in range(0, rows, stack):
        for k in range(groups):
            part = source_ref[start : start + stack, k * LANES : (k + 1) * LANES]
            target_ref[pl.ds(start * groups + k, stack, stride=groups), :] = part.astype(jnp.float32)


def row_at(ref, index, groups):
    return ref[pl.ds(pl.multiple_of(index * groups, groups), groups), :]


def put_row(ref, index, groups, value):
    ref[pl.ds(pl.multiple_of(index * groups, groups), groups), :] = value


def power_sum(near_ref, lead_of, states, groups, near, count, init):

    def turn(n, acc):
        leads = lead_of(n)
        acc = list(acc)
        for a in range(count):
            acc[a * near] = acc[a * near] + leads[a][0]
        for u in range(1, near):
            real = row_at(near_ref, n * (2 * near) + 2 * u, groups)
            imag = row_at(near_ref, n * (2 * near) + 2 * u + 1, groups)
            for a in range(count):
                slot = a * near + u
                acc[slot] = acc[slot] + (leads[a][0] * real - leads[a][1] * imag)
        return tuple(acc)

    return lax.fori_loop(0, states, turn, tuple(init), unroll=16)


def power_of(base, exponent):
    result = None
    while exponent:
        if exponent & 1:
            result = base if result is None else cmul(result, base)
        exponent //= 2
        if exponent:
            base = cmul(base, base)
    return result


def start_copies(pairs, sems):
    copies = [pltpu.make_async_copy(pair[0], pair[1], sems.at[i]) for i, pair in enumerate(pairs)]
    for copy in copies:
        copy.start()
    return copies


def pair_at(ref, index, groups):
    return tuple(row_at(ref, index + part, groups) for part in range(2))


def put_pair(ref, index, groups, value):
    for part in range(2):
        put_row(ref, index + part, groups, value[part])


def decayed_sum(signal_sp, powers, tokens, groups):
    a_tile = min(4, tokens // NEAR)
    total = None
    for first in range(0, tokens // NEAR, a_tile):
        real, imag = [None] * a_tile, [None] * a_tile
        for u in range(NEAR):
            power = NEAR - 1 - u
            for a in range(a_tile):
                row = ((first + a) * NEAR + u) * groups
                drive = signal_sp[row : row + groups, :]
                if power:
                    add_real, add_imag = powers[power][0] * drive, powers[power][1] * drive
                    real[a] = add_real if real[a] is None else real[a] + add_real
                    imag[a] = add_imag if imag[a] is None else imag[a] + add_imag
                else:
                    real[a] = real[a] + drive
        for a in range(a_tile):
            if total is None:
                total = (real[a], imag[a])
            else:
                moved = cmul(powers[NEAR], total)
                total = (moved[0] + real[a], moved[1] + imag[a])
    return total


def sums_kernel(
    signal_hbm, step_hbm, decay_hbm, freq_hbm, real_hbm, imag_hbm,
    seed_hbm, base_ref,
    signal_ref, step_ref, decay_ref, freq_ref, real_ref, imag_ref,
    signal_sp, decay_sp, freq_sp, real_sp, imag_sp, seed_ref, sems,
):
    copies = start_copies(
        (
            (step_hbm, step_ref), (decay_hbm, decay_ref), (freq_hbm, freq_ref),
            (signal_hbm, signal_ref), (real_hbm, real_ref), (imag_hbm, imag_ref),
        ),
        sems,
    )
    states, channels = decay_ref.shape
    groups = channels // LANES
    tokens = signal_ref.shape[0]
    for copy in copies:
        copy.wait()
    for source, target in ((decay_ref, decay_sp), (freq_ref, freq_sp), (real_ref, real_sp), (imag_ref, imag_sp)):
        spread_rows(source, target, states, groups, 8)
    spread_rows(signal_ref, signal_sp, tokens, groups, 16)
    step = step_ref[...]

    def prepare(n, carry):
        fade, lam = decay_step(step, row_at(decay_sp, n, groups), row_at(freq_sp, n, groups))
        gain = gain_of(fade)
        weight = (2.0 * row_at(real_sp, n, groups), 2.0 * row_at(imag_sp, n, groups))
        put_pair(seed_ref, 6 * n, groups, lam)
        put_pair(seed_ref, 6 * n + 2, groups, weight)
        put_pair(seed_ref, 6 * n + 4, groups, (weight[0] * gain, weight[1] * gain))
        own = decayed_sum(signal_sp, power_list(lam, NEAR), tokens, groups)
        put_pair(base_ref, 5 * n, groups, lam)
        put_pair(base_ref, 5 * n + 2, groups, (gain * own[0], gain * own[1]))
        put_row(base_ref, 5 * n + 4, groups, gain)
        return carry

    lax.fori_loop(0, states, prepare, 0, unroll=2)
    copy = pltpu.make_async_copy(seed_ref, seed_hbm, sems.at[0])
    copy.start()
    copy.wait()


def largest(value, most):
    return jnp.maximum(most, jnp.maximum(jnp.abs(value[0]), jnp.abs(value[1])))


def messages_kernel(n_in, n_early, base_ref, *refs):
    early_refs, out_refs, own_hbm = refs[:n_early], refs[n_early : n_early + n_in - 1], refs[n_early + n_in - 1]
    signal_sp, sums_ref, own_ref, code_ref, sems = refs[n_early + n_in :]
    tokens, channels = early_refs[0].shape
    groups = channels // LANES
    states = base_ref.shape[0] // (5 * groups)
    for j in range(n_early):
        spread_rows(early_refs[j], signal_sp.at[j], tokens, groups, 16)

    def gather(n, most):
        lam, own = pair_at(base_ref, 5 * n, groups), pair_at(base_ref, 5 * n + 2, groups)
        gain = row_at(base_ref, 5 * n + 4, groups)
        powers = power_list(lam, NEAR)
        block = power_of(powers[NEAR], tokens // NEAR * n_in)
        early = None
        for j in reversed(range(n_early)):
            part = decayed_sum(signal_sp.at[j], powers, tokens, groups)
            part = (gain * part[0], gain * part[1])
            if early is not None:
                moved = cmul(block, early)
                part = (part[0] + moved[0], part[1] + moved[1])
            early = part
        moved = cmul(block, early)
        later = (own[0] + moved[0], own[1] + moved[1])
        put_pair(sums_ref, 4 * n, groups, later)
        put_pair(sums_ref, 4 * n + 2, groups, early)
        put_pair(own_ref, 2 * n, groups, early)
        return (largest(later, most[0]), largest(early, most[1]))

    zero = jnp.zeros((groups, LANES), jnp.float32)
    most = lax.fori_loop(0, states, gather, (zero, zero), unroll=2)
    own_copy = pltpu.make_async_copy(own_ref, own_hbm, sems.at[0])
    own_copy.start()
    inverse = []
    for kind in range(2):
        scale = (1.01 * most[kind]).astype(jnp.bfloat16).astype(jnp.float32)
        inverse.append(jnp.where(scale > 1e-36, 1.0 / jnp.maximum(scale, 1e-36), 0.0))
        pair = jnp.concatenate([scale, scale], axis=0).astype(jnp.bfloat16)
        code_ref[kind, states * 2 * groups :, :] = pair

    def write(n, carry):
        for kind in range(2):
            value = pair_at(sums_ref, 4 * n + 2 * kind, groups)
            code = jnp.concatenate([encode(value[part], inverse[kind]) for part in range(2)], axis=0)
            row = pl.multiple_of(n * (2 * groups), 2 * groups)
            code_ref[kind, pl.ds(row, 2 * groups), :] = code.astype(jnp.bfloat16)
        return carry

    lax.fori_loop(0, states, write, 0, unroll=4)
    place = lax.axis_index("seqin")
    copies = [own_copy]
    for d in range(1, n_in):
        kind = (place + d) // n_in
        copies.append(pltpu.make_async_copy(code_ref.at[kind], out_refs[d - 1], sems.at[d]))
        copies[-1].start()
    for copy in copies:
        copy.wait()


def split_pack(pack_ref, tokens, states, groups):
    refs, start = [], 0
    for count in (tokens, states * 2 * FINAL_NEAR, 2 * states, 2 * states, 2 * states):
        refs.append(pack_ref.at[start * groups : (start + count) * groups])
        start += count
    return refs


def conv_kernel(
    signal_hbm, skip_hbm, seed_hbm, own_hbm, pack_ref,
    signal_ref, skip_ref, seed_ref, near_ref, lead_ref, signal_sp, taps_pad, sems,
):
    tokens, channels = signal_ref.shape
    groups = channels // LANES
    states = seed_ref.shape[0] // (6 * groups)
    outer = tokens // NEAR
    tile = 8
    out_ref, few_ref, shift_ref, hop_ref, own_ref = split_pack(pack_ref, tokens, states, groups)
    copies = start_copies(
        ((seed_hbm, seed_ref), (signal_hbm, signal_ref), (skip_hbm, skip_ref), (own_hbm, own_ref)), sems
    )
    taps_pad[0 : tile * groups, :] = jnp.zeros((tile * groups, LANES), jnp.float32)
    copies[0].wait()

    def prepare(n, carry):
        lam, weight, lead = (pair_at(seed_ref, 6 * n + 2 * i, groups) for i in range(3))
        powers = power_list(lam, NEAR)
        for u in range(1, NEAR):
            put_pair(near_ref, n * (2 * NEAR) + 2 * u, groups, powers[u])
        for u in range(FINAL_NEAR):
            put_pair(few_ref, n * (2 * FINAL_NEAR) + 2 * u, groups, powers[u if u else FINAL_NEAR])
        put_pair(shift_ref, 2 * n, groups, cmul(weight, lam))
        put_pair(hop_ref, 2 * n, groups, power_of(powers[NEAR], outer))
        for a in range(outer):
            if a:
                lead = cmul(lead, powers[NEAR])
            put_pair(lead_ref, n * (2 * outer) + 2 * a, groups, lead)
        return carry

    lax.fori_loop(0, states, prepare, 0, unroll=2)
    for copy in copies[1:]:
        copy.wait()
    spread_rows(signal_ref, signal_sp, tokens, groups, 16)
    zero = jnp.zeros((groups, LANES), jnp.float32)
    count = min(2, outer)
    for first in range(0, outer, count):

        def lead_of(n, first=first):
            return [pair_at(lead_ref, n * (2 * outer) + 2 * (first + a), groups) for a in range(count)]

        acc = power_sum(near_ref, lead_of, states, groups, NEAR, count, [zero] * (count * NEAR))
        for t in range(count * NEAR):
            put_row(taps_pad, tile + first * NEAR + t, groups, acc[t])

    skip = skip_ref[...]

    def col_tile(ji, acc, ti):
        gap = (ti - ji) * tile + 1
        window = [row_at(taps_pad, gap + m, groups) for m in range(2 * tile - 1)]
        acc = list(acc)
        for j in range(tile):
            drive = row_at(signal_sp, ji * tile + j, groups)
            for t in range(tile):
                acc[t] = acc[t] + window[t - j + tile - 1] * drive
        return tuple(acc)

    for ti in range(tokens // tile):
        init = tuple(skip * row_at(signal_sp, ti * tile + t, groups) for t in range(tile))
        acc = lax.fori_loop(0, ti + 1, functools.partial(col_tile, ti=ti), init, unroll=4)
        for t in range(tile):
            put_row(out_ref, ti * tile + t, groups, acc[t])


def encode(value, inverse):
    code = jnp.exp2(jnp.abs(value) * inverse * (2.0 * HALF_RANGE) - HALF_RANGE)
    return jnp.where(value < 0.0, -code, code)


def decode(code, scale):
    size = (jnp.log(jnp.abs(code)) * (0.5 / HALF_RANGE / LOG_TWO) + 0.5) * scale
    return jnp.where(code < 0.0, -size, size)


def final_kernel(states, pack_ref, *refs):
    message_refs, out_ref = refs[:-5], refs[-5]
    state_sp, rows_ref, out_buf, sems = refs[-4:]
    tokens, channels = out_ref.shape
    groups = channels // LANES
    near = FINAL_NEAR
    outer = tokens // near
    local_ref, near_ref, shift_ref, hop_ref, own_ref = split_pack(pack_ref, tokens, states, groups)
    scales = [ref[states * 2 * groups :, :].astype(jnp.float32)[0:groups, :] for ref in message_refs]

    def enter(n, carry):
        hop = pair_at(hop_ref, 2 * n, groups)
        state = pair_at(own_ref, 2 * n, groups)
        row = pl.multiple_of(n * (2 * groups), 2 * groups)
        for ref, scale in zip(reversed(message_refs), reversed(scales)):
            code = ref[pl.ds(row, 2 * groups), :].astype(jnp.float32)
            moved = cmul(hop, state)
            state = tuple(
                moved[part] + decode(code[part * groups : (part + 1) * groups, :], scale) for part in range(2)
            )
        put_pair(state_sp, 2 * n, groups, cmul(pair_at(shift_ref, 2 * n, groups), state))
        return carry

    lax.fori_loop(0, states, enter, 0, unroll=4)
    count = min(4, outer)
    span = count * near
    copies = []
    for index in range(outer // count):
        last = index + 1 == outer // count

        def lead_of(n, last=last):
            hop = pair_at(near_ref, n * (2 * near), groups)
            leads = [pair_at(state_sp, 2 * n, groups)]
            for _ in range(count - 1 if last else count):
                leads.append(cmul(leads[-1], hop))
            if not last:
                for part in range(2):
                    put_row(state_sp, 2 * n + part, groups, leads[count][part])
            return leads

        start = index * span
        init = [local_ref[(start + t) * groups : (start + t + 1) * groups, :] for t in range(span)]
        acc = power_sum(near_ref, lead_of, states, groups, near, count, init)
        for t in range(span):
            rows_ref[t * groups : (t + 1) * groups, :] = acc[t]
        for t in range(0, span, 8):
            for k in range(groups):
                out_buf[start + t : start + t + 8, k * LANES : (k + 1) * LANES] = rows_ref[
                    pl.ds(t * groups + k, 8, stride=groups), :
                ]
        copy = pltpu.make_async_copy(
            out_buf.at[pl.ds(start, span)], out_ref.at[pl.ds(start, span)], sems.at[index]
        )
        copy.start()
        copies.append(copy)
    for copy in copies:
        copy.wait()


def per_device(n_in, n_out, inputs, time_step, decay_rate, frequency, output_real, output_imag, skip_gain):
    signal = inputs[0]
    tokens, channels = signal.shape
    states = decay_rate.shape[0]
    groups = channels // LANES
    outer = tokens // NEAR
    code_rows = 2 * groups * (states + 1)
    f32 = jnp.float32
    any_space = pl.BlockSpec(memory_space=pl.ANY)
    in_vmem = pl.BlockSpec(memory_space=pltpu.VMEM)
    in_hbm = pl.BlockSpec(memory_space=pltpu.HBM)

    def rows(count, dtype=f32):
        return pltpu.VMEM((count * groups, LANES), dtype)

    def shape(*dims):
        return jax.ShapeDtypeStruct(dims, f32)

    def kept(count):
        return pltpu.HBM((count * groups, LANES), f32)

    def hbm(array):
        return pltpu.with_memory_space_constraint(array, pltpu.HBM)

    def call(kernel, name, flops, **options):
        return pl.pallas_call(
            kernel,
            compiler_params=pltpu.CompilerParams(vmem_limit_bytes=24 * 1024 * 1024),
            cost_estimate=pl.CostEstimate(flops=flops, bytes_accessed=2_000_000, transcendentals=0),
            name=name,
            **options,
        )

    early = [
        lax.ppermute(signal, "seqout", [(i, i + j) for i in range(n_out - j)]) for j in range(1, n_out)
    ]

    parameters = (time_step.reshape(groups, LANES), decay_rate, frequency, output_real, output_imag)
    seeds, base = call(
        sums_kernel,
        "sums",
        20_000_000,
        out_shape=(kept(6 * states), shape(5 * states * groups, LANES)),
        in_specs=[any_space] * 6,
        out_specs=(in_hbm, in_vmem),
        scratch_shapes=[
            pltpu.VMEM((tokens, channels), signal.dtype),
            rows(1),
            *[pltpu.VMEM((states, channels), f32)] * 4,
            rows(tokens),
            *[rows(states)] * 4,
            rows(6 * states),
            pltpu.SemaphoreType.DMA((6,)),
        ],
    )(hbm(signal), *(hbm(array) for array in parameters))

    *messages, own = call(
        functools.partial(messages_kernel, n_in, n_out - 1),
        "messages",
        20_000_000,
        out_shape=(
            *[pltpu.HBM((code_rows, LANES), jnp.bfloat16)] * (n_in - 1),
            kept(2 * states),
        ),
        out_specs=(in_hbm,) * n_in,
        scratch_shapes=[
            pltpu.VMEM((n_out - 1, tokens * groups, LANES), f32),
            rows(4 * states),
            rows(2 * states),
            pltpu.VMEM((2, code_rows, LANES), jnp.bfloat16),
            pltpu.SemaphoreType.DMA((n_in,)),
        ],
    )(base, *early)

    received = [
        lax.ppermute(messages[d - 1], "seqin", [(i, (i + d) % n_in) for i in range(n_in)]) for d in range(1, n_in)
    ]

    pack = call(
        conv_kernel,
        "conv",
        40_000_000,
        out_shape=shape((tokens + states * (2 * FINAL_NEAR + 6)) * groups, LANES),
        in_specs=[any_space] * 4,
        scratch_shapes=[
            pltpu.VMEM((tokens, channels), signal.dtype),
            rows(1),
            rows(6 * states),
            rows(2 * NEAR * states),
            rows(2 * outer * states),
            rows(tokens),
            rows(tokens + 8),
            pltpu.SemaphoreType.DMA((4,)),
        ],
    )(hbm(signal), hbm(skip_gain.reshape(groups, LANES)), hbm(seeds), hbm(own))

    count = min(4, tokens // FINAL_NEAR)
    outputs = call(
        functools.partial(final_kernel, states),
        "final",
        20_000_000,
        out_shape=shape(tokens, channels),
        out_specs=any_space,
        scratch_shapes=[
            rows(2 * states),
            rows(count * FINAL_NEAR),
            pltpu.VMEM((tokens, channels), f32),
            pltpu.SemaphoreType.DMA((tokens // FINAL_NEAR // count,)),
        ],
    )(pack, *received)
    return outputs[None]


def solution(mesh):
    in_specs = (
        P(("groups", "seqout"), "seqin", "chan"),
        P("chan"),
        P(None, "chan"),
        P(None, "chan"),
        P(None, "chan"),
        P(None, "chan"),
        P("chan"),
    )
    out_specs = P(("groups", "seqout"), "seqin", "chan")
    return jax.shard_map(
        functools.partial(per_device, mesh.shape["seqin"], mesh.shape["seqout"]),
        mesh=mesh,
        in_specs=in_specs,
        out_specs=out_specs,
        check_vma=False,
    )
```

time: 35.7 us -> 32.6 us (0.913)
  the two profiles are of different devices: /device:TPU:0 before, /device:TPU:11 now
where the time goes in v4:
time: 32.6 us; the launch traced here: 32.4 us
  Pallas kernels  19.9 us (61%)
  waiting for transfers between devices  7.3 us (22%)
  starting transfers between devices  5.11 us (16%)
    pallas_call x1, Pallas kernels, per_device(): call(conv_kernel, 'conv', 40000000, out_shape=shape((tokens + states * (2...  6.83 us
    pallas_call x1, Pallas kernels, per_device(): call(sums_kernel, 'sums', 20000000, out_shape=(kept(6 * states), shape(5...  5.39 us
    ppermute x3, waiting for transfers between devices, per_device(): lax.ppermute(messages[d - 1], 'seqin', [(i, (i + d) % n_in) for i in rang...  4.72 us
    pallas_call x1, Pallas kernels, per_device(): call(functools.partial(messages_kernel, n_in, n_out - 1), 'messages', 200...  4.03 us
    ppermute x3, starting transfers between devices, per_device(): lax.ppermute(messages[d - 1], 'seqin', [(i, (i + d) % n_in) for i in rang...  3.83 us
    pallas_call x1, Pallas kernels, per_device(): call(functools.partial(final_kernel, states), 'final', 20000000, out_shap...  3.68 us
    ppermute x1, waiting for transfers between devices, per_device(): lax.ppermute(signal, 'seqout', [(i, i + j) for i in range(n_out - j)])  2.59 us
    ppermute x1, starting transfers between devices, per_device(): lax.ppermute(signal, 'seqout', [(i, i + j) for i in range(n_out - j)])  1.28 us
  transfers between devices with their start and end apart: 4, of which 2 were waited for; matrix products, arithmetic and copies ran while one was open for 0% of the time, Pallas kernels for 38%

profile of v4, /device:TPU:11, one launch (start us, length us, event | category | flops | bytes accessed | tf_op | source)
XLA Modules:
  0.0 32.4 jit_solution(17385584559836736081)
XLA Ops:
  0.0 1.3 %collective-permute-start = (bf16[128,1024]{1,0:T(8,128)(2,1)}, bf16[128,1024]{1,0:T(8,128)(2,1)S(1)}, u32[]{:S(2)}, u32[]{:S(2)}) collective-permute-start(bf16[128,1024]{1,0:T(8,128)(2,1)} %bitcast.4), channel_id=1, source_target_pairs={{0,2},{1,3},{4,6},{5,7},{8,10},{9,11},{12,14},{13,15},{16,18},{17,... | collective-permute-start | bytes 786440 | tf_op jit(solution)/shard_map/ppermute | solution.py:434
  1.3 5.4 %sums.1 = (f32[1536,128]{1,0:T(8,128)}, f32[1280,128]{1,0:T(8,128)S(1)}) custom-call(bf16[128,1024]{1,0:T(8,128)(2,1)} %bitcast.5, f32[8,128]{1,0:T(8,128)} %bitcast.7, f32[32,1024]{1,0:T(8,128)} %decay_hbm.1, f32[32,1024]{1,0:T(8,128)} %freq_hbm.1, f32[32,1024]{1,0:T(8,128)} %real_hbm.1, f32[32,1024]{1,0:T(8,128)} %imag_hbm.1), custom_call_target="tpu_custom_call" | custom-call | flops 20000000 | bytes 2000000 | tf_op jit(solution)/shard_map/sums/pallas_call | solution.py:438
  6.7 2.6 %collective-permute-done.refs_0_ = bf16[128,1024]{1,0:T(8,128)(2,1)S(1)} collective-permute-done((bf16[128,1024]{1,0:T(8,128)(2,1)}, bf16[128,1024]{1,0:T(8,128)(2,1)S(1)}, u32[]{:S(2)}, u32[]{:S(2)}) %collective-permute-start) | collective-permute-done | bytes 262176 | tf_op jit(solution)/shard_map/ppermute | solution.py:434
  9.3 4.0 %messages.1 = (bf16[528,128]{1,0:T(8,128)(2,1)}, bf16[528,128]{1,0:T(8,128)(2,1)}, bf16[528,128]{1,0:T(8,128)(2,1)}, f32[512,128]{1,0:T(8,128)}) custom-call(f32[1280,128]{1,0:T(8,128)S(1)} %get-tuple-element.12.base_ref, bf16[128,1024]{1,0:T(8,128)(2,1)S(1)} %collective-permute-done.refs_0_), custom_call_target="tpu_custom_call" | custom-call | flops 20000000 | bytes 2000000 | tf_op jit(solution)/shard_map/messages/pallas_call | solution.py:456
  13.3 1.3 %collective-permute-start.1 = (bf16[528,128]{1,0:T(8,128)(2,1)}, bf16[528,128]{1,0:T(8,128)(2,1)S(1)}, u32[]{:S(2)}, u32[]{:S(2)}) collective-permute-start(bf16[528,128]{1,0:T(8,128)(2,1)} %get-tuple-element.14), channel_id=1, source_target_pairs={{0,4},{4,8},{8,12},{12,0},{1,5},{5,9},{9,13},{13,1},{2,6},{6,10},{... | collective-permute-start | bytes 405512 | tf_op jit(solution)/shard_map/ppermute | solution.py:475
  14.7 1.1 %collective-permute-start.2 = (bf16[528,128]{1,0:T(8,128)(2,1)}, bf16[528,128]{1,0:T(8,128)(2,1)S(1)}, u32[]{:S(2)}, u32[]{:S(2)}) collective-permute-start(bf16[528,128]{1,0:T(8,128)(2,1)} %get-tuple-element.15), channel_id=1, source_target_pairs={{0,8},{4,12},{8,0},{12,4},{1,9},{5,13},{9,1},{13,5},{2,10},{6,14},... | collective-permute-start | bytes 405512 | tf_op jit(solution)/shard_map/ppermute | solution.py:475
  15.8 1.4 %collective-permute-start.3 = (bf16[528,128]{1,0:T(8,128)(2,1)}, bf16[528,128]{1,0:T(8,128)(2,1)S(1)}, u32[]{:S(2)}, u32[]{:S(2)}) collective-permute-start(bf16[528,128]{1,0:T(8,128)(2,1)} %get-tuple-element.16), channel_id=1, source_target_pairs={{0,12},{4,0},{8,4},{12,8},{1,13},{5,1},{9,5},{13,9},{2,14},{6,2},{... | collective-permute-start | bytes 405512 | tf_op jit(solution)/shard_map/ppermute | solution.py:475
  17.1 6.8 %conv.1.pack_ref = f32[6656,128]{1,0:T(8,128)S(1)} custom-call(bf16[128,1024]{1,0:T(8,128)(2,1)} %bitcast.6, f32[8,128]{1,0:T(8,128)} %bitcast.8, f32[1536,128]{1,0:T(8,128)} %get-tuple-element.11.seed_hbm, f32[512,128]{1,0:T(8,128)} %get-tuple-element.13.own_hbm), custom_call_target="tpu_custom_call" | custom-call | flops 40000000 | bytes 2000000 | tf_op jit(solution)/shard_map/conv/pallas_call | solution.py:478
  24.0 0.0 collective-permute-done.1.refs_0_
  24.0 0.0 collective-permute-done.2.refs_1_
  24.0 4.7 %collective-permute-done.3.refs_2_ = bf16[528,128]{1,0:T(8,128)(2,1)S(1)} collective-permute-done((bf16[528,128]{1,0:T(8,128)(2,1)}, bf16[528,128]{1,0:T(8,128)(2,1)S(1)}, u32[]{:S(2)}, u32[]{:S(2)}) %collective-permute-start.3) | collective-permute-done | bytes 135200 | tf_op jit(solution)/shard_map/ppermute | solution.py:475
  28.7 3.7 %final.1 = f32[128,1024]{1,0:T(8,128)} custom-call(f32[6656,128]{1,0:T(8,128)S(1)} %conv.1.pack_ref, bf16[528,128]{1,0:T(8,128)(2,1)S(1)} %collective-permute-done.1.refs_0_, bf16[528,128]{1,0:T(8,128)(2,1)S(1)} %collective-permute-done.2.refs_1_, bf16[528,128]{1,0:T(8,128)(2,1)S(1)} %collective-permute-done.3.refs_2_), custom_call_target="tpu_custom_call" | custom-call | flops 20000000 | bytes 2000000 | tf_op jit(solution)/shard_map/final/pallas_call | solution.py:497
Async XLA Ops:
  0.0 9.3 %collective-permute-start = (bf16[128,1024]{1,0:T(8,128)(2,1)}, bf16[128,1024]{1,0:T(8,128)(2,1)S(1)}, u32[]{:S(2)}, u32[]{:S(2)}) collective-permute-start(bf16[128,1024]{1,0:T(8,128)(2,1)} %bitcast.4), channel_id=1, source_target_pairs={{0,2},{1,3},{4,6},{5,7},{8,10},{9,11},{12,14},{13,15},{16,18},{17,... | collective-permute-start | bytes 786440 | tf_op jit(solution)/shard_map/ppermute | solution.py:434
  13.3 10.7 %collective-permute-start.1 = (bf16[528,128]{1,0:T(8,128)(2,1)}, bf16[528,128]{1,0:T(8,128)(2,1)S(1)}, u32[]{:S(2)}, u32[]{:S(2)}) collective-permute-start(bf16[528,128]{1,0:T(8,128)(2,1)} %get-tuple-element.14), channel_id=1, source_target_pairs={{0,4},{4,8},{8,12},{12,0},{1,5},{5,9},{9,13},{13,1},{2,6},{6,10},{... | collective-permute-start | bytes 405512 | tf_op jit(solution)/shard_map/ppermute | solution.py:475
  14.7 9.3 %collective-permute-start.2 = (bf16[528,128]{1,0:T(8,128)(2,1)}, bf16[528,128]{1,0:T(8,128)(2,1)S(1)}, u32[]{:S(2)}, u32[]{:S(2)}) collective-permute-start(bf16[528,128]{1,0:T(8,128)(2,1)} %get-tuple-element.15), channel_id=1, source_target_pairs={{0,8},{4,12},{8,0},{12,4},{1,9},{5,13},{9,1},{13,5},{2,10},{6,14},... | collective-permute-start | bytes 405512 | tf_op jit(solution)/shard_map/ppermute | solution.py:475
  15.8 13.0 %collective-permute-start.3 = (bf16[528,128]{1,0:T(8,128)(2,1)}, bf16[528,128]{1,0:T(8,128)(2,1)S(1)}, u32[]{:S(2)}, u32[]{:S(2)}) collective-permute-start(bf16[528,128]{1,0:T(8,128)(2,1)} %get-tuple-element.16), channel_id=1, source_target_pairs={{0,12},{4,0},{8,4},{12,8},{1,13},{5,1},{9,5},{13,9},{2,14},{6,2},{... | collective-permute-start | bytes 405512 | tf_op jit(solution)/shard_map/ppermute | solution.py:475

commit v5 on v4

--- a/solution.py
+++ b/solution.py
@@ -12,6 +12,7 @@
 FINAL_NEAR = 8
 HALF_RANGE = 125.0
 LOG_TWO = 0.6931471805599453
+SMALLEST_CODE = 2.0**-125
 
 
 def cmul(a, b):
@@ -150,107 +151,139 @@
     return total
 
 
-def sums_kernel(
-    signal_hbm, step_hbm, decay_hbm, freq_hbm, real_hbm, imag_hbm,
-    seed_hbm, base_ref,
-    signal_ref, step_ref, decay_ref, freq_ref, real_ref, imag_ref,
-    signal_sp, decay_sp, freq_sp, real_sp, imag_sp, seed_ref, sems,
-):
-    copies = start_copies(
-        (
-            (step_hbm, step_ref), (decay_hbm, decay_ref), (freq_hbm, freq_ref),
-            (signal_hbm, signal_ref), (real_hbm, real_ref), (imag_hbm, imag_ref),
-        ),
-        sems,
-    )
-    states, channels = decay_ref.shape
-    groups = channels // LANES
-    tokens = signal_ref.shape[0]
-    for copy in copies:
-        copy.wait()
-    for source, target in ((decay_ref, decay_sp), (freq_ref, freq_sp), (real_ref, real_sp), (imag_ref, imag_sp)):
-        spread_rows(source, target, states, groups, 8)
-    spread_rows(signal_ref, signal_sp, tokens, groups, 16)
-    step = step_ref[...]
-
-    def prepare(n, carry):
-        fade, lam = decay_step(step, row_at(decay_sp, n, groups), row_at(freq_sp, n, groups))
-        gain = gain_of(fade)
-        weight = (2.0 * row_at(real_sp, n, groups), 2.0 * row_at(imag_sp, n, groups))
-        put_pair(seed_ref, 6 * n, groups, lam)
-        put_pair(seed_ref, 6 * n + 2, groups, weight)
-        put_pair(seed_ref, 6 * n + 4, groups, (weight[0] * gain, weight[1] * gain))
-        own = decayed_sum(signal_sp, power_list(lam, NEAR), tokens, groups)
-        put_pair(base_ref, 5 * n, groups, lam)
-        put_pair(base_ref, 5 * n + 2, groups, (gain * own[0], gain * own[1]))
-        put_row(base_ref, 5 * n + 4, groups, gain)
-        return carry
-
-    lax.fori_loop(0, states, prepare, 0, unroll=2)
-    copy = pltpu.make_async_copy(seed_ref, seed_hbm, sems.at[0])
-    copy.start()
-    copy.wait()
+def encode(value, inverse):
+    code = jnp.exp2(jnp.abs(value) * inverse * (2.0 * HALF_RANGE) - HALF_RANGE)
+    return jnp.where(value < 0.0, -code, code)
+
+
+def decode(code, scale):
+    size = (jnp.log(jnp.maximum(jnp.abs(code), SMALLEST_CODE)) * (0.5 / HALF_RANGE / LOG_TWO) + 0.5) * scale
+    return jnp.where(code < 0.0, -size, size)
 
 
 def largest(value, most):
     return jnp.maximum(most, jnp.maximum(jnp.abs(value[0]), jnp.abs(value[1])))
 
 
-def messages_kernel(n_in, n_early, base_ref, *refs):
-    early_refs, out_refs, own_hbm = refs[:n_early], refs[n_early : n_early + n_in - 1], refs[n_early + n_in - 1]
-    signal_sp, sums_ref, own_ref, code_ref, sems = refs[n_early + n_in :]
-    tokens, channels = early_refs[0].shape
-    groups = channels // LANES
-    states = base_ref.shape[0] // (5 * groups)
-    for j in range(n_early):
-        spread_rows(early_refs[j], signal_sp.at[j], tokens, groups, 16)
-
-    def gather(n, most):
-        lam, own = pair_at(base_ref, 5 * n, groups), pair_at(base_ref, 5 * n + 2, groups)
-        gain = row_at(base_ref, 5 * n + 4, groups)
-        powers = power_list(lam, NEAR)
-        block = power_of(powers[NEAR], tokens // NEAR * n_in)
-        early = None
-        for j in reversed(range(n_early)):
-            part = decayed_sum(signal_sp.at[j], powers, tokens, groups)
-            part = (gain * part[0], gain * part[1])
-            if early is not None:
-                moved = cmul(block, early)
-                part = (part[0] + moved[0], part[1] + moved[1])
-            early = part
-        moved = cmul(block, early)
-        later = (own[0] + moved[0], own[1] + moved[1])
-        put_pair(sums_ref, 4 * n, groups, later)
-        put_pair(sums_ref, 4 * n + 2, groups, early)
-        put_pair(own_ref, 2 * n, groups, early)
-        return (largest(later, most[0]), largest(early, most[1]))
-
-    zero = jnp.zeros((groups, LANES), jnp.float32)
-    most = lax.fori_loop(0, states, gather, (zero, zero), unroll=2)
-    own_copy = pltpu.make_async_copy(own_ref, own_hbm, sems.at[0])
-    own_copy.start()
-    inverse = []
-    for kind in range(2):
-        scale = (1.01 * most[kind]).astype(jnp.bfloat16).astype(jnp.float32)
-        inverse.append(jnp.where(scale > 1e-36, 1.0 / jnp.maximum(scale, 1e-36), 0.0))
-        pair = jnp.concatenate([scale, scale], axis=0).astype(jnp.bfloat16)
-        code_ref[kind, states * 2 * groups :, :] = pair
+def write_codes(value_of, code_ref, most, states, groups):
+    scale = (1.01 * most).astype(jnp.bfloat16).astype(jnp.float32)
+    inverse = jnp.where(scale > 1e-36, 1.0 / jnp.maximum(scale, 1e-36), 0.0)
+    code_ref[states * 2 * groups :, :] = jnp.concatenate([scale, scale], axis=0).astype(jnp.bfloat16)
 
     def write(n, carry):
-        for kind in range(2):
-            value = pair_at(sums_ref, 4 * n + 2 * kind, groups)
-            code = jnp.concatenate([encode(value[part], inverse[kind]) for part in range(2)], axis=0)
-            row = pl.multiple_of(n * (2 * groups), 2 * groups)
-            code_ref[kind, pl.ds(row, 2 * groups), :] = code.astype(jnp.bfloat16)
+        value = value_of(n)
+        code = jnp.concatenate([encode(value[part], inverse) for part in range(2)], axis=0)
+        row = pl.multiple_of(n * (2 * groups), 2 * groups)
+        code_ref[pl.ds(row, 2 * groups), :] = code.astype(jnp.bfloat16)
         return carry
 
     lax.fori_loop(0, states, write, 0, unroll=4)
+
+
+def scale_at(code_ref, states, groups):
+    return code_ref[states * 2 * groups :, :].astype(jnp.float32)[0:groups, :]
+
+
+def decode_at(code_ref, n, scale, groups):
+    row = pl.multiple_of(n * (2 * groups), 2 * groups)
+    code = code_ref[pl.ds(row, 2 * groups), :].astype(jnp.float32)
+    return tuple(decode(code[part * groups : (part + 1) * groups, :], scale) for part in range(2))
+
+
+def sums_kernel(
+    n_in, send, signal_hbm, step_hbm, decay_hbm, freq_hbm,
+    result_ref,
+    signal_ref, step_ref, decay_ref, freq_ref,
+    signal_sp, decay_sp, freq_sp, base_ref, code_ref, sems,
+):
+    place = lax.axis_index("seqout")
+    needed = place < lax.axis_size("seqout") - 1 if send else place > 0
+
+    @pl.when(needed)
+    def _():
+        copies = start_copies(
+            ((step_hbm, step_ref), (decay_hbm, decay_ref), (freq_hbm, freq_ref), (signal_hbm, signal_ref)), sems
+        )
+        states, channels = decay_ref.shape
+        groups = channels // LANES
+        tokens = signal_ref.shape[0]
+        for copy in copies[:3]:
+            copy.wait()
+        for source, target in ((decay_ref, decay_sp), (freq_ref, freq_sp)):
+            spread_rows(source, target, states, groups, 8)
+        copies[3].wait()
+        spread_rows(signal_ref, signal_sp, tokens, groups, 16)
+        step = step_ref[...]
+        target_ref = base_ref if send else result_ref
+
+        def prepare(n, most):
+            fade, lam = decay_step(step, row_at(decay_sp, n, groups), row_at(freq_sp, n, groups))
+            gain = gain_of(fade)
+            powers = power_list(lam, NEAR)
+            own = decayed_sum(signal_sp, powers, tokens, groups)
+            own = (gain * own[0], gain * own[1])
+            if not send:
+                put_pair(target_ref, 4 * n, groups, power_of(powers[NEAR], tokens // NEAR * n_in))
+            put_pair(target_ref, 4 * n + 2, groups, own)
+            return largest(own, most)
+
+        most = lax.fori_loop(0, states, prepare, jnp.zeros((groups, LANES), jnp.float32), unroll=4)
+        if send:
+            write_codes(lambda n: pair_at(base_ref, 4 * n + 2, groups), code_ref, most, states, groups)
+            copy = pltpu.make_async_copy(code_ref, result_ref, sems.at[0])
+            copy.start()
+            copy.wait()
+
+
+def messages_kernel(n_in, n_early, base_ref, sent_hbm, *refs):
+    received_refs, out_refs, own_hbm = refs[:n_early], refs[n_early : n_early + n_in - 1], refs[n_early + n_in - 1]
+    later_ref, own_ref, code_ref, sems = refs[n_early + n_in :]
+    groups = (received_refs[0].shape[0] - base_ref.shape[0] // 2) // 2
+    states = base_ref.shape[0] // (4 * groups)
+    first_block = lax.axis_index("seqout") == 0
+
+    @pl.when(first_block)
+    def _():
+        copy = pltpu.make_async_copy(sent_hbm, code_ref.at[0], sems.at[0])
+        copy.start()
+        own_ref[...] = jnp.zeros_like(own_ref)
+        code_ref[1] = jnp.zeros_like(code_ref[1])
+        copy.wait()
+
+    @pl.when(jnp.logical_not(first_block))
+    def _():
+        scales = [scale_at(ref, states, groups) for ref in received_refs]
+
+        def gather(n, most):
+            block, own = pair_at(base_ref, 4 * n, groups), pair_at(base_ref, 4 * n + 2, groups)
+            early = None
+            for ref, scale in zip(reversed(received_refs), reversed(scales)):
+                part = decode_at(ref, n, scale, groups)
+                if early is not None:
+                    moved = cmul(block, early)
+                    part = (part[0] + moved[0], part[1] + moved[1])
+                early = part
+            moved = cmul(block, early)
+            later = (own[0] + moved[0], own[1] + moved[1])
+            put_pair(later_ref, 2 * n, groups, later)
+            put_pair(own_ref, 2 * n, groups, early)
+            return (largest(later, most[0]), largest(early, most[1]))
+
+        zero = jnp.zeros((groups, LANES), jnp.float32)
+        most = lax.fori_loop(0, states, gather, (zero, zero), unroll=4)
+        write_codes(lambda n: pair_at(later_ref, 2 * n, groups), code_ref.at[0], most[0], states, groups)
+        if n_early == 1:
+            code_ref[1] = received_refs[0][...]
+        else:
+            write_codes(lambda n: pair_at(own_ref, 2 * n, groups), code_ref.at[1], most[1], states, groups)
+
     place = lax.axis_index("seqin")
-    copies = [own_copy]
+    copies = [pltpu.make_async_copy(own_ref, own_hbm, sems.at[0])]
     for d in range(1, n_in):
         kind = (place + d) // n_in
         copies.append(pltpu.make_async_copy(code_ref.at[kind], out_refs[d - 1], sems.at[d]))
-        copies[-1].start()
+    for copy in copies:
+        copy.start()
     for copy in copies:
         copy.wait()
 
@@ -264,23 +297,35 @@
 
 
 def conv_kernel(
-    signal_hbm, skip_hbm, seed_hbm, own_hbm, pack_ref,
-    signal_ref, skip_ref, seed_ref, near_ref, lead_ref, signal_sp, taps_pad, sems,
+    signal_hbm, skip_hbm, step_hbm, decay_hbm, freq_hbm, real_hbm, imag_hbm, own_hbm, pack_ref,
+    signal_ref, skip_ref, step_ref, decay_ref, freq_ref, real_ref, imag_ref,
+    decay_sp, freq_sp, real_sp, imag_sp, near_ref, lead_ref, signal_sp, taps_pad, sems,
 ):
     tokens, channels = signal_ref.shape
     groups = channels // LANES
-    states = seed_ref.shape[0] // (6 * groups)
+    states = decay_ref.shape[0]
     outer = tokens // NEAR
     tile = 8
     out_ref, few_ref, shift_ref, hop_ref, own_ref = split_pack(pack_ref, tokens, states, groups)
     copies = start_copies(
-        ((seed_hbm, seed_ref), (signal_hbm, signal_ref), (skip_hbm, skip_ref), (own_hbm, own_ref)), sems
+        (
+            (step_hbm, step_ref), (decay_hbm, decay_ref), (freq_hbm, freq_ref), (real_hbm, real_ref),
+            (imag_hbm, imag_ref), (signal_hbm, signal_ref), (skip_hbm, skip_ref), (own_hbm, own_ref),
+        ),
+        sems,
     )
     taps_pad[0 : tile * groups, :] = jnp.zeros((tile * groups, LANES), jnp.float32)
-    copies[0].wait()
+    for copy in copies[:5]:
+        copy.wait()
+    for source, target in ((decay_ref, decay_sp), (freq_ref, freq_sp), (real_ref, real_sp), (imag_ref, imag_sp)):
+        spread_rows(source, target, states, groups, 8)
+    step = step_ref[...]
 
     def prepare(n, carry):
-        lam, weight, lead = (pair_at(seed_ref, 6 * n + 2 * i, groups) for i in range(3))
+        fade, lam = decay_step(step, row_at(decay_sp, n, groups), row_at(freq_sp, n, groups))
+        gain = gain_of(fade)
+        weight = (2.0 * row_at(real_sp, n, groups), 2.0 * row_at(imag_sp, n, groups))
+        lead = (weight[0] * gain, weight[1] * gain)
         powers = power_list(lam, NEAR)
         for u in range(1, NEAR):
             put_pair(near_ref, n * (2 * NEAR) + 2 * u, groups, powers[u])
@@ -295,7 +340,7 @@
         return carry
 
     lax.fori_loop(0, states, prepare, 0, unroll=2)
-    for copy in copies[1:]:
+    for copy in copies[5:]:
         copy.wait()
     spread_rows(signal_ref, signal_sp, tokens, groups, 16)
     zero = jnp.zeros((groups, LANES), jnp.float32)
@@ -328,16 +373,6 @@
             put_row(out_ref, ti * tile + t, groups, acc[t])
 
 
-def encode(value, inverse):
-    code = jnp.exp2(jnp.abs(value) * inverse * (2.0 * HALF_RANGE) - HALF_RANGE)
-    return jnp.where(value < 0.0, -code, code)
-
-
-def decode(code, scale):
-    size = (jnp.log(jnp.abs(code)) * (0.5 / HALF_RANGE / LOG_TWO) + 0.5) * scale
-    return jnp.where(code < 0.0, -size, size)
-
-
 def final_kernel(states, pack_ref, *refs):
     message_refs, out_ref = refs[:-5], refs[-5]
     state_sp, rows_ref, out_buf, sems = refs[-4:]
@@ -346,18 +381,14 @@
     near = FINAL_NEAR
     outer = tokens // near
     local_ref, near_ref, shift_ref, hop_ref, own_ref = split_pack(pack_ref, tokens, states, groups)
-    scales = [ref[states * 2 * groups :, :].astype(jnp.float32)[0:groups, :] for ref in message_refs]
+    scales = [scale_at(ref, states, groups) for ref in message_refs]
 
     def enter(n, carry):
         hop = pair_at(hop_ref, 2 * n, groups)
         state = pair_at(own_ref, 2 * n, groups)
-        row = pl.multiple_of(n * (2 * groups), 2 * groups)
         for ref, scale in zip(reversed(message_refs), reversed(scales)):
-            code = ref[pl.ds(row, 2 * groups), :].astype(jnp.float32)
-            moved = cmul(hop, state)
-            state = tuple(
-                moved[part] + decode(code[part * groups : (part + 1) * groups, :], scale) for part in range(2)
-            )
+            moved, part = cmul(hop, state), decode_at(ref, n, scale, groups)
+            state = (moved[0] + part[0], moved[1] + part[1])
         put_pair(state_sp, 2 * n, groups, cmul(pair_at(shift_ref, 2 * n, groups), state))
         return carry
 
@@ -430,46 +461,49 @@
             **options,
         )
 
-    early = [
-        lax.ppermute(signal, "seqout", [(i, i + j) for i in range(n_out - j)]) for j in range(1, n_out)
-    ]
-
-    parameters = (time_step.reshape(groups, LANES), decay_rate, frequency, output_real, output_imag)
-    seeds, base = call(
-        sums_kernel,
-        "sums",
-        20_000_000,
-        out_shape=(kept(6 * states), shape(5 * states * groups, LANES)),
-        in_specs=[any_space] * 6,
-        out_specs=(in_hbm, in_vmem),
-        scratch_shapes=[
-            pltpu.VMEM((tokens, channels), signal.dtype),
-            rows(1),
-            *[pltpu.VMEM((states, channels), f32)] * 4,
-            rows(tokens),
-            *[rows(states)] * 4,
-            rows(6 * states),
-            pltpu.SemaphoreType.DMA((6,)),
-        ],
-    )(hbm(signal), *(hbm(array) for array in parameters))
+    parameters = tuple(hbm(array) for array in (time_step.reshape(groups, LANES), decay_rate, frequency))
+    codes = pltpu.HBM((code_rows, LANES), jnp.bfloat16)
+
+    def sums(send):
+        return call(
+            functools.partial(sums_kernel, n_in, send),
+            "sums" if send else "base",
+            20_000_000,
+            out_shape=codes if send else shape(4 * states * groups, LANES),
+            in_specs=[any_space] * 4,
+            out_specs=in_hbm if send else in_vmem,
+            scratch_shapes=[
+                pltpu.VMEM((tokens, channels), signal.dtype),
+                rows(1),
+                *[pltpu.VMEM((states, channels), f32)] * 2,
+                rows(tokens),
+                *[rows(states)] * 2,
+                rows(4 * states if send else 1),
+                pltpu.VMEM((code_rows if send else 16, LANES), jnp.bfloat16),
+                pltpu.SemaphoreType.DMA((4,)),
+            ],
+        )(hbm(signal), *parameters)
+
+    code = sums(True)
+    early = [lax.ppermute(code, "seqout", [(i, i + j) for i in range(n_out - j)]) for j in range(1, n_out)]
+    parameters = lax.optimization_barrier((code, *parameters))[1:]
+    parameters = tuple(hbm(array) for array in parameters)
+    base = sums(False)
 
     *messages, own = call(
         functools.partial(messages_kernel, n_in, n_out - 1),
         "messages",
-        20_000_000,
-        out_shape=(
-            *[pltpu.HBM((code_rows, LANES), jnp.bfloat16)] * (n_in - 1),
-            kept(2 * states),
-        ),
+        4_000_000,
+        out_shape=(*[codes] * (n_in - 1), kept(2 * states)),
+        in_specs=(in_vmem, any_space, *[in_vmem] * (n_out - 1)),
         out_specs=(in_hbm,) * n_in,
         scratch_shapes=[
-            pltpu.VMEM((n_out - 1, tokens * groups, LANES), f32),
-            rows(4 * states),
+            rows(2 * states),
             rows(2 * states),
             pltpu.VMEM((2, code_rows, LANES), jnp.bfloat16),
             pltpu.SemaphoreType.DMA((n_in,)),
         ],
-    )(base, *early)
+    )(base, hbm(code), *early)
 
     received = [
         lax.ppermute(messages[d - 1], "seqin", [(i, (i + d) % n_in) for i in range(n_in)]) for d in range(1, n_in)
@@ -480,18 +514,23 @@
         "conv",
         40_000_000,
         out_shape=shape((tokens + states * (2 * FINAL_NEAR + 6)) * groups, LANES),
-        in_specs=[any_space] * 4,
+        in_specs=[any_space] * 8,
         scratch_shapes=[
             pltpu.VMEM((tokens, channels), signal.dtype),
             rows(1),
-            rows(6 * states),
+            rows(1),
+            *[pltpu.VMEM((states, channels), f32)] * 4,
+            *[rows(states)] * 4,
             rows(2 * NEAR * states),
             rows(2 * outer * states),
             rows(tokens),
             rows(tokens + 8),
-            pltpu.SemaphoreType.DMA((4,)),
+            pltpu.SemaphoreType.DMA((8,)),
         ],
-    )(hbm(signal), hbm(skip_gain.reshape(groups, LANES)), hbm(seeds), hbm(own))
+    )(
+        hbm(signal), hbm(skip_gain.reshape(groups, LANES)), *parameters,
+        hbm(output_real), hbm(output_imag), hbm(own),
+    )
 
     count = min(4, tokens // FINAL_NEAR)
     outputs = call(

time: 32.6 us -> 30.7 us (0.942)
  Pallas kernels: 19.9 us -> 16.7 us
  waiting for transfers between devices: 7.3 us -> 8.61 us
    pallas_call x2 -> x3, Pallas kernels: 9.42 us -> 5.6 us  [the longest x2 4.34 us: sums(): call(functools.partial(sums_kernel, n_in, send), 'sums' if send else 'bas...]
    ppermute x1, waiting for transfers between devices: 2.59 us -> 4.52 us  [per_device(): lax.ppermute(code, 'seqout', [(i, i + j) for i in range(n_out - j)])]
    ppermute x3, waiting for transfers between devices: 4.72 us -> 4.09 us  [per_device(): lax.ppermute(messages[d - 1], 'seqin', [(i, (i + d) % n_in) for i in rang...]
    pallas_call x1, Pallas kernels: 6.83 us -> 7.37 us  [per_device(): call(conv_kernel, 'conv', 40000000, out_shape=shape((tokens + states * (2...]
  transfers between devices with their start and end apart: 4 -> 4, of which waited for: 2 -> 3; matrix products, arithmetic and copies ran while one was open for 0% -> 0% of each run, Pallas kernels for 38% -> 38%
where the time goes in v5:
time: 30.7 us; the launch traced here: 30.5 us
  Pallas kernels  16.7 us (54%)
  waiting for transfers between devices  8.61 us (28%)
  starting transfers between devices  5.12 us (17%)
    pallas_call x1, Pallas kernels, per_device(): call(conv_kernel, 'conv', 40000000, out_shape=shape((tokens + states * (2...  7.37 us
    ppermute x1, waiting for transfers between devices, per_device(): lax.ppermute(code, 'seqout', [(i, i + j) for i in range(n_out - j)])  4.52 us
    pallas_call x2, Pallas kernels, sums(): call(functools.partial(sums_kernel, n_in, send), 'sums' if send else 'bas...  4.34 us
    ppermute x3, waiting for transfers between devices, per_device(): lax.ppermute(messages[d - 1], 'seqin', [(i, (i + d) % n_in) for i in rang...  4.09 us
    ppermute x3, starting transfers between devices, per_device(): lax.ppermute(messages[d - 1], 'seqin', [(i, (i + d) % n_in) for i in rang...  3.83 us
    pallas_call x1, Pallas kernels, per_device(): call(functools.partial(final_kernel, states), 'final', 20000000, out_shap...  3.74 us
    ppermute x1, starting transfers between devices, per_device(): lax.ppermute(code, 'seqout', [(i, i + j) for i in range(n_out - j)])  1.29 us
    pallas_call x1, Pallas kernels, per_device(): call(functools.partial(messages_kernel, n_in, n_out - 1), 'messages', 400...  1.26 us
  transfers between devices with their start and end apart: 4, of which 3 were waited for; matrix products, arithmetic and copies ran while one was open for 0% of the time, Pallas kernels for 38%

profile of v5, /device:TPU:11, one launch (start us, length us, event | category | flops | bytes accessed | tf_op | source)
XLA Modules:
  0.0 30.5 jit_solution(609233465373744023)
XLA Ops:
  0.0 1.3 %collective-permute-start = (bf16[528,128]{1,0:T(8,128)(2,1)}, bf16[528,128]{1,0:T(8,128)(2,1)S(1)}, u32[]{:S(2)}, u32[]{:S(2)}) collective-permute-start(bf16[528,128]{1,0:T(8,128)(2,1)} %sums.1.sent_hbm), channel_id=1, source_target_pairs={{0,2},{1,3},{4,6},{5,7},{8,10},{9,11},{12,14},{13,15},{16,18},{17,... | collective-permute-start | bytes 405512 | tf_op jit(solution)/shard_map/ppermute | solution.py:488
  1.3 4.3 %base.1.base_ref = f32[1024,128]{1,0:T(8,128)S(1)} custom-call(bf16[128,1024]{1,0:T(8,128)(2,1)} %bitcast.5, f32[8,128]{1,0:T(8,128)} %bitcast.8, f32[32,1024]{1,0:T(8,128)} %decay_hbm.3, f32[32,1024]{1,0:T(8,128)} %freq_hbm.3), custom_call_target="tpu_custom_call" | custom-call | flops 20000000 | bytes 2000000 | tf_op jit(solution)/shard_map/base/pallas_call | solution.py:468
  5.7 4.5 %collective-permute-done.refs_0_ = bf16[528,128]{1,0:T(8,128)(2,1)S(1)} collective-permute-done((bf16[528,128]{1,0:T(8,128)(2,1)}, bf16[528,128]{1,0:T(8,128)(2,1)S(1)}, u32[]{:S(2)}, u32[]{:S(2)}) %collective-permute-start) | collective-permute-done | bytes 135200 | tf_op jit(solution)/shard_map/ppermute | solution.py:488
  10.2 1.3 %messages.1 = (bf16[528,128]{1,0:T(8,128)(2,1)}, bf16[528,128]{1,0:T(8,128)(2,1)}, bf16[528,128]{1,0:T(8,128)(2,1)}, f32[512,128]{1,0:T(8,128)}) custom-call(f32[1024,128]{1,0:T(8,128)S(1)} %base.1.base_ref, bf16[528,128]{1,0:T(8,128)(2,1)} %sums.1.sent_hbm, bf16[528,128]{1,0:T(8,128)(2,1)S(1)} %collective-permute-done.refs_0_), custom_call_target="tpu_custom_call" | custom-call | flops 4000000 | bytes 2000000 | tf_op jit(solution)/shard_map/messages/pallas_call | solution.py:493
  11.4 1.3 %collective-permute-start.1 = (bf16[528,128]{1,0:T(8,128)(2,1)}, bf16[528,128]{1,0:T(8,128)(2,1)S(1)}, u32[]{:S(2)}, u32[]{:S(2)}) collective-permute-start(bf16[528,128]{1,0:T(8,128)(2,1)} %get-tuple-element.16), channel_id=1, source_target_pairs={{0,4},{4,8},{8,12},{12,0},{1,5},{5,9},{9,13},{13,1},{2,6},{6,10},{... | collective-permute-start | bytes 405512 | tf_op jit(solution)/shard_map/ppermute | solution.py:509
  12.8 1.1 %collective-permute-start.2 = (bf16[528,128]{1,0:T(8,128)(2,1)}, bf16[528,128]{1,0:T(8,128)(2,1)S(1)}, u32[]{:S(2)}, u32[]{:S(2)}) collective-permute-start(bf16[528,128]{1,0:T(8,128)(2,1)} %get-tuple-element.17), channel_id=1, source_target_pairs={{0,8},{4,12},{8,0},{12,4},{1,9},{5,13},{9,1},{13,5},{2,10},{6,14},... | collective-permute-start | bytes 405512 | tf_op jit(solution)/shard_map/ppermute | solution.py:509
  13.9 1.4 %collective-permute-start.3 = (bf16[528,128]{1,0:T(8,128)(2,1)}, bf16[528,128]{1,0:T(8,128)(2,1)S(1)}, u32[]{:S(2)}, u32[]{:S(2)}) collective-permute-start(bf16[528,128]{1,0:T(8,128)(2,1)} %get-tuple-element.18), channel_id=1, source_target_pairs={{0,12},{4,0},{8,4},{12,8},{1,13},{5,1},{9,5},{13,9},{2,14},{6,2},{... | collective-permute-start | bytes 405512 | tf_op jit(solution)/shard_map/ppermute | solution.py:509
  15.3 7.4 %conv.1.pack_ref = f32[6656,128]{1,0:T(8,128)S(1)} custom-call(bf16[128,1024]{1,0:T(8,128)(2,1)} %bitcast.6, f32[8,128]{1,0:T(8,128)} %bitcast.10, f32[8,128]{1,0:T(8,128)} %bitcast.9, f32[32,1024]{1,0:T(8,128)} %decay_hbm.3, f32[32,1024]{1,0:T(8,128)} %freq_hbm.3, f32[32,1024]{1,0:T(8,128)} %real_hbm.1, f32[32,1024]{1,0:T(8,128)} %imag_hbm.1, ...), custom_call_target="tpu_custom_call" | custom-call | flops 40000000 | bytes 2000000 | tf_op jit(solution)/shard_map/conv/pallas_call | solution.py:512
  22.7 0.0 collective-permute-done.1.refs_0_
  22.7 0.8 %collective-permute-done.2.refs_1_ = bf16[528,128]{1,0:T(8,128)(2,1)S(1)} collective-permute-done((bf16[528,128]{1,0:T(8,128)(2,1)}, bf16[528,128]{1,0:T(8,128)(2,1)S(1)}, u32[]{:S(2)}, u32[]{:S(2)}) %collective-permute-start.2) | collective-permute-done | bytes 135200 | tf_op jit(solution)/shard_map/ppermute | solution.py:509
  23.5 3.3 %collective-permute-done.3.refs_2_ = bf16[528,128]{1,0:T(8,128)(2,1)S(1)} collective-permute-done((bf16[528,128]{1,0:T(8,128)(2,1)}, bf16[528,128]{1,0:T(8,128)(2,1)S(1)}, u32[]{:S(2)}, u32[]{:S(2)}) %collective-permute-start.3) | collective-permute-done | bytes 135200 | tf_op jit(solution)/shard_map/ppermute | solution.py:509
  26.8 3.7 %final.1 = f32[128,1024]{1,0:T(8,128)} custom-call(f32[6656,128]{1,0:T(8,128)S(1)} %conv.1.pack_ref, bf16[528,128]{1,0:T(8,128)(2,1)S(1)} %collective-permute-done.1.refs_0_, bf16[528,128]{1,0:T(8,128)(2,1)S(1)} %collective-permute-done.2.refs_1_, bf16[528,128]{1,0:T(8,128)(2,1)S(1)} %collective-permute-done.3.refs_2_), custom_call_target="tpu_custom_call" | custom-call | flops 20000000 | bytes 2000000 | tf_op jit(solution)/shard_map/final/pallas_call | solution.py:536
  (1 shorter events, 0.0 us)
Async XLA Ops:
  0.0 10.1 %collective-permute-start = (bf16[528,128]{1,0:T(8,128)(2,1)}, bf16[528,128]{1,0:T(8,128)(2,1)S(1)}, u32[]{:S(2)}, u32[]{:S(2)}) collective-permute-start(bf16[528,128]{1,0:T(8,128)(2,1)} %sums.1.sent_hbm), channel_id=1, source_target_pairs={{0,2},{1,3},{4,6},{5,7},{8,10},{9,11},{12,14},{13,15},{16,18},{17,... | collective-permute-start | bytes 405512 | tf_op jit(solution)/shard_map/ppermute | solution.py:488
  11.4 11.2 %collective-permute-start.1 = (bf16[528,128]{1,0:T(8,128)(2,1)}, bf16[528,128]{1,0:T(8,128)(2,1)S(1)}, u32[]{:S(2)}, u32[]{:S(2)}) collective-permute-start(bf16[528,128]{1,0:T(8,128)(2,1)} %get-tuple-element.16), channel_id=1, source_target_pairs={{0,4},{4,8},{8,12},{12,0},{1,5},{5,9},{9,13},{13,1},{2,6},{6,10},{... | collective-permute-start | bytes 405512 | tf_op jit(solution)/shard_map/ppermute | solution.py:509
  12.8 10.7 %collective-permute-start.2 = (bf16[528,128]{1,0:T(8,128)(2,1)}, bf16[528,128]{1,0:T(8,128)(2,1)S(1)}, u32[]{:S(2)}, u32[]{:S(2)}) collective-permute-start(bf16[528,128]{1,0:T(8,128)(2,1)} %get-tuple-element.17), channel_id=1, source_target_pairs={{0,8},{4,12},{8,0},{12,4},{1,9},{5,13},{9,1},{13,5},{2,10},{6,14},... | collective-permute-start | bytes 405512 | tf_op jit(solution)/shard_map/ppermute | solution.py:509
  13.9 12.9 %collective-permute-start.3 = (bf16[528,128]{1,0:T(8,128)(2,1)}, bf16[528,128]{1,0:T(8,128)(2,1)S(1)}, u32[]{:S(2)}, u32[]{:S(2)}) collective-permute-start(bf16[528,128]{1,0:T(8,128)(2,1)} %get-tuple-element.18), channel_id=1, source_target_pairs={{0,12},{4,0},{8,4},{12,8},{1,13},{5,1},{9,5},{13,9},{2,14},{6,2},{... | collective-permute-start | bytes 405512 | tf_op jit(solution)/shard_map/ppermute | solution.py:509

commit v6 on v5

--- a/solution.py
+++ b/solution.py
@@ -10,6 +10,7 @@
 LANES = 128
 NEAR = 16
 FINAL_NEAR = 8
+SUM_NEAR = 8
 HALF_RANGE = 125.0
 LOG_TWO = 0.6931471805599453
 SMALLEST_CODE = 2.0**-125
@@ -127,14 +128,14 @@
 
 
 def decayed_sum(signal_sp, powers, tokens, groups):
-    a_tile = min(4, tokens // NEAR)
+    a_tile = min(4, tokens // SUM_NEAR)
     total = None
-    for first in range(0, tokens // NEAR, a_tile):
+    for first in range(0, tokens // SUM_NEAR, a_tile):
         real, imag = [None] * a_tile, [None] * a_tile
-        for u in range(NEAR):
-            power = NEAR - 1 - u
+        for u in range(SUM_NEAR):
+            power = SUM_NEAR - 1 - u
             for a in range(a_tile):
-                row = ((first + a) * NEAR + u) * groups
+                row = ((first + a) * SUM_NEAR + u) * groups
                 drive = signal_sp[row : row + groups, :]
                 if power:
                     add_real, add_imag = powers[power][0] * drive, powers[power][1] * drive
@@ -146,7 +147,7 @@
             if total is None:
                 total = (real[a], imag[a])
             else:
-                moved = cmul(powers[NEAR], total)
+                moved = cmul(powers[SUM_NEAR], total)
                 total = (moved[0] + real[a], moved[1] + imag[a])
     return total
 
@@ -217,13 +218,11 @@
         target_ref = base_ref if send else result_ref
 
         def prepare(n, most):
-            fade, lam = decay_step(step, row_at(decay_sp, n, groups), row_at(freq_sp, n, groups))
-            gain = gain_of(fade)
-            powers = power_list(lam, NEAR)
+            _, lam = decay_step(step, row_at(decay_sp, n, groups), row_at(freq_sp, n, groups))
+            powers = power_list(lam, SUM_NEAR)
             own = decayed_sum(signal_sp, powers, tokens, groups)
-            own = (gain * own[0], gain * own[1])
             if not send:
-                put_pair(target_ref, 4 * n, groups, power_of(powers[NEAR], tokens // NEAR * n_in))
+                put_pair(target_ref, 4 * n, groups, power_of(powers[SUM_NEAR], tokens // SUM_NEAR * n_in))
             put_pair(target_ref, 4 * n + 2, groups, own)
             return largest(own, most)
 
@@ -331,7 +330,7 @@
             put_pair(near_ref, n * (2 * NEAR) + 2 * u, groups, powers[u])
         for u in range(FINAL_NEAR):
             put_pair(few_ref, n * (2 * FINAL_NEAR) + 2 * u, groups, powers[u if u else FINAL_NEAR])
-        put_pair(shift_ref, 2 * n, groups, cmul(weight, lam))
+        put_pair(shift_ref, 2 * n, groups, cmul(lead, lam))
         put_pair(hop_ref, 2 * n, groups, power_of(powers[NEAR], outer))
         for a in range(outer):
             if a:
@@ -354,7 +353,177 @@
         for t in range(count * NEAR):
             put_row(taps_pad, tile + first * NEAR + t, groups, acc[t])
 
-    skip = skip_ref[...]
+    convolve(signal_sp, taps_pad, skip_ref[...], out_ref, tokens, groups)
+
+
+def pair_sums_body(signal_hbm, step_hbm, decay_hbm, freq_hbm, base_ref, code_ref, buffers, sems):
+    signal_ref, step_ref, decay_ref, freq_ref, signal_sp, decay_sp, freq_sp = buffers
+    copies = start_copies(
+        ((step_hbm, step_ref), (decay_hbm, decay_ref), (freq_hbm, freq_ref), (signal_hbm, signal_ref)), sems
+    )
+    states, channels = decay_ref.shape
+    groups = channels // LANES
+    tokens = signal_ref.shape[0]
+    for copy in copies[:3]:
+        copy.wait()
+    for source, target in ((decay_ref, decay_sp), (freq_ref, freq_sp)):
+        spread_rows(source, target, states, groups, 8)
+    copies[3].wait()
+    spread_rows(signal_ref, signal_sp, tokens, groups, 16)
+    step = step_ref[...]
+
+    def prepare(n, most):
+        _, lam = decay_step(step, row_at(decay_sp, n, groups), row_at(freq_sp, n, groups))
+        powers = power_list(lam, SUM_NEAR)
+        own = decayed_sum(signal_sp, powers, tokens, groups)
+        put_pair(base_ref, 4 * n, groups, power_of(powers[SUM_NEAR], tokens // SUM_NEAR))
+        put_pair(base_ref, 4 * n + 2, groups, own)
+        return largest(own, most)
+
+    most = lax.fori_loop(0, states, prepare, jnp.zeros((groups, LANES), jnp.float32), unroll=4)
+    write_codes(lambda n: pair_at(base_ref, 4 * n + 2, groups), code_ref, most, states, groups)
+
+
+def pair_sums_kernel(
+    first_block, signal_hbm, step_hbm, decay_hbm, freq_hbm, *rest
+):
+    if not first_block:
+        rest = rest[2:]
+    *out_refs, signal_ref, step_ref, decay_ref, freq_ref, signal_sp, decay_sp, freq_sp, base_ref, code_ref, sems = rest
+    buffers = (signal_ref, step_ref, decay_ref, freq_ref, signal_sp, decay_sp, freq_sp)
+
+    @pl.when((lax.axis_index("seqout") == 0) == first_block)
+    def _():
+        pair_sums_body(signal_hbm, step_hbm, decay_hbm, freq_hbm, base_ref, code_ref, buffers, sems)
+        pairs = [(base_ref, out_refs[0])] + [(code_ref, ref) for ref in out_refs[1:]]
+        for copy in start_copies(pairs, sems):
+            copy.wait()
+
+
+def joined(hop, mine, other, second):
+    before = tuple(jnp.where(second, other[part], mine[part]) for part in range(2))
+    after = tuple(jnp.where(second, mine[part], other[part]) for part in range(2))
+    moved = cmul(hop, before)
+    return (moved[0] + after[0], moved[1] + after[1])
+
+
+def pair_early_kernel(base_ref, early_ref, early_partner_ref, held_ref):
+    groups = (early_ref.shape[0] - base_ref.shape[0] // 2) // 2
+    states = base_ref.shape[0] // (4 * groups)
+    second = lax.rem(lax.axis_index("seqin"), 2) == 1
+    scales = [scale_at(ref, states, groups) for ref in (early_ref, early_partner_ref)]
+
+    def gather(n, carry):
+        hop = pair_at(base_ref, 4 * n, groups)
+        early, early_partner = (
+            decode_at(ref, n, scale, groups) for ref, scale in zip((early_ref, early_partner_ref), scales)
+        )
+        put_pair(held_ref, 6 * n, groups, hop)
+        put_pair(held_ref, 6 * n + 2, groups, pair_at(base_ref, 4 * n + 2, groups))
+        put_pair(held_ref, 6 * n + 4, groups, joined(hop, early, early_partner, second))
+        return carry
+
+    lax.fori_loop(0, states, gather, 0, unroll=4)
+
+
+def pair_message_kernel(held_ref, partner_ref, message_hbm, known_hbm, *scratch):
+    message_ref, known_ref, code_ref, sems = scratch
+    groups = (partner_ref.shape[0] - held_ref.shape[0] // 3) // 2
+    states = held_ref.shape[0] // (6 * groups)
+    place = lax.axis_index("seqin")
+    second = lax.rem(place, 2) == 1
+    upper = place >= 2
+    scale = scale_at(partner_ref, states, groups)
+
+    def gather(n, most):
+        hop, own, early_total = (pair_at(held_ref, 6 * n + 2 * i, groups) for i in range(3))
+        partner = decode_at(partner_ref, n, scale, groups)
+        total = joined(hop, own, partner, second)
+        hop2 = cmul(hop, hop)
+        moved2 = cmul(hop2, early_total)
+        moved4 = cmul(hop2, moved2)
+        moved3 = cmul(hop, moved2)
+        message = tuple(jnp.where(upper, early_total[part], total[part] + moved4[part]) for part in range(2))
+        known = tuple(jnp.where(second, moved3[part] + partner[part], moved2[part]) for part in range(2))
+        put_pair(message_ref, 2 * n, groups, message)
+        put_pair(known_ref, 2 * n, groups, known)
+        return largest(message, most)
+
+    most = lax.fori_loop(0, states, gather, jnp.zeros((groups, LANES), jnp.float32), unroll=4)
+    known_copy = pltpu.make_async_copy(known_ref, known_hbm, sems.at[0])
+    known_copy.start()
+    write_codes(lambda n: pair_at(message_ref, 2 * n, groups), code_ref, most, states, groups)
+    copy = pltpu.make_async_copy(code_ref, message_hbm, sems.at[1])
+    copy.start()
+    known_copy.wait()
+    copy.wait()
+
+
+def taps_kernel(
+    step_hbm, decay_hbm, freq_hbm, real_hbm, imag_hbm, base_hbm,
+    taps_hbm, tables_hbm, late_hbm, base_ref,
+    step_ref, decay_ref, freq_ref, real_ref, imag_ref,
+    decay_sp, freq_sp, real_sp, imag_sp, near_ref, lead_ref, late_ref, taps_ref, tables_ref, sems,
+):
+    copies = start_copies(
+        (
+            (step_hbm, step_ref), (decay_hbm, decay_ref), (freq_hbm, freq_ref), (real_hbm, real_ref),
+            (imag_hbm, imag_ref), (base_hbm, base_ref),
+        ),
+        sems,
+    )
+    states, channels = decay_ref.shape
+    groups = channels // LANES
+    half = taps_ref.shape[0] // groups
+    outer = half // NEAR
+    shift_row, hop_row = states * 2 * FINAL_NEAR, states * (2 * FINAL_NEAR + 2)
+    for copy in copies[:5]:
+        copy.wait()
+    for source, target in ((decay_ref, decay_sp), (freq_ref, freq_sp), (real_ref, real_sp), (imag_ref, imag_sp)):
+        spread_rows(source, target, states, groups, 8)
+    step = step_ref[...]
+
+    def prepare(n, carry):
+        fade, lam = decay_step(step, row_at(decay_sp, n, groups), row_at(freq_sp, n, groups))
+        gain = gain_of(fade)
+        weight = (2.0 * row_at(real_sp, n, groups), 2.0 * row_at(imag_sp, n, groups))
+        lead = (weight[0] * gain, weight[1] * gain)
+        powers = power_list(lam, NEAR)
+        for u in range(1, NEAR):
+            put_pair(near_ref, n * (2 * NEAR) + 2 * u, groups, powers[u])
+        for u in range(FINAL_NEAR):
+            put_pair(tables_ref, n * (2 * FINAL_NEAR) + 2 * u, groups, powers[u if u else FINAL_NEAR])
+        put_pair(tables_ref, shift_row + 2 * n, groups, cmul(lead, lam))
+        put_pair(tables_ref, hop_row + 2 * n, groups, power_of(powers[NEAR], 2 * outer))
+        for a in range(outer):
+            if a:
+                lead = cmul(lead, powers[NEAR])
+            put_pair(lead_ref, n * (2 * outer) + 2 * a, groups, lead)
+        put_pair(late_ref, 2 * n, groups, cmul(lead, powers[NEAR]))
+        return carry
+
+    lax.fori_loop(0, states, prepare, 0, unroll=2)
+    copies[5].wait()
+    tables_copies = start_copies(((tables_ref, tables_hbm), (late_ref, late_hbm)), sems)
+    zero = jnp.zeros((groups, LANES), jnp.float32)
+    count = min(2, outer)
+    for first in range(0, outer, count):
+
+        def lead_of(n, first=first):
+            return [pair_at(lead_ref, n * (2 * outer) + 2 * (first + a), groups) for a in range(count)]
+
+        acc = power_sum(near_ref, lead_of, states, groups, NEAR, count, [zero] * (count * NEAR))
+        for t in range(count * NEAR):
+            put_row(taps_ref, first * NEAR + t, groups, acc[t])
+    taps_copy = pltpu.make_async_copy(taps_ref, taps_hbm, sems.at[2])
+    taps_copy.start()
+    for copy in tables_copies:
+        copy.wait()
+    taps_copy.wait()
+
+
+def convolve(signal_sp, taps_pad, skip, out_ref, tokens, groups, low=0, high=None):
+    tile = 8
 
     def col_tile(ji, acc, ti):
         gap = (ti - ji) * tile + 1
@@ -366,14 +535,64 @@
                 acc[t] = acc[t] + window[t - j + tile - 1] * drive
         return tuple(acc)
 
-    for ti in range(tokens // tile):
-        init = tuple(skip * row_at(signal_sp, ti * tile + t, groups) for t in range(tile))
-        acc = lax.fori_loop(0, ti + 1, functools.partial(col_tile, ti=ti), init, unroll=4)
+    for ti in range(low, tokens // tile):
+        first = 0 if high is None else max(0, ti - high + 1)
+        if low:
+            init = tuple(row_at(out_ref, ti * tile + t, groups) for t in range(tile))
+        else:
+            init = tuple(skip * row_at(signal_sp, ti * tile + t, groups) for t in range(tile))
+        acc = lax.fori_loop(first, ti - low + 1, functools.partial(col_tile, ti=ti), init, unroll=4)
         for t in range(tile):
             put_row(out_ref, ti * tile + t, groups, acc[t])
 
 
-def final_kernel(states, pack_ref, *refs):
+def pair_conv_kernel(
+    signal_hbm, skip_hbm, taps_hbm, tables_hbm, known_hbm, late_hbm, pack_ref,
+    signal_ref, skip_ref, late_ref, signal_sp, taps_pad, sems,
+):
+    tokens, channels = signal_ref.shape
+    groups = channels // LANES
+    states = late_ref.shape[0] // (2 * groups)
+    half, tile = tokens // 2, 8
+    first, last = tokens * groups, tokens * groups + tables_hbm.shape[0]
+    near_ref = pack_ref.at[first:last]
+    copies = start_copies(
+        (
+            (signal_hbm, signal_ref), (skip_hbm, skip_ref),
+            (taps_hbm, taps_pad.at[tile * groups : (tile + half) * groups]),
+            (late_hbm, late_ref), (tables_hbm, near_ref),
+            (known_hbm, pack_ref.at[last : last + known_hbm.shape[0]]),
+        ),
+        sems,
+    )
+    taps_pad[0 : tile * groups, :] = jnp.zeros((tile * groups, LANES), jnp.float32)
+    for copy in copies[:3]:
+        copy.wait()
+    spread_rows(signal_ref, signal_sp, tokens, groups, 16)
+    skip = skip_ref[...]
+    out_ref = pack_ref.at[0:first]
+    convolve(signal_sp, taps_pad, skip, out_ref, tokens, groups, 0, half // tile)
+    for copy in copies[3:]:
+        copy.wait()
+    zero = jnp.zeros((groups, LANES), jnp.float32)
+    count = 4
+
+    def lead_of(n):
+        hop = pair_at(near_ref, n * (2 * FINAL_NEAR), groups)
+        leads = [pair_at(late_ref, 2 * n, groups)]
+        for _ in range(count):
+            leads.append(cmul(leads[-1], hop))
+        put_pair(late_ref, 2 * n, groups, leads[count])
+        return leads
+
+    for start in range(half, tokens, count * FINAL_NEAR):
+        acc = power_sum(near_ref, lead_of, states, groups, FINAL_NEAR, count, [zero] * (count * FINAL_NEAR))
+        for t in range(count * FINAL_NEAR):
+            put_row(taps_pad, tile + start + t, groups, acc[t])
+    convolve(signal_sp, taps_pad, skip, out_ref, tokens, groups, half // tile)
+
+
+def final_kernel(states, pairs, pack_ref, *refs):
     message_refs, out_ref = refs[:-5], refs[-5]
     state_sp, rows_ref, out_buf, sems = refs[-4:]
     tokens, channels = out_ref.shape
@@ -382,10 +601,17 @@
     outer = tokens // near
     local_ref, near_ref, shift_ref, hop_ref, own_ref = split_pack(pack_ref, tokens, states, groups)
     scales = [scale_at(ref, states, groups) for ref in message_refs]
+    second = lax.rem(lax.axis_index("seqin"), 2).astype(jnp.float32)
 
     def enter(n, carry):
         hop = pair_at(hop_ref, 2 * n, groups)
         state = pair_at(own_ref, 2 * n, groups)
+        if pairs:
+            part = decode_at(message_refs[0], n, scales[0], groups)
+            moved = cmul((1.0 + second * (hop[0] - 1.0), second * hop[1]), part)
+            state = (moved[0] + state[0], moved[1] + state[1])
+            put_pair(state_sp, 2 * n, groups, cmul(pair_at(shift_ref, 2 * n, groups), state))
+            return carry
         for ref, scale in zip(reversed(message_refs), reversed(scales)):
             moved, part = cmul(hop, state), decode_at(ref, n, scale, groups)
             state = (moved[0] + part[0], moved[1] + part[1])
@@ -464,77 +690,175 @@
     parameters = tuple(hbm(array) for array in (time_step.reshape(groups, LANES), decay_rate, frequency))
     codes = pltpu.HBM((code_rows, LANES), jnp.bfloat16)
 
-    def sums(send):
-        return call(
-            functools.partial(sums_kernel, n_in, send),
-            "sums" if send else "base",
+    pairs = (n_in, n_out) == (4, 2) and tokens == 128
+    if pairs:
+        sum_buffers = [
+            pltpu.VMEM((tokens, channels), signal.dtype),
+            rows(1),
+            *[pltpu.VMEM((states, channels), f32)] * 2,
+            rows(tokens),
+            *[rows(states)] * 2,
+        ]
+        code_buffer = pltpu.VMEM((code_rows, LANES), jnp.bfloat16)
+        sum_scratch = [*sum_buffers, rows(4 * states), code_buffer, pltpu.SemaphoreType.DMA((4,))]
+        base, kept_code, code = call(
+            functools.partial(pair_sums_kernel, True),
+            "sums",
             20_000_000,
-            out_shape=codes if send else shape(4 * states * groups, LANES),
+            out_shape=(kept(4 * states), codes, codes),
             in_specs=[any_space] * 4,
-            out_specs=in_hbm if send else in_vmem,
+            out_specs=(in_hbm,) * 3,
+            scratch_shapes=sum_scratch,
+        )(hbm(signal), *parameters)
+        across = lax.ppermute(
+            code, ("seqin", "seqout"), [(z * n_out, (z ^ 1) * n_out + 1) for z in range(n_in)]
+        )
+        early = lax.ppermute(code, "seqout", [(0, 1)])
+        base, code = call(
+            functools.partial(pair_sums_kernel, False),
+            "base",
+            20_000_000,
+            out_shape=(kept(4 * states), codes),
+            in_specs=[any_space] * 4 + [in_hbm] * 2,
+            out_specs=(in_hbm,) * 2,
+            input_output_aliases={4: 0, 5: 1},
+            scratch_shapes=sum_scratch,
+        )(hbm(signal), *parameters, base, kept_code)
+        partner = lax.ppermute(code, "seqin", [(z, z ^ 1) for z in range(n_in)])
+
+        table_rows = states * (2 * FINAL_NEAR + 4)
+        taps, tables, late, base = call(
+            taps_kernel,
+            "taps",
+            24_000_000,
+            out_shape=(kept(tokens // 2), kept(table_rows), kept(2 * states), shape(4 * states * groups, LANES)),
+            in_specs=[any_space] * 6,
+            out_specs=(in_hbm, in_hbm, in_hbm, in_vmem),
+            scratch_shapes=[
+                rows(1),
+                *[pltpu.VMEM((states, channels), f32)] * 4,
+                *[rows(states)] * 4,
+                rows(2 * NEAR * states),
+                rows(outer * states),
+                rows(2 * states),
+                rows(tokens // 2),
+                rows(table_rows),
+                pltpu.SemaphoreType.DMA((6,)),
+            ],
+        )(*parameters, hbm(output_real), hbm(output_imag), hbm(base))
+
+        held = call(
+            pair_early_kernel,
+            "early",
+            100_000_000,
+            out_shape=shape(6 * states * groups, LANES),
+            in_specs=[in_vmem] * 3,
+        )(base, early, across)
+
+        message, own = call(
+            pair_message_kernel,
+            "messages",
+            6_000_000,
+            out_shape=(codes, kept(2 * states)),
+            in_specs=[in_vmem] * 2,
+            out_specs=(in_hbm, in_hbm),
+            scratch_shapes=[
+                rows(2 * states),
+                rows(2 * states),
+                code_buffer,
+                pltpu.SemaphoreType.DMA((2,)),
+            ],
+        )(held, partner)
+
+        received = [lax.ppermute(message, "seqin", [(z, z ^ 2) for z in range(n_in)])]
+
+        pack = call(
+            pair_conv_kernel,
+            "conv",
+            18_000_000,
+            out_shape=shape((tokens + table_rows + 2 * states) * groups, LANES),
+            in_specs=[any_space] * 6,
             scratch_shapes=[
                 pltpu.VMEM((tokens, channels), signal.dtype),
                 rows(1),
-                *[pltpu.VMEM((states, channels), f32)] * 2,
+                rows(2 * states),
                 rows(tokens),
-                *[rows(states)] * 2,
-                rows(4 * states if send else 1),
-                pltpu.VMEM((code_rows if send else 16, LANES), jnp.bfloat16),
-                pltpu.SemaphoreType.DMA((4,)),
+                rows(tokens + 8),
+                pltpu.SemaphoreType.DMA((6,)),
             ],
-        )(hbm(signal), *parameters)
-
-    code = sums(True)
-    early = [lax.ppermute(code, "seqout", [(i, i + j) for i in range(n_out - j)]) for j in range(1, n_out)]
-    parameters = lax.optimization_barrier((code, *parameters))[1:]
-    parameters = tuple(hbm(array) for array in parameters)
-    base = sums(False)
-
-    *messages, own = call(
-        functools.partial(messages_kernel, n_in, n_out - 1),
-        "messages",
-        4_000_000,
-        out_shape=(*[codes] * (n_in - 1), kept(2 * states)),
-        in_specs=(in_vmem, any_space, *[in_vmem] * (n_out - 1)),
-        out_specs=(in_hbm,) * n_in,
-        scratch_shapes=[
-            rows(2 * states),
-            rows(2 * states),
-            pltpu.VMEM((2, code_rows, LANES), jnp.bfloat16),
-            pltpu.SemaphoreType.DMA((n_in,)),
-        ],
-    )(base, hbm(code), *early)
-
-    received = [
-        lax.ppermute(messages[d - 1], "seqin", [(i, (i + d) % n_in) for i in range(n_in)]) for d in range(1, n_in)
-    ]
-
-    pack = call(
-        conv_kernel,
-        "conv",
-        40_000_000,
-        out_shape=shape((tokens + states * (2 * FINAL_NEAR + 6)) * groups, LANES),
-        in_specs=[any_space] * 8,
-        scratch_shapes=[
-            pltpu.VMEM((tokens, channels), signal.dtype),
-            rows(1),
-            rows(1),
-            *[pltpu.VMEM((states, channels), f32)] * 4,
-            *[rows(states)] * 4,
-            rows(2 * NEAR * states),
-            rows(2 * outer * states),
-            rows(tokens),
-            rows(tokens + 8),
-            pltpu.SemaphoreType.DMA((8,)),
-        ],
-    )(
-        hbm(signal), hbm(skip_gain.reshape(groups, LANES)), *parameters,
-        hbm(output_real), hbm(output_imag), hbm(own),
-    )
+        )(hbm(signal), hbm(skip_gain.reshape(groups, LANES)), hbm(taps), hbm(tables), hbm(own), hbm(late))
+    else:
+        def sums(send, given):
+            return call(
+                functools.partial(sums_kernel, n_in, send),
+                "sums" if send else "base",
+                20_000_000,
+                out_shape=codes if send else shape(4 * states * groups, LANES),
+                in_specs=[any_space] * 4,
+                out_specs=in_hbm if send else in_vmem,
+                scratch_shapes=[
+                    pltpu.VMEM((tokens, channels), signal.dtype),
+                    rows(1),
+                    *[pltpu.VMEM((states, channels), f32)] * 2,
+                    rows(tokens),
+                    *[rows(states)] * 2,
+                    rows(4 * states if send else 1),
+                    pltpu.VMEM((code_rows if send else 16, LANES), jnp.bfloat16),
+                    pltpu.SemaphoreType.DMA((4,)),
+                ],
+            )(hbm(signal), *given)
+
+        code = sums(True, parameters)
+        early = [lax.ppermute(code, "seqout", [(i, i + j) for i in range(n_out - j)]) for j in range(1, n_out)]
+        later = lax.optimization_barrier((code, *parameters))[1:]
+        parameters = tuple(hbm(array) for array in later)
+        base = sums(False, parameters)
+
+        *messages, own = call(
+            functools.partial(messages_kernel, n_in, n_out - 1),
+            "messages",
+            4_000_000,
+            out_shape=(*[codes] * (n_in - 1), kept(2 * states)),
+            in_specs=(in_vmem, any_space, *[in_vmem] * (n_out - 1)),
+            out_specs=(in_hbm,) * n_in,
+            scratch_shapes=[
+                rows(2 * states),
+                rows(2 * states),
+                pltpu.VMEM((2, code_rows, LANES), jnp.bfloat16),
+                pltpu.SemaphoreType.DMA((n_in,)),
+            ],
+        )(base, hbm(code), *early)
+
+        received = [
+            lax.ppermute(messages[d - 1], "seqin", [(i, (i + d) % n_in) for i in range(n_in)]) for d in range(1, n_in)
+        ]
+
+        pack = call(
+            conv_kernel,
+            "conv",
+            40_000_000,
+            out_shape=shape((tokens + states * (2 * FINAL_NEAR + 6)) * groups, LANES),
+            in_specs=[any_space] * 8,
+            scratch_shapes=[
+                pltpu.VMEM((tokens, channels), signal.dtype),
+                rows(1),
+                rows(1),
+                *[pltpu.VMEM((states, channels), f32)] * 4,
+                *[rows(states)] * 4,
+                rows(2 * NEAR * states),
+                rows(2 * outer * states),
+                rows(tokens),
+                rows(tokens + 8),
+                pltpu.SemaphoreType.DMA((8,)),
+            ],
+        )(
+            hbm(signal), hbm(skip_gain.reshape(groups, LANES)), *parameters,
+            hbm(output_real), hbm(output_imag), hbm(own),
+        )
 
     count = min(4, tokens // FINAL_NEAR)
     outputs = call(
-        functools.partial(final_kernel, states),
+        functools.partial(final_kernel, states, pairs),
         "final",
         20_000_000,
         out_shape=shape(tokens, channels),

time: 30.7 us -> 30.1 us (0.980)
  the two profiles are of different devices: /device:TPU:11 before, /device:TPU:0 now
where the time goes in v6:
time: 30.1 us; the launch traced here: 29.8 us
  Pallas kernels  19.5 us (65%)
  starting transfers between devices  8.33 us (28%)
  waiting for transfers between devices  1.93 us (6%)
    pallas_call x1, Pallas kernels, per_device(): call(functools.partial(pair_sums_kernel, True), 'sums', 20000000, out_sha...  5.23 us
    pallas_call x1, Pallas kernels, per_device(): call(pair_conv_kernel, 'conv', 18000000, out_shape=shape((tokens + table_...  5.03 us
    pallas_call x1, Pallas kernels, per_device(): call(taps_kernel, 'taps', 24000000, out_shape=(kept(tokens // 2), kept(ta...  4.12 us
    pallas_call x1, Pallas kernels, per_device(): call(functools.partial(final_kernel, states, pairs), 'final', 20000000, o...  3.48 us
    ppermute x1, starting transfers between devices, per_device(): partner = lax.ppermute(code, 'seqin', [(z, z ^ 1) for z in range(n_in)])  3.09 us
    ppermute x1, starting transfers between devices, per_device(): lax.ppermute(message, 'seqin', [(z, z ^ 2) for z in range(n_in)])  2.64 us
    ppermute x1, starting transfers between devices, per_device(): early = lax.ppermute(code, 'seqout', [(0, 1)])  1.3 us
    ppermute x1, starting transfers between devices, per_device(): lax.ppermute(code, ('seqin', 'seqout'), [(z * n_out, (z ^ 1) * n_out + 1)...  1.3 us
  transfers between devices with their start and end apart: 4, of which 2 were waited for; matrix products, arithmetic and copies ran while one was open for 0% of the time, Pallas kernels for 32%

profile of v6, /device:TPU:0, one launch (start us, length us, event | category | flops | bytes accessed | tf_op | source)
XLA Modules:
  0.0 29.8 jit_solution(10365342234458251110)
XLA Ops:
  0.0 5.2 %sums.1 = (f32[1024,128]{1,0:T(8,128)}, bf16[528,128]{1,0:T(8,128)(2,1)}, bf16[528,128]{1,0:T(8,128)(2,1)}) custom-call(bf16[128,1024]{1,0:T(8,128)(2,1)} %bitcast.4, f32[8,128]{1,0:T(8,128)} %bitcast.7, f32[32,1024]{1,0:T(8,128)} %decay_hbm.5, f32[32,1024]{1,0:T(8,128)} %freq_hbm.5), custom_call_target="tpu_custom_call" | custom-call | flops 20000000 | bytes 2000000 | tf_op jit(solution)/shard_map/sums/pallas_call | solution.py:704
  5.2 1.3 %collective-permute-start.1 = (bf16[528,128]{1,0:T(8,128)(2,1)}, bf16[528,128]{1,0:T(8,128)(2,1)S(1)}, u32[]{:S(2)}, u32[]{:S(2)}) collective-permute-start(bf16[528,128]{1,0:T(8,128)(2,1)} %get-tuple-element.22), channel_id=1, source_target_pairs={{0,6},{4,2},{8,14},{12,10},{1,7},{5,3},{9,15},{13,11},{16,22},{20,... | collective-permute-start | bytes 405512 | tf_op jit(solution)/shard_map/ppermute | solution.py:713
  6.5 1.3 %collective-permute-start = (bf16[528,128]{1,0:T(8,128)(2,1)}, bf16[528,128]{1,0:T(8,128)(2,1)S(1)}, u32[]{:S(2)}, u32[]{:S(2)}) collective-permute-start(bf16[528,128]{1,0:T(8,128)(2,1)} %get-tuple-element.22), channel_id=1, source_target_pairs={{0,2},{1,3},{4,6},{5,7},{8,10},{9,11},{12,14},{13,15},{16,18},{17,... | collective-permute-start | bytes 405512 | tf_op jit(solution)/shard_map/ppermute | solution.py:716
  7.8 0.1 base.1
  7.9 3.1 %collective-permute-start.2 = (bf16[528,128]{1,0:T(8,128)(2,1)}, bf16[528,128]{1,0:T(8,128)(2,1)S(1)}, u32[]{:S(2)}, u32[]{:S(2)}) collective-permute-start(bf16[528,128]{1,0:T(8,128)(2,1)} %get-tuple-element.23), channel_id=1, source_target_pairs={{0,4},{4,0},{8,12},{12,8},{1,5},{5,1},{9,13},{13,9},{2,6},{6,2},{1... | collective-permute-start | bytes 405512 | tf_op jit(solution)/shard_map/ppermute | solution.py:727
  11.0 4.1 %taps.1 = (f32[512,128]{1,0:T(8,128)}, f32[5120,128]{1,0:T(8,128)}, f32[512,128]{1,0:T(8,128)}, f32[1024,128]{1,0:T(8,128)S(1)}) custom-call(f32[8,128]{1,0:T(8,128)} %bitcast.9, f32[32,1024]{1,0:T(8,128)} %decay_hbm.5, f32[32,1024]{1,0:T(8,128)} %freq_hbm.5, f32[32,1024]{1,0:T(8,128)} %real_hbm.1, f32[32,1024]{1,0:T(8,128)} %imag_hbm.1, ...), custom_call_target="tpu_custom_call" | custom-call | flops 24000000 | bytes 2000000 | tf_op jit(solution)/shard_map/taps/pallas_call | solution.py:730
  15.1 0.0 collective-permute-done.1.early_partner_ref
  15.1 0.0 collective-permute-done.early_ref
  15.2 0.4 %early.1.held_ref = f32[1536,128]{1,0:T(8,128)S(1)} custom-call(f32[1024,128]{1,0:T(8,128)S(1)} %get-tuple-element.21.base_ref, bf16[528,128]{1,0:T(8,128)(2,1)S(1)} %collective-permute-done.early_ref, bf16[528,128]{1,0:T(8,128)(2,1)S(1)} %collective-permute-done.1.early_partner_ref), custom_call_target="tpu_custom_call" | custom-call | flops 100000000 | bytes 2000000 | tf_op jit(solution)/shard_map/early/pallas_call | solution.py:750
  15.5 0.8 %collective-permute-done.2.partner_ref = bf16[528,128]{1,0:T(8,128)(2,1)S(1)} collective-permute-done((bf16[528,128]{1,0:T(8,128)(2,1)}, bf16[528,128]{1,0:T(8,128)(2,1)S(1)}, u32[]{:S(2)}, u32[]{:S(2)}) %collective-permute-start.2) | collective-permute-done | bytes 135200 | tf_op jit(solution)/shard_map/ppermute | solution.py:727
  16.3 1.2 %messages.1 = (bf16[528,128]{1,0:T(8,128)(2,1)}, f32[512,128]{1,0:T(8,128)}) custom-call(f32[1536,128]{1,0:T(8,128)S(1)} %early.1.held_ref, bf16[528,128]{1,0:T(8,128)(2,1)S(1)} %collective-permute-done.2.partner_ref), custom_call_target="tpu_custom_call" | custom-call | flops 6000000 | bytes 2000000 | tf_op jit(solution)/shard_map/messages/pallas_call | solution.py:758
  17.5 2.6 %collective-permute-start.3 = (bf16[528,128]{1,0:T(8,128)(2,1)}, bf16[528,128]{1,0:T(8,128)(2,1)S(1)}, u32[]{:S(2)}, u32[]{:S(2)}) collective-permute-start(bf16[528,128]{1,0:T(8,128)(2,1)} %get-tuple-element.26), channel_id=1, source_target_pairs={{0,8},{4,12},{8,0},{12,4},{1,9},{5,13},{9,1},{13,5},{2,10},{6,14},... | collective-permute-start | bytes 405512 | tf_op jit(solution)/shard_map/ppermute | solution.py:773
  20.1 5.0 %conv.1.pack_ref = f32[6656,128]{1,0:T(8,128)S(1)} custom-call(bf16[128,1024]{1,0:T(8,128)(2,1)} %bitcast.6, f32[8,128]{1,0:T(8,128)} %bitcast.10, f32[512,128]{1,0:T(8,128)} %get-tuple-element.19.taps_hbm, f32[5120,128]{1,0:T(8,128)} %get-tuple-element.20.tables_hbm, f32[512,128]{1,0:T(8,128)} %get-tuple-element.24.known_hbm, ...), custom_call_target="tpu_custom_call" | custom-call | flops 18000000 | bytes 2000000 | tf_op jit(solution)/shard_map/conv/pallas_call | solution.py:775
  25.2 1.2 %collective-permute-done.3.refs_0_ = bf16[528,128]{1,0:T(8,128)(2,1)S(1)} collective-permute-done((bf16[528,128]{1,0:T(8,128)(2,1)}, bf16[528,128]{1,0:T(8,128)(2,1)S(1)}, u32[]{:S(2)}, u32[]{:S(2)}) %collective-permute-start.3) | collective-permute-done | bytes 135200 | tf_op jit(solution)/shard_map/ppermute | solution.py:773
  26.3 3.5 %final.1 = f32[128,1024]{1,0:T(8,128)} custom-call(f32[6656,128]{1,0:T(8,128)S(1)} %conv.1.pack_ref, bf16[528,128]{1,0:T(8,128)(2,1)S(1)} %collective-permute-done.3.refs_0_), custom_call_target="tpu_custom_call" | custom-call | flops 20000000 | bytes 2000000 | tf_op jit(solution)/shard_map/final/pallas_call | solution.py:860
Async XLA Ops:
  5.2 9.9 %collective-permute-start.1 = (bf16[528,128]{1,0:T(8,128)(2,1)}, bf16[528,128]{1,0:T(8,128)(2,1)S(1)}, u32[]{:S(2)}, u32[]{:S(2)}) collective-permute-start(bf16[528,128]{1,0:T(8,128)(2,1)} %get-tuple-element.22), channel_id=1, source_target_pairs={{0,6},{4,2},{8,14},{12,10},{1,7},{5,3},{9,15},{13,11},{16,22},{20,... | collective-permute-start | bytes 405512 | tf_op jit(solution)/shard_map/ppermute | solution.py:713
  6.5 8.6 %collective-permute-start = (bf16[528,128]{1,0:T(8,128)(2,1)}, bf16[528,128]{1,0:T(8,128)(2,1)S(1)}, u32[]{:S(2)}, u32[]{:S(2)}) collective-permute-start(bf16[528,128]{1,0:T(8,128)(2,1)} %get-tuple-element.22), channel_id=1, source_target_pairs={{0,2},{1,3},{4,6},{5,7},{8,10},{9,11},{12,14},{13,15},{16,18},{17,... | collective-permute-start | bytes 405512 | tf_op jit(solution)/shard_map/ppermute | solution.py:716
  7.9 8.4 %collective-permute-start.2 = (bf16[528,128]{1,0:T(8,128)(2,1)}, bf16[528,128]{1,0:T(8,128)(2,1)S(1)}, u32[]{:S(2)}, u32[]{:S(2)}) collective-permute-start(bf16[528,128]{1,0:T(8,128)(2,1)} %get-tuple-element.23), channel_id=1, source_target_pairs={{0,4},{4,0},{8,12},{12,8},{1,5},{5,1},{9,13},{13,9},{2,6},{6,2},{1... | collective-permute-start | bytes 405512 | tf_op jit(solution)/shard_map/ppermute | solution.py:727
  17.5 8.9 %collective-permute-start.3 = (bf16[528,128]{1,0:T(8,128)(2,1)}, bf16[528,128]{1,0:T(8,128)(2,1)S(1)}, u32[]{:S(2)}, u32[]{:S(2)}) collective-permute-start(bf16[528,128]{1,0:T(8,128)(2,1)} %get-tuple-element.26), channel_id=1, source_target_pairs={{0,8},{4,12},{8,0},{12,4},{1,9},{5,13},{9,1},{13,5},{2,10},{6,14},... | collective-permute-start | bytes 405512 | tf_op jit(solution)/shard_map/ppermute | solution.py:773

commit v7 on v6

--- a/solution.py
+++ b/solution.py
@@ -9,7 +9,7 @@
 
 LANES = 128
 NEAR = 16
-FINAL_NEAR = 8
+FINAL_NEAR = 16
 SUM_NEAR = 8
 HALF_RANGE = 125.0
 LOG_TWO = 0.6931471805599453
@@ -97,7 +97,7 @@
                 acc[slot] = acc[slot] + (leads[a][0] * real - leads[a][1] * imag)
         return tuple(acc)
 
-    return lax.fori_loop(0, states, turn, tuple(init), unroll=16)
+    return lax.fori_loop(0, states, turn, tuple(init), unroll=32)
 
 
 def power_of(base, exponent):
@@ -356,7 +356,7 @@
     convolve(signal_sp, taps_pad, skip_ref[...], out_ref, tokens, groups)
 
 
-def pair_sums_body(signal_hbm, step_hbm, decay_hbm, freq_hbm, base_ref, code_ref, buffers, sems):
+def pair_sums_body(signal_hbm, step_hbm, decay_hbm, freq_hbm, base_hbm, base_ref, code_ref, buffers, sems):
     signal_ref, step_ref, decay_ref, freq_ref, signal_sp, decay_sp, freq_sp = buffers
     copies = start_copies(
         ((step_hbm, step_ref), (decay_hbm, decay_ref), (freq_hbm, freq_ref), (signal_hbm, signal_ref)), sems
@@ -380,8 +380,11 @@
         put_pair(base_ref, 4 * n + 2, groups, own)
         return largest(own, most)
 
-    most = lax.fori_loop(0, states, prepare, jnp.zeros((groups, LANES), jnp.float32), unroll=4)
+    most = lax.fori_loop(0, states, prepare, jnp.zeros((groups, LANES), jnp.float32), unroll=8)
+    base_copy = pltpu.make_async_copy(base_ref, base_hbm, sems.at[3])
+    base_copy.start()
     write_codes(lambda n: pair_at(base_ref, 4 * n + 2, groups), code_ref, most, states, groups)
+    return base_copy
 
 
 def pair_sums_kernel(
@@ -394,10 +397,12 @@
 
     @pl.when((lax.axis_index("seqout") == 0) == first_block)
     def _():
-        pair_sums_body(signal_hbm, step_hbm, decay_hbm, freq_hbm, base_ref, code_ref, buffers, sems)
-        pairs = [(base_ref, out_refs[0])] + [(code_ref, ref) for ref in out_refs[1:]]
-        for copy in start_copies(pairs, sems):
+        base_copy = pair_sums_body(
+            signal_hbm, step_hbm, decay_hbm, freq_hbm, out_refs[0], base_ref, code_ref, buffers, sems
+        )
+        for copy in start_copies([(code_ref, ref) for ref in out_refs[1:]], sems):
             copy.wait()
+        base_copy.wait()
 
 
 def joined(hop, mine, other, second):
@@ -423,7 +428,7 @@
         put_pair(held_ref, 6 * n + 4, groups, joined(hop, early, early_partner, second))
         return carry
 
-    lax.fori_loop(0, states, gather, 0, unroll=4)
+    lax.fori_loop(0, states, gather, 0, unroll=8)
 
 
 def pair_message_kernel(held_ref, partner_ref, message_hbm, known_hbm, *scratch):
@@ -449,7 +454,7 @@
         put_pair(known_ref, 2 * n, groups, known)
         return largest(message, most)
 
-    most = lax.fori_loop(0, states, gather, jnp.zeros((groups, LANES), jnp.float32), unroll=4)
+    most = lax.fori_loop(0, states, gather, jnp.zeros((groups, LANES), jnp.float32), unroll=8)
     known_copy = pltpu.make_async_copy(known_ref, known_hbm, sems.at[0])
     known_copy.start()
     write_codes(lambda n: pair_at(message_ref, 2 * n, groups), code_ref, most, states, groups)
@@ -575,7 +580,7 @@
     for copy in copies[3:]:
         copy.wait()
     zero = jnp.zeros((groups, LANES), jnp.float32)
-    count = 4
+    count = 32 // FINAL_NEAR
 
     def lead_of(n):
         hop = pair_at(near_ref, n * (2 * FINAL_NEAR), groups)
@@ -618,8 +623,8 @@
         put_pair(state_sp, 2 * n, groups, cmul(pair_at(shift_ref, 2 * n, groups), state))
         return carry
 
-    lax.fori_loop(0, states, enter, 0, unroll=4)
-    count = min(4, outer)
+    lax.fori_loop(0, states, enter, 0, unroll=8)
+    count = min(32 // near, outer)
     span = count * near
     copies = []
     for index in range(outer // count):
@@ -856,7 +861,7 @@
             hbm(output_real), hbm(output_imag), hbm(own),
         )
 
-    count = min(4, tokens // FINAL_NEAR)
+    count = min(32 // FINAL_NEAR, tokens // FINAL_NEAR)
     outputs = call(
         functools.partial(final_kernel, states, pairs),
         "final",

time: 30.1 us -> 29.5 us (0.980)
  waiting for transfers between devices: 1.93 us -> 1.5 us
    pallas_call x1, Pallas kernels: 4.12 us -> 4.67 us  [per_device(): call(taps_kernel, 'taps', 24000000, out_shape=(kept(tokens // 2), kept(ta...]
    ppermute x1, waiting for transfers between devices: 0.75 us -> 0.26 us  [per_device(): partner = lax.ppermute(code, 'seqin', [(z, z ^ 1) for z in range(n_in)])]
  transfers between devices with their start and end apart: 4 -> 4, of which waited for: 2 -> 2; matrix products, arithmetic and copies ran while one was open for 0% -> 0% of each run, Pallas kernels for 32% -> 34%
where the time goes in v7:
time: 29.5 us; the launch traced here: 29.2 us
  Pallas kernels  19.3 us (65%)
  starting transfers between devices  8.33 us (28%)
  waiting for transfers between devices  1.5 us (5%)
    pallas_call x1, Pallas kernels, per_device(): call(functools.partial(pair_sums_kernel, True), 'sums', 20000000, out_sha...  5.03 us
    pallas_call x1, Pallas kernels, per_device(): call(pair_conv_kernel, 'conv', 18000000, out_shape=shape((tokens + table_...  4.9 us
    pallas_call x1, Pallas kernels, per_device(): call(taps_kernel, 'taps', 24000000, out_shape=(kept(tokens // 2), kept(ta...  4.67 us
    pallas_call x1, Pallas kernels, per_device(): call(functools.partial(final_kernel, states, pairs), 'final', 20000000, o...  3.22 us
    ppermute x1, starting transfers between devices, per_device(): partner = lax.ppermute(code, 'seqin', [(z, z ^ 1) for z in range(n_in)])  3.09 us
    ppermute x1, starting transfers between devices, per_device(): lax.ppermute(message, 'seqin', [(z, z ^ 2) for z in range(n_in)])  2.64 us
    ppermute x1, starting transfers between devices, per_device(): lax.ppermute(code, ('seqin', 'seqout'), [(z * n_out, (z ^ 1) * n_out + 1)...  1.3 us
    ppermute x1, starting transfers between devices, per_device(): early = lax.ppermute(code, 'seqout', [(0, 1)])  1.3 us
  transfers between devices with their start and end apart: 4, of which 2 were waited for; matrix products, arithmetic and copies ran while one was open for 0% of the time, Pallas kernels for 34%

profile of v7, /device:TPU:0, one launch (start us, length us, event | category | flops | bytes accessed | tf_op | source)
XLA Modules:
  0.0 29.2 jit_solution(11806272605224982496)
XLA Ops:
  0.0 5.0 %sums.1 = (f32[1024,128]{1,0:T(8,128)}, bf16[528,128]{1,0:T(8,128)(2,1)}, bf16[528,128]{1,0:T(8,128)(2,1)}) custom-call(bf16[128,1024]{1,0:T(8,128)(2,1)} %bitcast.4, f32[8,128]{1,0:T(8,128)} %bitcast.7, f32[32,1024]{1,0:T(8,128)} %decay_hbm.5, f32[32,1024]{1,0:T(8,128)} %freq_hbm.5), custom_call_target="tpu_custom_call" | custom-call | flops 20000000 | bytes 2000000 | tf_op jit(solution)/shard_map/sums/pallas_call | solution.py:709
  5.0 1.3 %collective-permute-start.1 = (bf16[528,128]{1,0:T(8,128)(2,1)}, bf16[528,128]{1,0:T(8,128)(2,1)S(1)}, u32[]{:S(2)}, u32[]{:S(2)}) collective-permute-start(bf16[528,128]{1,0:T(8,128)(2,1)} %get-tuple-element.22), channel_id=1, source_target_pairs={{0,6},{4,2},{8,14},{12,10},{1,7},{5,3},{9,15},{13,11},{16,22},{20,... | collective-permute-start | bytes 405512 | tf_op jit(solution)/shard_map/ppermute | solution.py:718
  6.3 1.3 %collective-permute-start = (bf16[528,128]{1,0:T(8,128)(2,1)}, bf16[528,128]{1,0:T(8,128)(2,1)S(1)}, u32[]{:S(2)}, u32[]{:S(2)}) collective-permute-start(bf16[528,128]{1,0:T(8,128)(2,1)} %get-tuple-element.22), channel_id=1, source_target_pairs={{0,2},{1,3},{4,6},{5,7},{8,10},{9,11},{12,14},{13,15},{16,18},{17,... | collective-permute-start | bytes 405512 | tf_op jit(solution)/shard_map/ppermute | solution.py:721
  7.6 0.1 base.1
  7.7 3.1 %collective-permute-start.2 = (bf16[528,128]{1,0:T(8,128)(2,1)}, bf16[528,128]{1,0:T(8,128)(2,1)S(1)}, u32[]{:S(2)}, u32[]{:S(2)}) collective-permute-start(bf16[528,128]{1,0:T(8,128)(2,1)} %get-tuple-element.23), channel_id=1, source_target_pairs={{0,4},{4,0},{8,12},{12,8},{1,5},{5,1},{9,13},{13,9},{2,6},{6,2},{1... | collective-permute-start | bytes 405512 | tf_op jit(solution)/shard_map/ppermute | solution.py:732
  10.8 4.7 %taps.1 = (f32[512,128]{1,0:T(8,128)}, f32[9216,128]{1,0:T(8,128)}, f32[512,128]{1,0:T(8,128)}, f32[1024,128]{1,0:T(8,128)S(1)}) custom-call(f32[8,128]{1,0:T(8,128)} %bitcast.9, f32[32,1024]{1,0:T(8,128)} %decay_hbm.5, f32[32,1024]{1,0:T(8,128)} %freq_hbm.5, f32[32,1024]{1,0:T(8,128)} %real_hbm.1, f32[32,1024]{1,0:T(8,128)} %imag_hbm.1, ...), custom_call_target="tpu_custom_call" | custom-call | flops 24000000 | bytes 2000000 | tf_op jit(solution)/shard_map/taps/pallas_call | solution.py:735
  15.5 0.0 collective-permute-done.1.early_partner_ref
  15.5 0.0 collective-permute-done.early_ref
  15.5 0.3 %early.1.held_ref = f32[1536,128]{1,0:T(8,128)S(1)} custom-call(f32[1024,128]{1,0:T(8,128)S(1)} %get-tuple-element.21.base_ref, bf16[528,128]{1,0:T(8,128)(2,1)S(1)} %collective-permute-done.early_ref, bf16[528,128]{1,0:T(8,128)(2,1)S(1)} %collective-permute-done.1.early_partner_ref), custom_call_target="tpu_custom_call" | custom-call | flops 100000000 | bytes 2000000 | tf_op jit(solution)/shard_map/early/pallas_call | solution.py:755
  15.8 0.3 collective-permute-done.2.partner_ref
  16.1 1.2 %messages.1 = (bf16[528,128]{1,0:T(8,128)(2,1)}, f32[512,128]{1,0:T(8,128)}) custom-call(f32[1536,128]{1,0:T(8,128)S(1)} %early.1.held_ref, bf16[528,128]{1,0:T(8,128)(2,1)S(1)} %collective-permute-done.2.partner_ref), custom_call_target="tpu_custom_call" | custom-call | flops 6000000 | bytes 2000000 | tf_op jit(solution)/shard_map/messages/pallas_call | solution.py:763
  17.2 2.6 %collective-permute-start.3 = (bf16[528,128]{1,0:T(8,128)(2,1)}, bf16[528,128]{1,0:T(8,128)(2,1)S(1)}, u32[]{:S(2)}, u32[]{:S(2)}) collective-permute-start(bf16[528,128]{1,0:T(8,128)(2,1)} %get-tuple-element.26), channel_id=1, source_target_pairs={{0,8},{4,12},{8,0},{12,4},{1,9},{5,13},{9,1},{13,5},{2,10},{6,14},... | collective-permute-start | bytes 405512 | tf_op jit(solution)/shard_map/ppermute | solution.py:778
  19.9 4.9 %conv.1.pack_ref = f32[10752,128]{1,0:T(8,128)S(1)} custom-call(bf16[128,1024]{1,0:T(8,128)(2,1)} %bitcast.6, f32[8,128]{1,0:T(8,128)} %bitcast.10, f32[512,128]{1,0:T(8,128)} %get-tuple-element.19.taps_hbm, f32[9216,128]{1,0:T(8,128)} %get-tuple-element.20.tables_hbm, f32[512,128]{1,0:T(8,128)} %get-tuple-element.24.known_hbm, ...), custom_call_target="tpu_custom_call" | custom-call | flops 18000000 | bytes 2000000 | tf_op jit(solution)/shard_map/conv/pallas_call | solution.py:780
  24.8 1.2 %collective-permute-done.3.refs_0_ = bf16[528,128]{1,0:T(8,128)(2,1)S(1)} collective-permute-done((bf16[528,128]{1,0:T(8,128)(2,1)}, bf16[528,128]{1,0:T(8,128)(2,1)S(1)}, u32[]{:S(2)}, u32[]{:S(2)}) %collective-permute-start.3) | collective-permute-done | bytes 135200 | tf_op jit(solution)/shard_map/ppermute | solution.py:778
  26.0 3.2 %final.1 = f32[128,1024]{1,0:T(8,128)} custom-call(f32[10752,128]{1,0:T(8,128)S(1)} %conv.1.pack_ref, bf16[528,128]{1,0:T(8,128)(2,1)S(1)} %collective-permute-done.3.refs_0_), custom_call_target="tpu_custom_call" | custom-call | flops 20000000 | bytes 2000000 | tf_op jit(solution)/shard_map/final/pallas_call | solution.py:865
Async XLA Ops:
  5.0 10.4 %collective-permute-start.1 = (bf16[528,128]{1,0:T(8,128)(2,1)}, bf16[528,128]{1,0:T(8,128)(2,1)S(1)}, u32[]{:S(2)}, u32[]{:S(2)}) collective-permute-start(bf16[528,128]{1,0:T(8,128)(2,1)} %get-tuple-element.22), channel_id=1, source_target_pairs={{0,6},{4,2},{8,14},{12,10},{1,7},{5,3},{9,15},{13,11},{16,22},{20,... | collective-permute-start | bytes 405512 | tf_op jit(solution)/shard_map/ppermute | solution.py:718
  6.3 9.2 %collective-permute-start = (bf16[528,128]{1,0:T(8,128)(2,1)}, bf16[528,128]{1,0:T(8,128)(2,1)S(1)}, u32[]{:S(2)}, u32[]{:S(2)}) collective-permute-start(bf16[528,128]{1,0:T(8,128)(2,1)} %get-tuple-element.22), channel_id=1, source_target_pairs={{0,2},{1,3},{4,6},{5,7},{8,10},{9,11},{12,14},{13,15},{16,18},{17,... | collective-permute-start | bytes 405512 | tf_op jit(solution)/shard_map/ppermute | solution.py:721
  7.7 8.4 %collective-permute-start.2 = (bf16[528,128]{1,0:T(8,128)(2,1)}, bf16[528,128]{1,0:T(8,128)(2,1)S(1)}, u32[]{:S(2)}, u32[]{:S(2)}) collective-permute-start(bf16[528,128]{1,0:T(8,128)(2,1)} %get-tuple-element.23), channel_id=1, source_target_pairs={{0,4},{4,0},{8,12},{12,8},{1,5},{5,1},{9,13},{13,9},{2,6},{6,2},{1... | collective-permute-start | bytes 405512 | tf_op jit(solution)/shard_map/ppermute | solution.py:732
  17.2 8.8 %collective-permute-start.3 = (bf16[528,128]{1,0:T(8,128)(2,1)}, bf16[528,128]{1,0:T(8,128)(2,1)S(1)}, u32[]{:S(2)}, u32[]{:S(2)}) collective-permute-start(bf16[528,128]{1,0:T(8,128)(2,1)} %get-tuple-element.26), channel_id=1, source_target_pairs={{0,8},{4,12},{8,0},{12,4},{1,9},{5,13},{9,1},{13,5},{2,10},{6,14},... | collective-permute-start | bytes 405512 | tf_op jit(solution)/shard_map/ppermute | solution.py:778

commit v8 on v7

--- a/solution.py
+++ b/solution.py
@@ -11,6 +11,7 @@
 NEAR = 16
 FINAL_NEAR = 16
 SUM_NEAR = 8
+EARLY_PARTS = 4
 HALF_RANGE = 125.0
 LOG_TWO = 0.6931471805599453
 SMALLEST_CODE = 2.0**-125
@@ -499,7 +500,7 @@
         for u in range(FINAL_NEAR):
             put_pair(tables_ref, n * (2 * FINAL_NEAR) + 2 * u, groups, powers[u if u else FINAL_NEAR])
         put_pair(tables_ref, shift_row + 2 * n, groups, cmul(lead, lam))
-        put_pair(tables_ref, hop_row + 2 * n, groups, power_of(powers[NEAR], 2 * outer))
+        put_pair(tables_ref, hop_row + 2 * n, groups, power_of(powers[NEAR], EARLY_PARTS * outer))
         for a in range(outer):
             if a:
                 lead = cmul(lead, powers[NEAR])
@@ -507,9 +508,19 @@
         put_pair(late_ref, 2 * n, groups, cmul(lead, powers[NEAR]))
         return carry
 
-    lax.fori_loop(0, states, prepare, 0, unroll=2)
+    tables_copies, chunks = [], 4
+    for chunk in range(chunks):
+        span = states // chunks
+        lax.fori_loop(chunk * span, (chunk + 1) * span, prepare, 0, unroll=2)
+        part = pl.ds(chunk * span * 2 * FINAL_NEAR * groups, span * 2 * FINAL_NEAR * groups)
+        tables_copies.append(pltpu.make_async_copy(tables_ref.at[part], tables_hbm.at[part], sems.at[chunk]))
+        tables_copies[-1].start()
     copies[5].wait()
-    tables_copies = start_copies(((tables_ref, tables_hbm), (late_ref, late_hbm)), sems)
+    part = pl.ds(shift_row * groups, 4 * states * groups)
+    tables_copies.append(pltpu.make_async_copy(tables_ref.at[part], tables_hbm.at[part], sems.at[chunks]))
+    tables_copies.append(pltpu.make_async_copy(late_ref, late_hbm, sems.at[5]))
+    for copy in tables_copies[chunks:]:
+        copy.start()
     zero = jnp.zeros((groups, LANES), jnp.float32)
     count = min(2, outer)
     for first in range(0, outer, count):
@@ -520,7 +531,7 @@
         acc = power_sum(near_ref, lead_of, states, groups, NEAR, count, [zero] * (count * NEAR))
         for t in range(count * NEAR):
             put_row(taps_ref, first * NEAR + t, groups, acc[t])
-    taps_copy = pltpu.make_async_copy(taps_ref, taps_hbm, sems.at[2])
+    taps_copy = pltpu.make_async_copy(taps_ref, taps_hbm, sems.at[6])
     taps_copy.start()
     for copy in tables_copies:
         copy.wait()
@@ -558,7 +569,7 @@
     tokens, channels = signal_ref.shape
     groups = channels // LANES
     states = late_ref.shape[0] // (2 * groups)
-    half, tile = tokens // 2, 8
+    half, tile = tokens // EARLY_PARTS, 8
     first, last = tokens * groups, tokens * groups + tables_hbm.shape[0]
     near_ref = pack_ref.at[first:last]
     copies = start_copies(
@@ -736,7 +747,7 @@
             taps_kernel,
             "taps",
             24_000_000,
-            out_shape=(kept(tokens // 2), kept(table_rows), kept(2 * states), shape(4 * states * groups, LANES)),
+            out_shape=(kept(tokens // EARLY_PARTS), kept(table_rows), kept(2 * states), shape(4 * states * groups, LANES)),
             in_specs=[any_space] * 6,
             out_specs=(in_hbm, in_hbm, in_hbm, in_vmem),
             scratch_shapes=[
@@ -746,9 +757,9 @@
                 rows(2 * NEAR * states),
                 rows(outer * states),
                 rows(2 * states),
-                rows(tokens // 2),
+                rows(tokens // EARLY_PARTS),
                 rows(table_rows),
-                pltpu.SemaphoreType.DMA((6,)),
+                pltpu.SemaphoreType.DMA((7,)),
             ],
         )(*parameters, hbm(output_real), hbm(output_imag), hbm(base))
 

time: 29.5 us -> 29.5 us (level)
    pallas_call x1, Pallas kernels: 4.9 us -> 5.85 us  [per_device(): call(pair_conv_kernel, 'conv', 18000000, out_shape=shape((tokens + table_...]
    ppermute x1, waiting for transfers between devices: 1.24 us -> 0.29 us  [per_device(): lax.ppermute(message, 'seqin', [(z, z ^ 2) for z in range(n_in)])]
    ppermute x1, waiting for transfers between devices: 0.26 us -> 1.15 us  [per_device(): partner = lax.ppermute(code, 'seqin', [(z, z ^ 1) for z in range(n_in)])]
    pallas_call x1, Pallas kernels: 4.67 us -> 3.78 us  [per_device(): call(taps_kernel, 'taps', 24000000, out_shape=(kept(tokens // EARLY_PARTS...]
where the time goes in v8:
time: 29.5 us; the launch traced here: 29.2 us
  Pallas kernels  19.4 us (66%)
  starting transfers between devices  8.33 us (28%)
  waiting for transfers between devices  1.45 us (5%)
    pallas_call x1, Pallas kernels, per_device(): call(pair_conv_kernel, 'conv', 18000000, out_shape=shape((tokens + table_...  5.85 us
    pallas_call x1, Pallas kernels, per_device(): call(functools.partial(pair_sums_kernel, True), 'sums', 20000000, out_sha...  5.01 us
    pallas_call x1, Pallas kernels, per_device(): call(taps_kernel, 'taps', 24000000, out_shape=(kept(tokens // EARLY_PARTS...  3.78 us
    pallas_call x1, Pallas kernels, per_device(): call(functools.partial(final_kernel, states, pairs), 'final', 20000000, o...  3.22 us
    ppermute x1, starting transfers between devices, per_device(): partner = lax.ppermute(code, 'seqin', [(z, z ^ 1) for z in range(n_in)])  3.09 us
    ppermute x1, starting transfers between devices, per_device(): lax.ppermute(message, 'seqin', [(z, z ^ 2) for z in range(n_in)])  2.64 us
    ppermute x1, starting transfers between devices, per_device(): lax.ppermute(code, ('seqin', 'seqout'), [(z * n_out, (z ^ 1) * n_out + 1)...  1.3 us
    ppermute x1, starting transfers between devices, per_device(): early = lax.ppermute(code, 'seqout', [(0, 1)])  1.3 us
  transfers between devices with their start and end apart: 4, of which 2 were waited for; matrix products, arithmetic and copies ran while one was open for 0% of the time, Pallas kernels for 34%

profile of v8, /device:TPU:0, one launch (start us, length us, event | category | flops | bytes accessed | tf_op | source)
XLA Modules:
  0.0 29.2 jit_solution(11103180561674383740)
XLA Ops:
  0.0 5.0 %sums.1 = (f32[1024,128]{1,0:T(8,128)}, bf16[528,128]{1,0:T(8,128)(2,1)}, bf16[528,128]{1,0:T(8,128)(2,1)}) custom-call(bf16[128,1024]{1,0:T(8,128)(2,1)} %bitcast.4, f32[8,128]{1,0:T(8,128)} %bitcast.7, f32[32,1024]{1,0:T(8,128)} %decay_hbm.5, f32[32,1024]{1,0:T(8,128)} %freq_hbm.5), custom_call_target="tpu_custom_call" | custom-call | flops 20000000 | bytes 2000000 | tf_op jit(solution)/shard_map/sums/pallas_call | solution.py:720
  5.0 1.3 %collective-permute-start.1 = (bf16[528,128]{1,0:T(8,128)(2,1)}, bf16[528,128]{1,0:T(8,128)(2,1)S(1)}, u32[]{:S(2)}, u32[]{:S(2)}) collective-permute-start(bf16[528,128]{1,0:T(8,128)(2,1)} %get-tuple-element.22), channel_id=1, source_target_pairs={{0,6},{4,2},{8,14},{12,10},{1,7},{5,3},{9,15},{13,11},{16,22},{20,... | collective-permute-start | bytes 405512 | tf_op jit(solution)/shard_map/ppermute | solution.py:729
  6.3 1.3 %collective-permute-start = (bf16[528,128]{1,0:T(8,128)(2,1)}, bf16[528,128]{1,0:T(8,128)(2,1)S(1)}, u32[]{:S(2)}, u32[]{:S(2)}) collective-permute-start(bf16[528,128]{1,0:T(8,128)(2,1)} %get-tuple-element.22), channel_id=1, source_target_pairs={{0,2},{1,3},{4,6},{5,7},{8,10},{9,11},{12,14},{13,15},{16,18},{17,... | collective-permute-start | bytes 405512 | tf_op jit(solution)/shard_map/ppermute | solution.py:732
  7.6 0.1 base.1
  7.7 3.1 %collective-permute-start.2 = (bf16[528,128]{1,0:T(8,128)(2,1)}, bf16[528,128]{1,0:T(8,128)(2,1)S(1)}, u32[]{:S(2)}, u32[]{:S(2)}) collective-permute-start(bf16[528,128]{1,0:T(8,128)(2,1)} %get-tuple-element.23), channel_id=1, source_target_pairs={{0,4},{4,0},{8,12},{12,8},{1,5},{5,1},{9,13},{13,9},{2,6},{6,2},{1... | collective-permute-start | bytes 405512 | tf_op jit(solution)/shard_map/ppermute | solution.py:743
  10.8 3.8 %taps.1 = (f32[256,128]{1,0:T(8,128)}, f32[9216,128]{1,0:T(8,128)}, f32[512,128]{1,0:T(8,128)}, f32[1024,128]{1,0:T(8,128)S(1)}) custom-call(f32[8,128]{1,0:T(8,128)} %bitcast.9, f32[32,1024]{1,0:T(8,128)} %decay_hbm.5, f32[32,1024]{1,0:T(8,128)} %freq_hbm.5, f32[32,1024]{1,0:T(8,128)} %real_hbm.1, f32[32,1024]{1,0:T(8,128)} %imag_hbm.1, ...), custom_call_target="tpu_custom_call" | custom-call | flops 24000000 | bytes 2000000 | tf_op jit(solution)/shard_map/taps/pallas_call | solution.py:746
  14.6 0.0 collective-permute-done.1.early_partner_ref
  14.6 0.0 collective-permute-done.early_ref
  14.6 0.3 %early.1.held_ref = f32[1536,128]{1,0:T(8,128)S(1)} custom-call(f32[1024,128]{1,0:T(8,128)S(1)} %get-tuple-element.21.base_ref, bf16[528,128]{1,0:T(8,128)(2,1)S(1)} %collective-permute-done.early_ref, bf16[528,128]{1,0:T(8,128)(2,1)S(1)} %collective-permute-done.1.early_partner_ref), custom_call_target="tpu_custom_call" | custom-call | flops 100000000 | bytes 2000000 | tf_op jit(solution)/shard_map/early/pallas_call | solution.py:766
  14.9 1.2 %collective-permute-done.2.partner_ref = bf16[528,128]{1,0:T(8,128)(2,1)S(1)} collective-permute-done((bf16[528,128]{1,0:T(8,128)(2,1)}, bf16[528,128]{1,0:T(8,128)(2,1)S(1)}, u32[]{:S(2)}, u32[]{:S(2)}) %collective-permute-start.2) | collective-permute-done | bytes 135200 | tf_op jit(solution)/shard_map/ppermute | solution.py:743
  16.1 1.1 %messages.1 = (bf16[528,128]{1,0:T(8,128)(2,1)}, f32[512,128]{1,0:T(8,128)}) custom-call(f32[1536,128]{1,0:T(8,128)S(1)} %early.1.held_ref, bf16[528,128]{1,0:T(8,128)(2,1)S(1)} %collective-permute-done.2.partner_ref), custom_call_target="tpu_custom_call" | custom-call | flops 6000000 | bytes 2000000 | tf_op jit(solution)/shard_map/messages/pallas_call | solution.py:774
  17.2 2.6 %collective-permute-start.3 = (bf16[528,128]{1,0:T(8,128)(2,1)}, bf16[528,128]{1,0:T(8,128)(2,1)S(1)}, u32[]{:S(2)}, u32[]{:S(2)}) collective-permute-start(bf16[528,128]{1,0:T(8,128)(2,1)} %get-tuple-element.26), channel_id=1, source_target_pairs={{0,8},{4,12},{8,0},{12,4},{1,9},{5,13},{9,1},{13,5},{2,10},{6,14},... | collective-permute-start | bytes 405512 | tf_op jit(solution)/shard_map/ppermute | solution.py:789
  19.8 5.9 %conv.1.pack_ref = f32[10752,128]{1,0:T(8,128)S(1)} custom-call(bf16[128,1024]{1,0:T(8,128)(2,1)} %bitcast.6, f32[8,128]{1,0:T(8,128)} %bitcast.10, f32[256,128]{1,0:T(8,128)} %get-tuple-element.19.taps_hbm, f32[9216,128]{1,0:T(8,128)} %get-tuple-element.20.tables_hbm, f32[512,128]{1,0:T(8,128)} %get-tuple-element.24.known_hbm, ...), custom_call_target="tpu_custom_call" | custom-call | flops 18000000 | bytes 2000000 | tf_op jit(solution)/shard_map/conv/pallas_call | solution.py:791
  25.7 0.3 collective-permute-done.3.refs_0_
  26.0 3.2 %final.1 = f32[128,1024]{1,0:T(8,128)} custom-call(f32[10752,128]{1,0:T(8,128)S(1)} %conv.1.pack_ref, bf16[528,128]{1,0:T(8,128)(2,1)S(1)} %collective-permute-done.3.refs_0_), custom_call_target="tpu_custom_call" | custom-call | flops 20000000 | bytes 2000000 | tf_op jit(solution)/shard_map/final/pallas_call | solution.py:876
Async XLA Ops:
  5.0 9.6 %collective-permute-start.1 = (bf16[528,128]{1,0:T(8,128)(2,1)}, bf16[528,128]{1,0:T(8,128)(2,1)S(1)}, u32[]{:S(2)}, u32[]{:S(2)}) collective-permute-start(bf16[528,128]{1,0:T(8,128)(2,1)} %get-tuple-element.22), channel_id=1, source_target_pairs={{0,6},{4,2},{8,14},{12,10},{1,7},{5,3},{9,15},{13,11},{16,22},{20,... | collective-permute-start | bytes 405512 | tf_op jit(solution)/shard_map/ppermute | solution.py:729
  6.3 8.3 %collective-permute-start = (bf16[528,128]{1,0:T(8,128)(2,1)}, bf16[528,128]{1,0:T(8,128)(2,1)S(1)}, u32[]{:S(2)}, u32[]{:S(2)}) collective-permute-start(bf16[528,128]{1,0:T(8,128)(2,1)} %get-tuple-element.22), channel_id=1, source_target_pairs={{0,2},{1,3},{4,6},{5,7},{8,10},{9,11},{12,14},{13,15},{16,18},{17,... | collective-permute-start | bytes 405512 | tf_op jit(solution)/shard_map/ppermute | solution.py:732
  7.7 8.4 %collective-permute-start.2 = (bf16[528,128]{1,0:T(8,128)(2,1)}, bf16[528,128]{1,0:T(8,128)(2,1)S(1)}, u32[]{:S(2)}, u32[]{:S(2)}) collective-permute-start(bf16[528,128]{1,0:T(8,128)(2,1)} %get-tuple-element.23), channel_id=1, source_target_pairs={{0,4},{4,0},{8,12},{12,8},{1,5},{5,1},{9,13},{13,9},{2,6},{6,2},{1... | collective-permute-start | bytes 405512 | tf_op jit(solution)/shard_map/ppermute | solution.py:743
  17.2 8.8 %collective-permute-start.3 = (bf16[528,128]{1,0:T(8,128)(2,1)}, bf16[528,128]{1,0:T(8,128)(2,1)S(1)}, u32[]{:S(2)}, u32[]{:S(2)}) collective-permute-start(bf16[528,128]{1,0:T(8,128)(2,1)} %get-tuple-element.26), channel_id=1, source_target_pairs={{0,8},{4,12},{8,0},{12,4},{1,9},{5,13},{9,1},{13,5},{2,10},{6,14},... | collective-permute-start | bytes 405512 | tf_op jit(solution)/shard_map/ppermute | solution.py:789
